TPU v7x, 512 devices: a whole 4x8x8 slice. The times are simulated.
512 devices in a mesh: ctx: 128 (over z, y, core), tp: 4 (over x).
Axes of the slice: x: 4, y: 8, z: 8, core: 2. Of those that a mesh axis runs over, the one named last changes fastest.
Arguments:
- query: bfloat16 [32768, 4096], P('ctx', 'tp'), may hold values from -96 to 96
- key: bfloat16 [32768, 4096], P('ctx', 'tp'), may hold values from -4 to 4
- value: bfloat16 [32768, 4096], P('ctx', 'tp'), may hold values from -6 to 6
- xin: bfloat16 [32768, 4096], P('ctx', 'tp'), may hold values from -1 to 8
- gate_z: bfloat16 [32768, 4096], P('ctx', 'tp'), may hold values from -6 to 6
- w_bc: bfloat16 [4096, 32], P('tp'), may hold values from -1 to 1
- dt_low: bfloat16 [32768, 256], P('ctx'), may hold values from -4 to 9
- dt_proj: bfloat16 [256, 4096], P(None, 'tp'), may hold values from -3 to 3
- dt_bias: float32 [4096], P('tp'), may hold values from -20 to 0
- a_rate: float32 [16, 4096], P(None, 'tp'), may hold values from 1 to 16
- skip: float32 [4096], P('tp'), may hold values from 0.2 to 2
Outputs:
- attended: bfloat16 [32768, 4096], P('ctx', 'tp')
- mixed: bfloat16 [32768, 4096], P('ctx', 'tp')
All inputs are finite; a program needn't handle non-finite values.
Results may differ from a plain program's by a relative error of at most 0.0085.
Values may be sent and summed in bfloat16 or wider, within the bound.
No kernel may reach another device: no remote copies, remote signals or barrier semaphores. Data moves between devices by JAX's collectives and lax.ppermute only.
A program may use at most 128 MiB of HBM per device.

v0:
```python
import jax
import jax.numpy as jnp
from jax import lax
from jax.sharding import PartitionSpec as P

HD = 128
WINDOW = 2048
NS = 16


def passed_along(block, axis, distance):
    devices = range(lax.axis_size(axis))
    route = [(i - distance, i) for i in devices if i - distance in devices]
    return lax.ppermute(block, axis, route)


def entering(shard, axis, combine, identity):
    peers, here = (lax.axis_size(axis), lax.axis_index(axis))
    everything = jax.tree.map(lambda part: lax.all_gather(part, axis), shard)
    start = jax.tree.map(
        lambda part, zero: jnp.broadcast_to(jnp.asarray(zero, part.dtype), part.shape),
        shard,
        identity,
    )

    def step(k, before):
        reached = k < here
        new = combine(before, jax.tree.map(lambda part: part[k], everything))
        return jax.tree.map(lambda a, b: jnp.where(reached, a, b), new, before)

    return lax.fori_loop(0, peers, step, start)


def combine_states(earlier, later):
    return (earlier[0] * later[0], later[0] * earlier[1] + later[1])


def sweep_states(start_state, decay_rates, step_sizes, driven, b_rows, c_rows, with_output):
    tok_rows, channels = step_sizes.shape
    length = 32
    blocks = tok_rows // length
    inputs = (
        step_sizes.reshape(blocks, length, channels),
        driven.reshape(blocks, length, channels),
        b_rows.reshape(blocks, length, b_rows.shape[1]),
        c_rows.reshape(blocks, length, c_rows.shape[1]),
    )

    def advance(carried, block_in):
        sizes_block, drive_block, b_block, c_block = block_in
        outputs = []
        for offset in range(length):
            carried = (
                jnp.exp(-sizes_block[offset][None, :] * decay_rates) * carried
                + drive_block[offset][None, :] * b_block[offset][:, None]
            )
            if with_output:
                outputs.append(jnp.sum(c_block[offset][:, None] * carried, axis=0))
        if with_output:
            return (carried, jnp.stack(outputs))
        return (carried, None)

    last_state, produced = lax.scan(advance, start_state, inputs)
    if with_output:
        return (last_state, produced.reshape(tok_rows, channels))
    return (last_state, None)


def window_attention(query, pieces, place, reach):
    tok_rows = query.shape[0]
    ordered = jnp.concatenate(pieces[::-1], axis=1)
    key_pos = (place - reach) * tok_rows + jnp.arange(ordered.shape[1], dtype=jnp.int32)
    query_pos = place * tok_rows + jnp.arange(tok_rows, dtype=jnp.int32)
    allowed = (
        (key_pos[None, :] <= query_pos[:, None])
        & (key_pos[None, :] > query_pos[:, None] - WINDOW)
        & (key_pos[None, :] >= 0)
    )
    scale = HD ** (-0.5)
    heads_dev = query.shape[1] // HD
    results = []
    for head_num in range(heads_dev):
        column = slice(head_num * HD, (head_num + 1) * HD)
        scores = (
            lax.dot_general(
                query[:, column],
                ordered[0][:, column],
                (((1,), (1,)), ((), ())),
                preferred_element_type=jnp.float32,
            )
            * scale
        )
        masked = jnp.where(allowed, scores, -jnp.inf)
        row_max = jnp.max(masked, axis=1, keepdims=True)
        unscaled = jnp.where(allowed, jnp.exp(scores - row_max), 0.0)
        row_sum = jnp.sum(unscaled, axis=1, keepdims=True)
        probs = (unscaled / row_sum).astype(jnp.bfloat16)
        results.append(
            jnp.dot(probs, ordered[1][:, column], preferred_element_type=jnp.float32).astype(
                jnp.bfloat16
            )
        )
    return jnp.concatenate(results, axis=1)


def shards(query, key, value, xin, gate_z, w_bc, dt_low, dt_proj, dt_bias, a_rate, skip):
    tok_rows = query.shape[0]
    place = lax.axis_index("ctx")
    stacked = jnp.stack([key, value])
    reach = WINDOW // tok_rows
    pieces = [stacked]
    for distance in range(1, reach + 1):
        pieces.append(passed_along(stacked, "ctx", distance))
    partial_bc = jnp.dot(xin, w_bc, preferred_element_type=jnp.float32)
    summed_bc = lax.psum(partial_bc, "tp")
    b_rows = summed_bc[:, :NS]
    c_rows = summed_bc[:, NS:]
    step_sizes = jax.nn.softplus(
        jnp.dot(dt_low, dt_proj, preferred_element_type=jnp.float32) + dt_bias[None, :]
    )
    inputs_float = xin.astype(jnp.float32)
    driven = step_sizes * inputs_float
    zero_state = jnp.zeros((NS, step_sizes.shape[1]), jnp.float32)
    local_end, local_out = sweep_states(
        zero_state, a_rate, step_sizes, driven, b_rows, c_rows, False
    )
    through = jnp.sum(step_sizes, axis=0)
    decay_all = jnp.exp(-a_rate * through[None, :])
    prefix = entering(
        (decay_all, local_end),
        "ctx",
        combine_states,
        (jnp.ones_like(decay_all), jnp.zeros_like(local_end)),
    )
    incoming = prefix[1]
    attended = window_attention(query, pieces, place, reach)
    unused_state, outputs = sweep_states(incoming, a_rate, step_sizes, driven, b_rows, c_rows, True)
    mixed = (
        (outputs + skip[None, :] * inputs_float) * jax.nn.silu(gate_z.astype(jnp.float32))
    ).astype(jnp.bfloat16)
    return (attended, mixed)


def solution(mesh):
    in_specs = (
        P("ctx", "tp"),
        P("ctx", "tp"),
        P("ctx", "tp"),
        P("ctx", "tp"),
        P("ctx", "tp"),
        P("tp", None),
        P("ctx", None),
        P(None, "tp"),
        P("tp"),
        P(None, "tp"),
        P("tp"),
    )
    out_specs = (P("ctx", "tp"), P("ctx", "tp"))
    return jax.shard_map(shards, mesh=mesh, in_specs=in_specs, out_specs=out_specs, check_vma=False)
```

profile of v0, /device:TPU:1, one launch (start us, length us, event | category | flops | bytes accessed | tf_op | source)
XLA Modules:
  0.0 662.3 jit_solution(11239584919717683615)
XLA Ops:
  8.6 14.5 %psum.7 = f32[256,32]{0,1:T(8,128)S(1)} all-reduce(f32[256,32]{0,1:T(8,128)S(1)} %fusion.264), channel_id=1, replica_groups=mesh['ctx'=128,'tp'=4] {'tp'}, use_global_device_ids=true, to_apply=%region_17.18 | all-reduce | flops 8192 | bytes 65536 | tf_op jit(solution)/shard_map/psum | solution.py:115
  23.8 2.5 convert_multiply_fusion.2
  26.3 38.5 %while.38 = (s32[]{:T(128)}, f32[16,1024]{1,0:T(8,128)}, f32[8,32,1024]{2,1,0:T(8,128)S(1)}, f32[16,1024]{1,0:T(8,128)S(1)}, f32[8,32,1024]{2,1,0:T(8,128)S(1)},...) while((s32[]{:T(128)}, f32[16,1024]{1,0:T(8,128)}, ...), condition=%wide.region_19.20_spmd.clone, body=%wide.region_18.19_spmd.clone.sunk | while | flops 2146338 | bytes 990295 | solution.py:63
  67.5 8.1 %collective-permute-start = (bf16[2,256,1024]{2,1,0:T(8,128)(2,1)}, bf16[2,256,1024]{2,1,0:T(8,128)(2,1)}, u32[]{:S(2)}, u32[]{:S(2)}) collective-permute-start(bf16[2,256,1024]{2,1,0:T(8,128)(2,1)} %pad_maximum_fusion), channel_id=1, source_target_pairs={{0,32},{4,36},{8,40},{12,44},{16,48},{20,52},{24,56},{28,60},{32,6... | collective-permute-start | bytes 3145736 | tf_op jit(solution)/shard_map/ppermute | solution.py:14
  75.6 8.2 %collective-permute-start.1 = (bf16[2,256,1024]{2,1,0:T(8,128)(2,1)}, bf16[2,256,1024]{2,1,0:T(8,128)(2,1)}, u32[]{:S(2)}, u32[]{:S(2)}) collective-permute-start(bf16[2,256,1024]{2,1,0:T(8,128)(2,1)} %pad_maximum_fusion), channel_id=1, source_target_pairs={{0,28},{4,32},{8,36},{12,40},{16,44},{20,48},{24,52},{28,56},{32,6... | collective-permute-start | bytes 3145736 | tf_op jit(solution)/shard_map/ppermute | solution.py:14
  83.7 5.2 collective-permute-start.2
  91.2 5.2 collective-permute-start.4
  96.5 9.6 %collective-permute-done = bf16[2,256,1024]{2,1,0:T(8,128)(2,1)} collective-permute-done((bf16[2,256,1024]{2,1,0:T(8,128)(2,1)}, bf16[2,256,1024]{2,1,0:T(8,128)(2,1)}, u32[]{:S(2)}, u32[]{:S(2)}) %collective-permute-start) | collective-permute-done | bytes 1048608 | tf_op jit(solution)/shard_map/ppermute | solution.py:14
  106.0 27.5 %collective-permute-start.5 = (bf16[2,256,1024]{2,1,0:T(8,128)(2,1)}, bf16[2,256,1024]{2,1,0:T(8,128)(2,1)}, u32[]{:S(2)}, u32[]{:S(2)}) collective-permute-start(bf16[2,256,1024]{2,1,0:T(8,128)(2,1)} %pad_maximum_fusion), channel_id=1, source_target_pairs={{0,12},{4,16},{8,20},{12,24},{16,28},{20,32},{24,36},{28,40},{32,4... | collective-permute-start | bytes 3145736 | tf_op jit(solution)/shard_map/ppermute | solution.py:14
  133.7 31.2 %collective-permute-done.1 = bf16[2,256,1024]{2,1,0:T(8,128)(2,1)} collective-permute-done((bf16[2,256,1024]{2,1,0:T(8,128)(2,1)}, bf16[2,256,1024]{2,1,0:T(8,128)(2,1)}, u32[]{:S(2)}, u32[]{:S(2)}) %collective-permute-start.1) | collective-permute-done | bytes 1048608 | tf_op jit(solution)/shard_map/ppermute | solution.py:14
  166.2 66.4 %collective-permute-done.2 = bf16[2,256,1024]{2,1,0:T(8,128)(2,1)} collective-permute-done((bf16[2,256,1024]{2,1,0:T(8,128)(2,1)}, bf16[2,256,1024]{2,1,0:T(8,128)(2,1)}, u32[]{:S(2)}, u32[]{:S(2)}) %collective-permute-start.2) | collective-permute-done | bytes 1048608 | tf_op jit(solution)/shard_map/ppermute | solution.py:14
  232.6 60.1 %collective-permute-start.7 = (bf16[2,256,1024]{2,1,0:T(8,128)(2,1)}, bf16[2,256,1024]{2,1,0:T(8,128)(2,1)S(1)}, u32[]{:S(2)}, u32[]{:S(2)}) collective-permute-start(bf16[2,256,1024]{2,1,0:T(8,128)(2,1)} %pad_maximum_fusion), channel_id=1, source_target_pairs={{0,4},{4,8},{8,12},{12,16},{16,20},{20,24},{24,28},{28,32},{32,36}... | collective-permute-start | bytes 3145736 | tf_op jit(solution)/shard_map/ppermute | solution.py:14
  302.0 9.0 %collective-permute-done.4 = bf16[2,256,1024]{2,1,0:T(8,128)(2,1)} collective-permute-done((bf16[2,256,1024]{2,1,0:T(8,128)(2,1)}, bf16[2,256,1024]{2,1,0:T(8,128)(2,1)}, u32[]{:S(2)}, u32[]{:S(2)}) %collective-permute-start.4) | collective-permute-done | bytes 1048608 | tf_op jit(solution)/shard_map/ppermute | solution.py:14
  311.0 2.3 constant_dynamic-update-slice_fusion.4
  313.3 79.2 %collective-permute-done.5 = bf16[2,256,1024]{2,1,0:T(8,128)(2,1)} collective-permute-done((bf16[2,256,1024]{2,1,0:T(8,128)(2,1)}, bf16[2,256,1024]{2,1,0:T(8,128)(2,1)}, u32[]{:S(2)}, u32[]{:S(2)}) %collective-permute-start.5) | collective-permute-done | bytes 1048608 | tf_op jit(solution)/shard_map/ppermute | solution.py:14
  394.8 25.3 %collective-permute-done.6 = bf16[2,256,1024]{2,1,0:T(8,128)(2,1)S(1)} collective-permute-done((bf16[2,256,1024]{2,1,0:T(8,128)(2,1)}, bf16[2,256,1024]{2,1,0:T(8,128)(2,1)S(1)}, u32[]{:S(2)}, u32[]{:S(2)}) %collective-permute-start.6) | collective-permute-done | bytes 1048608 | tf_op jit(solution)/shard_map/ppermute | solution.py:14
  421.1 14.0 %collective-permute-done.7 = bf16[2,256,1024]{2,1,0:T(8,128)(2,1)S(1)} collective-permute-done((bf16[2,256,1024]{2,1,0:T(8,128)(2,1)}, bf16[2,256,1024]{2,1,0:T(8,128)(2,1)S(1)}, u32[]{:S(2)}, u32[]{:S(2)}) %collective-permute-start.7) | collective-permute-done | bytes 1048608 | tf_op jit(solution)/shard_map/ppermute | solution.py:14
  437.3 7.1 %slice_bitcast_fusion = (bf16[2304,1024]{1,0:T(8,128)(2,1)}, bf16[2304,1024]{1,0:T(8,128)(2,1)S(1)}) fusion(bf16[2,2304,1024]{2,1,0:T(8,128)(2,1)} %constant_dynamic-update-slice_fusion), kind=kLoop, calls=%fused_computation.478 | loop fusion | bytes 18874368 | tf_op jit(solution)/shard_map/squeeze | solution.py:99
  448.3 2.5 fusion.200
  452.2 4.0 fusion.199
  466.4 37.8 %all-gather.5.cloned.1.call-done = f32[2048,1024]{1,0:T(8,128)} async-done(((f32[16,1024]{1,0:T(8,128)}), f32[2048,1024]{1,0:T(8,128)}) %all-gather.5.cloned.1.call-update) | async-done | bytes 8388624 | tf_op jit(solution)/shard_map/all_gather | solution.py:19
  504.2 119.9 %while.39 = (s32[]{:T(128)}, f32[16,1024]{1,0:T(8,128)S(1)}, s32[]{:T(128)}, f32[128,16,1024]{2,1,0:T(8,128)}, f32[128,16,1024]{2,1,0:T(8,128)}, /*index=5*/s32[]{:T(128)}, s32[]{:T(128)}) while((s32[]{:T(128)}, f32[16,1024]{1,0:T(8,128)S(1)}, s32[]{:T(128)}, f32[128,16,1024]{2,1,0:T(8,128)}, f32[128,16,1024]{2,1,0:T(8,128)}, ...), condition=%wide.region_21.22_spmd.clone, body=%wide.region_20.21_spmd.clone.sunk | while | flops 65540 | bytes 262245 | solution.py:31
  624.1 28.7 %while.37 = (s32[]{:T(128)}, f32[16,1024]{1,0:T(8,128)S(1)}, f32[8,32,1024]{2,1,0:T(8,128)}, f32[8,32,1024]{2,1,0:T(8,128)S(1)}, f32[16,1024]{1,0:T(8,128)S(1)},...) while((s32[]{:T(128)}, f32[16,1024]{1,0:T(8,128)S(1)}, ...), condition=%wide.region_55.56_spmd, body=%wide.region_22.55_spmd.sunk | while | flops 4718625 | bytes 3357861 | solution.py:63
  652.8 2.6 fusion.227
  (395 shorter events, 221.6 us)
Async XLA Ops:
  7.2 16.6 %copy-start = (bf16[256,1024]{1,0:T(8,128)(2,1)S(1)}, bf16[256,1024]{1,0:T(8,128)(2,1)}, u32[]{:S(2)}) copy-start(bf16[256,1024]{1,0:T(8,128)(2,1)} %param.24) | copy-start | bytes 1572868
  7.2 459.2 %all-gather.7.cloned.1.call-start = ((), (), s32[]{:S(2)}) async-start(), calls=%async_computation.1 | async-start | bytes 8454144 | tf_op jit(solution)/shard_map/all_gather | solution.py:19
  7.2 19.1 %copy-start.2 = (f32[16,1024]{1,0:T(8,128)S(1)}, f32[16,1024]{1,0:T(8,128)}, u32[]{:S(2)}) copy-start(f32[16,1024]{1,0:T(8,128)} %param.26) | copy-start | bytes 196612
  26.3 40.0 %copy-start.4 = (bf16[256,1024]{1,0:T(8,128)(2,1)S(1)}, bf16[256,1024]{1,0:T(8,128)(2,1)}, u32[]{:S(2)}) copy-start(bf16[256,1024]{1,0:T(8,128)(2,1)} %param.19) | copy-start | bytes 1572868
  26.3 40.0 %copy-start.5 = (bf16[256,1024]{1,0:T(8,128)(2,1)S(1)}, bf16[256,1024]{1,0:T(8,128)(2,1)}, u32[]{:S(2)}) copy-start(bf16[256,1024]{1,0:T(8,128)(2,1)} %param.18) | copy-start | bytes 1572868
  64.9 68.7 %copy-start.7 = (f32[256,16]{0,1:T(8,128)S(1)}, f32[256,16]{0,1:T(8,128)}, u32[]{:S(2)}) copy-start(f32[256,16]{0,1:T(8,128)} %get-tuple-element.564) | copy-start | bytes 49156
  64.9 439.3 %all-gather.5.cloned.1.call-start = ((), (), s32[]{:S(2)}) async-start(), calls=%async_computation | async-start | bytes 8454144 | tf_op jit(solution)/shard_map/all_gather | solution.py:19
  67.5 38.6 %collective-permute-start = (bf16[2,256,1024]{2,1,0:T(8,128)(2,1)}, bf16[2,256,1024]{2,1,0:T(8,128)(2,1)}, u32[]{:S(2)}, u32[]{:S(2)}) collective-permute-start(bf16[2,256,1024]{2,1,0:T(8,128)(2,1)} %pad_maximum_fusion), channel_id=1, source_target_pairs={{0,32},{4,36},{8,40},{12,44},{16,48},{20,52},{24,56},{28,60},{32,6... | collective-permute-start | bytes 3145736 | tf_op jit(solution)/shard_map/ppermute | solution.py:14
  75.6 89.3 %collective-permute-start.1 = (bf16[2,256,1024]{2,1,0:T(8,128)(2,1)}, bf16[2,256,1024]{2,1,0:T(8,128)(2,1)}, u32[]{:S(2)}, u32[]{:S(2)}) collective-permute-start(bf16[2,256,1024]{2,1,0:T(8,128)(2,1)} %pad_maximum_fusion), channel_id=1, source_target_pairs={{0,28},{4,32},{8,36},{12,40},{16,44},{20,48},{24,52},{28,56},{32,6... | collective-permute-start | bytes 3145736 | tf_op jit(solution)/shard_map/ppermute | solution.py:14
  83.7 148.9 %collective-permute-start.2 = (bf16[2,256,1024]{2,1,0:T(8,128)(2,1)}, bf16[2,256,1024]{2,1,0:T(8,128)(2,1)}, u32[]{:S(2)}, u32[]{:S(2)}) collective-permute-start(bf16[2,256,1024]{2,1,0:T(8,128)(2,1)} %pad_maximum_fusion), channel_id=1, source_target_pairs={{0,24},{4,28},{8,32},{12,36},{16,40},{20,44},{24,48},{28,52},{32,5... | collective-permute-start | bytes 3145736 | tf_op jit(solution)/shard_map/ppermute | solution.py:14
  89.0 210.7 %collective-permute-start.3 = (bf16[2,256,1024]{2,1,0:T(8,128)(2,1)}, bf16[2,256,1024]{2,1,0:T(8,128)(2,1)}, u32[]{:S(2)}, u32[]{:S(2)}) collective-permute-start(bf16[2,256,1024]{2,1,0:T(8,128)(2,1)} %pad_maximum_fusion), channel_id=1, source_target_pairs={{0,20},{4,24},{8,28},{12,32},{16,36},{20,40},{24,44},{28,48},{32,5... | collective-permute-start | bytes 3145736 | tf_op jit(solution)/shard_map/ppermute | solution.py:14
  91.2 219.7 %collective-permute-start.4 = (bf16[2,256,1024]{2,1,0:T(8,128)(2,1)}, bf16[2,256,1024]{2,1,0:T(8,128)(2,1)}, u32[]{:S(2)}, u32[]{:S(2)}) collective-permute-start(bf16[2,256,1024]{2,1,0:T(8,128)(2,1)} %pad_maximum_fusion), channel_id=1, source_target_pairs={{0,16},{4,20},{8,24},{12,28},{16,32},{20,36},{24,40},{28,44},{32,4... | collective-permute-start | bytes 3145736 | tf_op jit(solution)/shard_map/ppermute | solution.py:14
  106.0 286.4 %collective-permute-start.5 = (bf16[2,256,1024]{2,1,0:T(8,128)(2,1)}, bf16[2,256,1024]{2,1,0:T(8,128)(2,1)}, u32[]{:S(2)}, u32[]{:S(2)}) collective-permute-start(bf16[2,256,1024]{2,1,0:T(8,128)(2,1)} %pad_maximum_fusion), channel_id=1, source_target_pairs={{0,12},{4,16},{8,20},{12,24},{16,28},{20,32},{24,36},{28,40},{32,4... | collective-permute-start | bytes 3145736 | tf_op jit(solution)/shard_map/ppermute | solution.py:14
  164.8 255.2 %collective-permute-start.6 = (bf16[2,256,1024]{2,1,0:T(8,128)(2,1)}, bf16[2,256,1024]{2,1,0:T(8,128)(2,1)S(1)}, u32[]{:S(2)}, u32[]{:S(2)}) collective-permute-start(bf16[2,256,1024]{2,1,0:T(8,128)(2,1)} %pad_maximum_fusion), channel_id=1, source_target_pairs={{0,8},{4,12},{8,16},{12,20},{16,24},{20,28},{24,32},{28,36},{32,40... | collective-permute-start | bytes 3145736 | tf_op jit(solution)/shard_map/ppermute | solution.py:14
  232.6 202.5 %collective-permute-start.7 = (bf16[2,256,1024]{2,1,0:T(8,128)(2,1)}, bf16[2,256,1024]{2,1,0:T(8,128)(2,1)S(1)}, u32[]{:S(2)}, u32[]{:S(2)}) collective-permute-start(bf16[2,256,1024]{2,1,0:T(8,128)(2,1)} %pad_maximum_fusion), channel_id=1, source_target_pairs={{0,4},{4,8},{8,12},{12,16},{16,20},{20,24},{24,28},{28,32},{32,36}... | collective-permute-start | bytes 3145736 | tf_op jit(solution)/shard_map/ppermute | solution.py:14
  437.3 7.1 %copy-start.6 = (bf16[256,1024]{1,0:T(8,128)(2,1)S(1)}, bf16[256,1024]{1,0:T(8,128)(2,1)}, u32[]{:S(2)}) copy-start(bf16[256,1024]{1,0:T(8,128)(2,1)} %param.17) | copy-start | bytes 1572868
  447.2 3.6 slice-start
  448.3 2.5 slice-start.1
  624.1 28.7 %copy-start.3 = (bf16[256,1024]{1,0:T(8,128)(2,1)S(1)}, bf16[256,1024]{1,0:T(8,128)(2,1)}, u32[]{:S(2)}) copy-start(bf16[256,1024]{1,0:T(8,128)(2,1)} %param.20) | copy-start | bytes 1572868
  624.1 28.7 %copy-start.8 = (f32[1024]{0:T(1024)S(1)}, f32[1024]{0:T(1024)}, u32[]{:S(2)}) copy-start(f32[1024]{0:T(1024)} %param.27) | copy-start | bytes 12292
  652.8 2.6 copy-start.1
Sparse Core Ops, SparseCore 0:
  65.0 344.9 all-gather.6
  413.1 90.9 all-gather.4
where the time goes:
time: 669 us; the launch traced here: 662 us
  waiting for transfers between devices  272 us (41%)
  other arithmetic  169 us (25%)
  starting transfers between devices  118 us (18%)
  local copies, waits for them, and re-layouts  49.5 us (7%)
  matrix products  20.8 us (3%)
  blocking collectives  14.5 us (2%)
  between operations  14.3 us (2%)
    ppermute x8, waiting for transfers between devices, passed_along(): return lax.ppermute(block, axis, route)  235 us
    ppermute x8, starting transfers between devices, passed_along(): return lax.ppermute(block, axis, route)  118 us
    select_n x128, other arithmetic, step(): return jax.tree.map(lambda a, b: jnp.where(reached, a, b), new, before)  117 us
    all_gather x2, waiting for transfers between devices, entering(): everything = jax.tree.map(lambda part: lax.all_gather(part, axis), shard)  37.8 us
    add x8, other arithmetic, advance(): jnp.exp(-sizes_block[offset][None, :] * decay_rates) * carried  18.2 us
    unnamed x32, local copies, waits for them, and re-layouts  17.1 us
    psum x1, blocking collectives, shards(): summed_bc = lax.psum(partial_bc, 'tp')  14.5 us
    reduce_sum x72, other arithmetic, advance(): outputs.append(jnp.sum(c_block[offset][:, None] * carried, axis=0))  14.1 us
  transfers between devices with their start and end apart: 10, of which 8 were waited for; matrix products, arithmetic and copies ran while one was open for 7% of the time, Pallas kernels for 0%

commit v1 on v0

v1 whole, which is shorter than its diff:
```python
import jax
import jax.numpy as jnp
from jax import lax
from jax.experimental import pallas as pl
from jax.experimental.pallas import tpu as pltpu
from jax.sharding import PartitionSpec as P


HD = 128
WINDOW = 2048
NS = 16
LANES = 128
TILES = 8
LOG2E = 1.4426950408889634
F32 = jnp.float32
BF16 = jnp.bfloat16
VMEM = pl.BlockSpec(memory_space=pltpu.VMEM)
SMEM = pl.BlockSpec(memory_space=pltpu.SMEM)


def cost(flops, moved, exps=0):
    return pl.CostEstimate(flops=flops, bytes_accessed=moved, transcendentals=exps)


def local(body, outs, scratch=(), scalars=0, arrays=1, estimate=None, limit=48 << 20):
    return pl.pallas_call(
        body,
        out_shape=outs,
        in_specs=[SMEM] * scalars + [VMEM] * arrays,
        out_specs=jax.tree.map(lambda _: VMEM, outs),
        scratch_shapes=list(scratch),
        cost_estimate=estimate,
        compiler_params=pltpu.CompilerParams(vmem_limit_bytes=limit),
    )


def parity_of(place):
    return place[0] & 1


def plane_of(place):
    return place[0] >> 4


def pack_body(*refs):
    *ins, out = refs
    rows = ins[0].shape[0]
    for head in range(out.shape[0]):
        for k, part in enumerate(ins):
            out[head, k * rows : (k + 1) * rows, :] = part[:, head * HD : (head + 1) * HD]


def pack(*parts):
    rows, width = parts[0].shape
    out = jax.ShapeDtypeStruct((width // HD, len(parts) * rows, HD), BF16)
    moved = 4 * len(parts) * rows * width
    return local(pack_body, out, arrays=len(parts), estimate=cost(0, moved))(*parts)


def unpack_body(blocks, out):
    for head in range(blocks.shape[0]):
        out[:, head * HD : (head + 1) * HD] = blocks[head]


def unpack(blocks):
    heads, rows, _ = blocks.shape
    out = jax.ShapeDtypeStruct((rows, heads * HD), BF16)
    return local(unpack_body, out, estimate=cost(0, 4 * rows * heads * HD))(blocks)


def attend_body(place, queries, own, other, old, past, out, ko, vo, kp, vp):
    blocks, rows, _ = queries.shape
    half = old.shape[0]
    parity = parity_of(place)
    live = plane_of(place) > 0
    key0 = jnp.where(parity == 0, own[0, 0:1, :].astype(F32), other[0, 0:1, :].astype(F32))
    key0 = jnp.broadcast_to(key0, (rows, HD)).astype(BF16)
    ones = jnp.ones((rows, HD), BF16)
    shown = jnp.where(live, jnp.ones((rows, HD), F32), jnp.zeros((rows, HD), F32)).astype(BF16)
    for keys, values, source in ((ko, vo, old), (kp, vp, past)):
        for b in range(half):
            at = slice(b * rows, (b + 1) * rows)
            values[at, 0:HD] = source[b, rows : 2 * rows, :]
            values[at, HD : 2 * HD] = shown

        @pl.when(live)
        def _():
            for b in range(half):
                keys[b * rows : (b + 1) * rows, :] = source[b, 0:rows, :]

        @pl.when(jnp.logical_not(live))
        def _():
            for b in range(half):
                keys[b * rows : (b + 1) * rows, :] = key0

    for keys, values, source in ((ko, vo, own), (kp, vp, other)):
        for b in range(blocks):
            at = slice((half + b) * rows, (half + b + 1) * rows)
            keys[at, :] = source[b, 0:rows, :]
            values[at, 0:HD] = source[b, rows : 2 * rows, :]
            values[at, HD : 2 * HD] = ones
    scale = HD**-0.5 * LOG2E
    columns = lax.broadcasted_iota(jnp.int32, (rows, rows), 1)
    below = columns <= lax.broadcasted_iota(jnp.int32, (rows, rows), 0)

    def dots(q, k):
        return lax.dot_general(q, k, (((1,), (1,)), ((), ())), preferred_element_type=F32)

    def span(block, count):
        return pl.ds(pl.multiple_of(block * rows, rows), count * rows)

    def one(i, carry):
        q = queries[i]
        edge = jnp.where(below, dots(q, ko[span(i + half, 1), :]), dots(q, ko[span(i, 1), :]))
        mid = dots(q, ko[span(i + 1, half - 1), :])
        par = dots(q, kp[span(i + parity, half), :])
        top = None
        for part in (edge, mid, par):
            for c in range(0, part.shape[1], LANES):
                piece = part[:, c : c + LANES]
                top = piece if top is None else jnp.maximum(top, piece)
        top = jnp.max(top, axis=1, keepdims=True) * scale
        weight = jnp.exp2(edge * scale - top)
        near = jnp.where(below, weight, 0.0).astype(BF16)
        far = jnp.where(below, 0.0, weight).astype(BF16)
        w_mid = jnp.exp2(mid * scale - top).astype(BF16)
        w_par = jnp.exp2(par * scale - top).astype(BF16)
        total = jnp.dot(w_mid, vo[span(i + 1, half - 1), :], preferred_element_type=F32)
        total += jnp.dot(w_par, vp[span(i + parity, half), :], preferred_element_type=F32)
        total += jnp.dot(near, vo[span(i + half, 1), :], preferred_element_type=F32)
        total += jnp.dot(far, vo[span(i, 1), :], preferred_element_type=F32)
        out[i] = (total[:, 0:HD] / total[:, HD : 2 * HD]).astype(BF16)
        return carry

    lax.fori_loop(0, blocks, one, 0, unroll=2)


def attend(place, queries, own, other, old, past):
    blocks, rows, _ = queries.shape
    ext = (blocks + old.shape[0]) * rows
    scratch = [pltpu.VMEM((ext, HD), BF16), pltpu.VMEM((ext, 2 * HD), BF16)] * 2
    out = jax.ShapeDtypeStruct(queries.shape, BF16)
    estimate = cost(4 * blocks * rows * WINDOW * 2 * HD, 8 << 20, blocks * rows * WINDOW)
    return local(attend_body, out, scratch, 1, 5, estimate)(place, queries, own, other, old, past)


def rows_of(step):
    return pl.ds(pl.multiple_of(step * TILES, TILES), TILES)


def project_body(xin, w_bc, out):
    out[...] = jnp.dot(xin[...], w_bc[...], preferred_element_type=F32).T


def project(xin, w_bc):
    out = jax.ShapeDtypeStruct((w_bc.shape[1], xin.shape[0]), F32)
    return local(project_body, out, arrays=2, estimate=cost(0, 2 * xin.size))(xin, w_bc)


def steps_body(low, proj, bias, xin, steps, drive):
    rows = low.shape[0]
    for c in range(TILES):
        col = slice(c * LANES, (c + 1) * LANES)
        raw = jnp.dot(low[...], proj[:, col], preferred_element_type=F32) + bias[:, col]
        size = jnp.maximum(raw, 0.0) + jnp.log1p(jnp.exp(-jnp.abs(raw)))
        steps[pl.ds(c, rows, stride=TILES), :] = size
        drive[pl.ds(c, rows, stride=TILES), :] = size * xin[:, col].astype(F32)


def step_sizes(low, proj, bias, xin):
    rows, width = xin.shape
    out = jax.ShapeDtypeStruct((rows * TILES, LANES), F32)
    estimate = cost(2 * rows * low.shape[1] * width, 12 * rows * width, 2 * rows * width)
    return local(steps_body, (out, out), arrays=4, estimate=estimate)(
        low, proj, bias.reshape(1, -1), xin
    )


def spread(parts, count, wide):
    total = parts[0][0:count, :]
    for part in parts[1:]:
        total = total + part[0:count, :]
    total = total.T
    rows = total.shape[0]
    for n in range(count):
        column = jnp.broadcast_to(total[:, n : n + 1], (rows, LANES))
        wide[pl.ds(n, rows, stride=count), :] = column


def load_rates(a_rate, held):
    for c in range(TILES):
        held[pl.ds(c, NS, stride=TILES), :] = a_rate[:, c * LANES : (c + 1) * LANES] * -LOG2E
    return [held[n * TILES : (n + 1) * TILES, :] for n in range(NS)]


def ends_body(steps, drive, p0, p1, p2, p3, a_rate, out, held, wide):
    rows = p0.shape[1]
    spread((p0, p1, p2, p3), NS, wide)
    rates = load_rates(a_rate, held)

    def step(t, carry):
        state, through = carry
        size, push = steps[rows_of(t), :], drive[rows_of(t), :]
        state = tuple(
            jnp.exp2(size * rates[n]) * state[n] + push * wide[pl.ds(t * NS + n, 1), :]
            for n in range(NS)
        )
        return state, through + size

    zero = jnp.zeros((TILES, LANES), F32)
    state, through = lax.fori_loop(0, rows, step, ((zero,) * NS, zero), unroll=4)
    for n in range(NS):
        out[n * TILES : (n + 1) * TILES, :] = state[n]
    out[NS * TILES :, :] = through


def block_ends(steps, drive, partials, a_rate):
    rows = partials[0].shape[1]
    out = jax.ShapeDtypeStruct(((NS + 1) * TILES, LANES), F32)
    rates = jax.ShapeDtypeStruct((NS * TILES, LANES), F32)
    scratch = [pltpu.VMEM((rows * NS, LANES), F32)]
    estimate = cost(6 * steps.size * NS, 8 * steps.size, steps.size * NS)
    return local(ends_body, (out, rates), scratch, 0, 7, estimate)(steps, drive, *partials, a_rate)


def fold(rates, parts):
    state = [parts[0][n * TILES : (n + 1) * TILES, :] for n in range(NS)]
    through = parts[0][NS * TILES :, :]
    for part in parts[1:]:
        size = part[NS * TILES :, :]
        for n in range(NS):
            row = slice(n * TILES, (n + 1) * TILES)
            state[n] = jnp.exp2(size * rates[row, :]) * state[n] + part[row, :]
        through = through + size
    return state, through


def join_body(rates, *refs):
    *parts, out = refs
    state, through = fold(rates, parts)
    for n in range(NS):
        out[n * TILES : (n + 1) * TILES, :] = state[n]
    out[NS * TILES :, :] = through


def join(rates, parts):
    out = jax.ShapeDtypeStruct(parts[0].shape, F32)
    estimate = cost(1 << 16, 1 << 18)
    return local(join_body, out, arrays=1 + len(parts), estimate=estimate)(rates, *parts)


def final_body(steps, drive, p0, p1, p2, p3, held, e0, e1, e2, e3, xin, gate, skip, out, wide, mix):
    rows = p0.shape[1]
    spread((p0, p1, p2, p3), 2 * NS, wide)
    rates = [held[n * TILES : (n + 1) * TILES, :] for n in range(NS)]
    state, _ = fold(held, (e0, e1, e2, e3))

    def step(t, state):
        size, push = steps[rows_of(t), :], drive[rows_of(t), :]
        after = []
        result = None
        for n in range(NS):
            at = t * 2 * NS + n
            now = jnp.exp2(size * rates[n]) * state[n] + push * wide[pl.ds(at, 1), :]
            after.append(now)
            term = now * wide[pl.ds(at + NS, 1), :]
            result = term if result is None else result + term
        mix[rows_of(t), :] = result
        return tuple(after)

    lax.fori_loop(0, rows, step, tuple(state), unroll=4)
    for c in range(TILES):
        col = slice(c * LANES, (c + 1) * LANES)
        mixed = mix[pl.ds(c, rows, stride=TILES), :] + skip[:, col] * xin[:, col].astype(F32)
        opened = gate[:, col].astype(F32)
        out[:, col] = (mixed * (opened / (1.0 + jnp.exp(-opened)))).astype(BF16)


def finish(steps, drive, partials, rates, entering, xin, gate, skip):
    rows = xin.shape[0]
    out = jax.ShapeDtypeStruct(xin.shape, BF16)
    scratch = [
        pltpu.VMEM((rows * 2 * NS, LANES), F32),
        pltpu.VMEM(steps.shape, F32),
    ]
    estimate = cost(9 * steps.size * NS, 14 * steps.size, steps.size * NS)
    return local(final_body, out, scratch, 0, 14, estimate)(
        steps, drive, *partials, rates, *entering, xin, gate, skip.reshape(1, -1)
    )


def exchange(x, groups):
    return lax.all_to_all(x, "ctx", 0, 0, axis_index_groups=groups, tiled=True)


def after(part, distance):
    count = lax.axis_size("ctx")
    return lax.ppermute(part, "ctx", [(i, i + distance) for i in range(count - distance)])


def shards(query, key, value, xin, gate_z, w_bc, dt_low, dt_proj, dt_bias, a_rate, skip):
    ctx, tp = lax.axis_size("ctx"), lax.axis_size("tp")
    side, planes = 8, ctx // 16
    line = 2 * side
    index = lax.axis_index("ctx")
    place = index.astype(jnp.int32).reshape(1)
    along_y = [[z * line + 2 * y + c for y in range(side)] for z in range(planes) for c in (0, 1)]
    partner = [(i, i ^ 1) for i in range(ctx)]
    next_row = [(i, i + line) for i in range(ctx - line)]

    own_kv = exchange(pack(key, value), along_y)
    partial = project(xin, w_bc)
    partials = [partial] + [
        lax.ppermute(partial, "tp", [(i, (i + d) % tp) for i in range(tp)])
        for d in range(1, tp)
    ]
    steps, drive = step_sizes(dt_low, dt_proj, dt_bias, xin)
    ends, rates = block_ends(steps, drive, partials, a_rate)
    queries = pack(query)
    own_kv, queries = lax.optimization_barrier((own_kv, queries))
    queries = exchange(queries, along_y)
    other_kv = lax.ppermute(own_kv, "ctx", partner)
    old_kv = lax.ppermute(own_kv[side // 2 :], "ctx", next_row)
    past_kv = lax.ppermute(old_kv, "ctx", partner)
    ends = join(rates, [after(ends, 2), after(ends, 1)])
    for stride in (2, 8):
        ends = join(rates, [after(ends, d * stride) for d in (3, 2, 1)] + [ends])
    entering = [after(ends, d * 32) for d in (3, 2, 1)] + [ends]
    attended = attend(place, queries, own_kv, other_kv, old_kv, past_kv)
    attended = exchange(attended, along_y)
    attended = unpack(attended)
    mixed = finish(
        steps, drive, partials, rates, entering, xin, gate_z, skip
    )
    return (attended, mixed)


def solution(mesh):
    in_specs = (
        P("ctx", "tp"),
        P("ctx", "tp"),
        P("ctx", "tp"),
        P("ctx", "tp"),
        P("ctx", "tp"),
        P("tp", None),
        P("ctx", None),
        P(None, "tp"),
        P("tp"),
        P(None, "tp"),
        P("tp"),
    )
    out_specs = (P("ctx", "tp"), P("ctx", "tp"))
    return jax.shard_map(shards, mesh=mesh, in_specs=in_specs, out_specs=out_specs, check_vma=False)
```

time: 669 us -> 175 us (0.26)
  the two profiles are of different devices: /device:TPU:1 before, /device:TPU:6 now
where the time goes in v1:
time: 175 us; the launch traced here: 174 us
  starting transfers between devices  83.8 us (48%)
  waiting for transfers between devices  56.3 us (32%)
  Pallas kernels  29.5 us (17%)
  local copies, waits for them, and re-layouts  3.12 us (2%)
    ppermute x11, starting transfers between devices, after(): lax.ppermute(part, 'ctx', [(i, i + distance) for i in range(count - dista...  52.7 us
    all_to_all x3, waiting for transfers between devices, exchange(): return lax.all_to_all(x, 'ctx', 0, 0, axis_index_groups=groups, tiled=True)  38.1 us
    all_to_all x3, starting transfers between devices, exchange(): return lax.all_to_all(x, 'ctx', 0, 0, axis_index_groups=groups, tiled=True)  14.4 us
    pallas_call x1, Pallas kernels, attend(): local(attend_body, out, scratch, 1, 5, estimate)  11.4 us
    pallas_call x1, Pallas kernels, finish(): local(final_body, out, scratch, 0, 14, estimate)  9.31 us
    ppermute x3, starting transfers between devices, shards(): lax.ppermute(partial, 'tp', [(i, (i + d) % tp) for i in range(tp)])  8.62 us
    ppermute x11, waiting for transfers between devices, after(): lax.ppermute(part, 'ctx', [(i, i + distance) for i in range(count - dista...  7.95 us
    ppermute x1, waiting for transfers between devices, shards(): old_kv = lax.ppermute(own_kv[side // 2:], 'ctx', next_row)  6.19 us
  transfers between devices with their start and end apart: 20, of which 11 were waited for; matrix products, arithmetic and copies ran while one was open for 0% of the time, Pallas kernels for 9%

profile of v1, /device:TPU:6, one launch (start us, length us, event | category | flops | bytes accessed | tf_op | source)
XLA Modules:
  0.0 173.7 jit_solution(16140090662347648868)
XLA Ops:
  3.9 7.2 %all-to-all-start = ((bf16[8,512,128]{2,1,0:T(8,128)(2,1)}), bf16[8,512,128]{2,1,0:T(8,128)(2,1)S(1)}, u32[]{:S(2)}, u32[]{:S(2)}) async-start(bf16[8,512,128]{2,1,0:T(8,128)(2,1)} %shard_map.122), calls=%async_computation | async-start | bytes 2097152 | tf_op jit(solution)/shard_map/all_to_all | solution.py:293
  12.0 27.8 %all-to-all-done.own = bf16[8,512,128]{2,1,0:T(8,128)(2,1)S(1)} async-done(((bf16[8,512,128]{2,1,0:T(8,128)(2,1)}), bf16[8,512,128]{2,1,0:T(8,128)(2,1)S(1)}, u32[]{:S(2)}, u32[]{:S(2)}) %all-to-all-start) | async-done | bytes 1048608 | tf_op jit(solution)/shard_map/all_to_all | solution.py:293
  40.7 4.3 %collective-permute-start.1 = (bf16[4,512,128]{2,1,0:T(8,128)(2,1)}, bf16[4,512,128]{2,1,0:T(8,128)(2,1)S(1)}, u32[]{:S(2)}, u32[]{:S(2)}) collective-permute-start(bf16[4,512,128]{2,1,0:T(8,128)(2,1)} %slice.3), channel_id=1, source_target_pairs={{0,64},{4,68},{8,72},{12,76},{16,80},{20,84},{24,88},{28,92},{32,9... | collective-permute-start | bytes 1572872 | tf_op jit(solution)/shard_map/ppermute | solution.py:323
  45.0 1.9 %collective-permute-start = (bf16[8,512,128]{2,1,0:T(8,128)(2,1)S(1)}, bf16[8,512,128]{2,1,0:T(8,128)(2,1)S(1)}, u32[]{:S(2)}, u32[]{:S(2)}) collective-permute-start(bf16[8,512,128]{2,1,0:T(8,128)(2,1)S(1)} %all-to-all-done.own), channel_id=1, source_target_pairs={{0,4},{4,0},{8,12},{12,8},{16,20},{20,16},{24,28},{28,24},{32,36},... | collective-permute-start | bytes 3145736 | tf_op jit(solution)/shard_map/ppermute | solution.py:322
  46.9 3.5 %all-to-all-start.1 = ((bf16[8,256,128]{2,1,0:T(8,128)(2,1)}), bf16[8,256,128]{2,1,0:T(8,128)(2,1)S(1)}, u32[]{:S(2)}, u32[]{:S(2)}) async-start(bf16[8,256,128]{2,1,0:T(8,128)(2,1)} %shard_map.123), calls=%async_computation.1 | async-start | bytes 1048576 | tf_op jit(solution)/shard_map/all_to_all | solution.py:293
  50.4 6.2 %collective-permute-done.1.old = bf16[4,512,128]{2,1,0:T(8,128)(2,1)S(1)} collective-permute-done((bf16[4,512,128]{2,1,0:T(8,128)(2,1)}, bf16[4,512,128]{2,1,0:T(8,128)(2,1)S(1)}, u32[]{:S(2)}, u32[]{:S(2)}) %collective-permute-start.1) | collective-permute-done | bytes 524320 | tf_op jit(solution)/shard_map/ppermute | solution.py:323
  58.5 10.3 %all-to-all-done.1.queries = bf16[8,256,128]{2,1,0:T(8,128)(2,1)S(1)} async-done(((bf16[8,256,128]{2,1,0:T(8,128)(2,1)}), bf16[8,256,128]{2,1,0:T(8,128)(2,1)S(1)}, u32[]{:S(2)}, u32[]{:S(2)}) %all-to-all-start.1) | async-done | bytes 524320 | tf_op jit(solution)/shard_map/all_to_all | solution.py:293
  68.8 11.4 %shard_map.124 = bf16[8,256,128]{2,1,0:T(8,128)(2,1)} custom-call(s32[1]{0:T(128)} %bitcast.place, bf16[8,256,128]{2,1,0:T(8,128)(2,1)S(1)} %all-to-all-done.1.queries, bf16[8,512,128]{2,1,0:T(8,128)(2,1)S(1)} %all-to-all-done.own, bf16[8,512,128]{2,1,0:T(8,128)(2,1)S(1)} %collective-permute-done.other, bf16[4,512,128]{2,1,0:T(8,128)(2,1)S(1)} %collective-permute-done.1.old, ...), custom_call_target="tpu_custom_call" | custom-call | flops 4294967296 | bytes 8388608 | tf_op jit(solution)/shard_map/pallas_call | solution.py:144
  80.2 3.6 %all-to-all-start.2 = ((bf16[8,256,128]{2,1,0:T(8,128)(2,1)}), bf16[8,256,128]{2,1,0:T(8,128)(2,1)S(1)}, u32[]{:S(2)}, u32[]{:S(2)}) async-start(bf16[8,256,128]{2,1,0:T(8,128)(2,1)} %shard_map.124), calls=%async_computation.2 | async-start | bytes 1048576 | tf_op jit(solution)/shard_map/all_to_all | solution.py:293
  84.4 2.4 %collective-permute-start.3 = (f32[32,256]{1,0:T(8,128)S(1)}, f32[32,256]{1,0:T(8,128)S(1)}, u32[]{:S(2)}, u32[]{:S(2)}) collective-permute-start(f32[32,256]{1,0:T(8,128)S(1)} %shard_map.127.p0), channel_id=1, source_target_pairs={{0,1},{1,2},{2,3},{3,0},{4,5},{5,6},{6,7},{7,4},{8,9},{9,10},{10,1... | collective-permute-start | bytes 98312 | tf_op jit(solution)/shard_map/ppermute | solution.py:314
  86.8 4.3 %collective-permute-start.4 = (f32[32,256]{1,0:T(8,128)S(1)}, f32[32,256]{1,0:T(8,128)S(1)}, u32[]{:S(2)}, u32[]{:S(2)}) collective-permute-start(f32[32,256]{1,0:T(8,128)S(1)} %shard_map.127.p0), channel_id=1, source_target_pairs={{0,2},{1,3},{2,0},{3,1},{4,6},{5,7},{6,4},{7,5},{8,10},{9,11},{10,... | collective-permute-start | bytes 98312 | tf_op jit(solution)/shard_map/ppermute | solution.py:314
  94.1 4.0 %collective-permute-done.5.p3 = f32[32,256]{1,0:T(8,128)S(1)} collective-permute-done((f32[32,256]{1,0:T(8,128)S(1)}, f32[32,256]{1,0:T(8,128)S(1)}, u32[]{:S(2)}, u32[]{:S(2)}) %collective-permute-start.5) | collective-permute-done | bytes 32800 | tf_op jit(solution)/shard_map/ppermute | solution.py:314
  98.1 4.4 %shard_map.128 = (f32[136,128]{1,0:T(8,128)S(1)}, f32[128,128]{1,0:T(8,128)S(1)}) custom-call(f32[2048,128]{1,0:T(8,128)S(1)} %get-tuple-element.10.steps, f32[2048,128]{1,0:T(8,128)S(1)} %get-tuple-element.11.drive, f32[32,256]{1,0:T(8,128)S(1)} %shard_map.127.p0, f32[32,256]{1,0:T(8,128)S(1)} %collective-permute-done.3.p1, ...), custom_call_target="tpu_custom_call" | custom-call | flops 25165824 | bytes 2097152 | tf_op jit(solution)/shard_map/pallas_call | solution.py:223
  102.6 3.8 %collective-permute-start.6 = (f32[136,128]{1,0:T(8,128)S(1)}, f32[136,128]{1,0:T(8,128)S(1)}, u32[]{:S(2)}, u32[]{:S(2)}) collective-permute-start(f32[136,128]{1,0:T(8,128)S(1)} %get-tuple-element.13), channel_id=1, source_target_pairs={{0,8},{4,12},{8,16},{12,20},{16,24},{20,28},{24,32},{28,36},{32,40... | collective-permute-start | bytes 208904 | tf_op jit(solution)/shard_map/ppermute | solution.py:298
  108.6 10.0 %collective-permute-start.8 = (f32[136,128]{1,0:T(8,128)S(1)}, f32[136,128]{1,0:T(8,128)S(1)}, u32[]{:S(2)}, u32[]{:S(2)}) collective-permute-start(f32[136,128]{1,0:T(8,128)S(1)} %shard_map.129.refs_3_), channel_id=1, source_target_pairs={{0,24},{4,28},{8,32},{12,36},{16,40},{20,44},{24,48},{28,52},{32,5... | collective-permute-start | bytes 208904 | tf_op jit(solution)/shard_map/ppermute | solution.py:298
  118.6 2.5 %collective-permute-start.9 = (f32[136,128]{1,0:T(8,128)S(1)}, f32[136,128]{1,0:T(8,128)S(1)}, u32[]{:S(2)}, u32[]{:S(2)}) collective-permute-start(f32[136,128]{1,0:T(8,128)S(1)} %shard_map.129.refs_3_), channel_id=1, source_target_pairs={{0,16},{4,20},{8,24},{12,28},{16,32},{20,36},{24,40},{28,44},{32,4... | collective-permute-start | bytes 208904 | tf_op jit(solution)/shard_map/ppermute | solution.py:298
  121.1 2.5 %collective-permute-start.10 = (f32[136,128]{1,0:T(8,128)S(1)}, f32[136,128]{1,0:T(8,128)S(1)}, u32[]{:S(2)}, u32[]{:S(2)}) collective-permute-start(f32[136,128]{1,0:T(8,128)S(1)} %shard_map.129.refs_3_), channel_id=1, source_target_pairs={{0,8},{4,12},{8,16},{12,20},{16,24},{20,28},{24,32},{28,36},{32,40... | collective-permute-start | bytes 208904 | tf_op jit(solution)/shard_map/ppermute | solution.py:298
  123.6 2.1 %collective-permute-done.9.refs_1_ = f32[136,128]{1,0:T(8,128)S(1)} collective-permute-done((f32[136,128]{1,0:T(8,128)S(1)}, f32[136,128]{1,0:T(8,128)S(1)}, u32[]{:S(2)}, u32[]{:S(2)}) %collective-permute-start.9) | collective-permute-done | bytes 69664 | tf_op jit(solution)/shard_map/ppermute | solution.py:298
  126.9 10.1 %collective-permute-start.11 = (f32[136,128]{1,0:T(8,128)S(1)}, f32[136,128]{1,0:T(8,128)S(1)}, u32[]{:S(2)}, u32[]{:S(2)}) collective-permute-start(f32[136,128]{1,0:T(8,128)S(1)} %shard_map.130.refs_3_), channel_id=1, source_target_pairs={{0,96},{4,100},{8,104},{12,108},{16,112},{20,116},{24,120},{28,124... | collective-permute-start | bytes 208904 | tf_op jit(solution)/shard_map/ppermute | solution.py:298
  137.0 5.5 %collective-permute-start.12 = (f32[136,128]{1,0:T(8,128)S(1)}, f32[136,128]{1,0:T(8,128)S(1)}, u32[]{:S(2)}, u32[]{:S(2)}) collective-permute-start(f32[136,128]{1,0:T(8,128)S(1)} %shard_map.130.refs_3_), channel_id=1, source_target_pairs={{0,64},{4,68},{8,72},{12,76},{16,80},{20,84},{24,88},{28,92},{32,9... | collective-permute-start | bytes 208904 | tf_op jit(solution)/shard_map/ppermute | solution.py:298
  142.5 6.4 %collective-permute-start.13 = (f32[136,128]{1,0:T(8,128)S(1)}, f32[136,128]{1,0:T(8,128)S(1)}, u32[]{:S(2)}, u32[]{:S(2)}) collective-permute-start(f32[136,128]{1,0:T(8,128)S(1)} %shard_map.130.refs_3_), channel_id=1, source_target_pairs={{0,32},{4,36},{8,40},{12,44},{16,48},{20,52},{24,56},{28,60},{32,6... | collective-permute-start | bytes 208904 | tf_op jit(solution)/shard_map/ppermute | solution.py:298
  150.9 4.6 %collective-permute-start.14 = (f32[136,128]{1,0:T(8,128)S(1)}, f32[136,128]{1,0:T(8,128)S(1)}, u32[]{:S(2)}, u32[]{:S(2)}) collective-permute-start(f32[136,128]{1,0:T(8,128)S(1)} %shard_map.131.e3), channel_id=1, source_target_pairs={{0,384},{4,388},{8,392},{12,396},{16,400},{20,404},{24,408},{28,41... | collective-permute-start | bytes 208904 | tf_op jit(solution)/shard_map/ppermute | solution.py:298
  155.5 4.7 %collective-permute-start.15 = (f32[136,128]{1,0:T(8,128)S(1)}, f32[136,128]{1,0:T(8,128)S(1)}, u32[]{:S(2)}, u32[]{:S(2)}) collective-permute-start(f32[136,128]{1,0:T(8,128)S(1)} %shard_map.131.e3), channel_id=1, source_target_pairs={{0,256},{4,260},{8,264},{12,268},{16,272},{20,276},{24,280},{28,28... | collective-permute-start | bytes 208904 | tf_op jit(solution)/shard_map/ppermute | solution.py:298
  163.5 9.3 %shard_map.132 = bf16[256,1024]{1,0:T(8,128)(2,1)} custom-call(f32[2048,128]{1,0:T(8,128)S(1)} %get-tuple-element.10.steps, f32[2048,128]{1,0:T(8,128)S(1)} %get-tuple-element.11.drive, f32[32,256]{1,0:T(8,128)S(1)} %shard_map.127.p0, f32[32,256]{1,0:T(8,128)S(1)} %collective-permute-done.3.p1, f32[32,256]{1,0:T(8,128)S(1)} %collective-permute-done.4.p2, ...), custom_call_target="tpu_custom_call" | custom-call | flops 37748736 | bytes 3670016 | tf_op jit(solution)/shard_map/pallas_call | solution.py:287
  (51 shorter events, 19.8 us)
Async XLA Ops:
  3.9 36.0 %all-to-all-start = ((bf16[8,512,128]{2,1,0:T(8,128)(2,1)}), bf16[8,512,128]{2,1,0:T(8,128)(2,1)S(1)}, u32[]{:S(2)}, u32[]{:S(2)}) async-start(bf16[8,512,128]{2,1,0:T(8,128)(2,1)} %shard_map.122), calls=%async_computation | async-start | bytes 2097152 | tf_op jit(solution)/shard_map/all_to_all | solution.py:293
  40.7 15.9 %collective-permute-start.1 = (bf16[4,512,128]{2,1,0:T(8,128)(2,1)}, bf16[4,512,128]{2,1,0:T(8,128)(2,1)S(1)}, u32[]{:S(2)}, u32[]{:S(2)}) collective-permute-start(bf16[4,512,128]{2,1,0:T(8,128)(2,1)} %slice.3), channel_id=1, source_target_pairs={{0,64},{4,68},{8,72},{12,76},{16,80},{20,84},{24,88},{28,92},{32,9... | collective-permute-start | bytes 1572872 | tf_op jit(solution)/shard_map/ppermute | solution.py:323
  45.0 23.8 %collective-permute-start = (bf16[8,512,128]{2,1,0:T(8,128)(2,1)S(1)}, bf16[8,512,128]{2,1,0:T(8,128)(2,1)S(1)}, u32[]{:S(2)}, u32[]{:S(2)}) collective-permute-start(bf16[8,512,128]{2,1,0:T(8,128)(2,1)S(1)} %all-to-all-done.own), channel_id=1, source_target_pairs={{0,4},{4,0},{8,12},{12,8},{16,20},{20,16},{24,28},{28,24},{32,36},... | collective-permute-start | bytes 3145736 | tf_op jit(solution)/shard_map/ppermute | solution.py:322
  46.9 21.9 %all-to-all-start.1 = ((bf16[8,256,128]{2,1,0:T(8,128)(2,1)}), bf16[8,256,128]{2,1,0:T(8,128)(2,1)S(1)}, u32[]{:S(2)}, u32[]{:S(2)}) async-start(bf16[8,256,128]{2,1,0:T(8,128)(2,1)} %shard_map.123), calls=%async_computation.1 | async-start | bytes 1048576 | tf_op jit(solution)/shard_map/all_to_all | solution.py:293
  56.6 12.2 %collective-permute-start.2 = (bf16[4,512,128]{2,1,0:T(8,128)(2,1)S(1)}, bf16[4,512,128]{2,1,0:T(8,128)(2,1)}, u32[]{:S(2)}, u32[]{:S(2)}) collective-permute-start(bf16[4,512,128]{2,1,0:T(8,128)(2,1)S(1)} %collective-permute-done.1.old), channel_id=1, source_target_pairs={{0,4},{4,0},{8,12},{12,8},{16,20},{20,16},{24,28},{28,24},{32,36},... | collective-permute-start | bytes 1572872 | tf_op jit(solution)/shard_map/ppermute | solution.py:324
  80.2 92.6 %all-to-all-start.2 = ((bf16[8,256,128]{2,1,0:T(8,128)(2,1)}), bf16[8,256,128]{2,1,0:T(8,128)(2,1)S(1)}, u32[]{:S(2)}, u32[]{:S(2)}) async-start(bf16[8,256,128]{2,1,0:T(8,128)(2,1)} %shard_map.124), calls=%async_computation.2 | async-start | bytes 1048576 | tf_op jit(solution)/shard_map/all_to_all | solution.py:293
  83.8 9.2 %copy-start.2 = (bf16[256,1024]{1,0:T(8,128)(2,1)S(1)}, bf16[256,1024]{1,0:T(8,128)(2,1)}, u32[]{:S(2)}) copy-start(bf16[256,1024]{1,0:T(8,128)(2,1)} %proj.1) | copy-start | bytes 1572868
  84.0 9.0 %copy-start.5 = (bf16[256,256]{1,0:T(8,128)(2,1)S(1)}, bf16[256,256]{1,0:T(8,128)(2,1)}, u32[]{:S(2)}) copy-start(bf16[256,256]{1,0:T(8,128)(2,1)} %low.1) | copy-start | bytes 393220
  84.4 9.7 %collective-permute-start.3 = (f32[32,256]{1,0:T(8,128)S(1)}, f32[32,256]{1,0:T(8,128)S(1)}, u32[]{:S(2)}, u32[]{:S(2)}) collective-permute-start(f32[32,256]{1,0:T(8,128)S(1)} %shard_map.127.p0), channel_id=1, source_target_pairs={{0,1},{1,2},{2,3},{3,0},{4,5},{5,6},{6,7},{7,4},{8,9},{9,10},{10,1... | collective-permute-start | bytes 98312 | tf_op jit(solution)/shard_map/ppermute | solution.py:314
  86.8 7.3 %collective-permute-start.4 = (f32[32,256]{1,0:T(8,128)S(1)}, f32[32,256]{1,0:T(8,128)S(1)}, u32[]{:S(2)}, u32[]{:S(2)}) collective-permute-start(f32[32,256]{1,0:T(8,128)S(1)} %shard_map.127.p0), channel_id=1, source_target_pairs={{0,2},{1,3},{2,0},{3,1},{4,6},{5,7},{6,4},{7,5},{8,10},{9,11},{10,... | collective-permute-start | bytes 98312 | tf_op jit(solution)/shard_map/ppermute | solution.py:314
  91.1 7.0 %collective-permute-start.5 = (f32[32,256]{1,0:T(8,128)S(1)}, f32[32,256]{1,0:T(8,128)S(1)}, u32[]{:S(2)}, u32[]{:S(2)}) collective-permute-start(f32[32,256]{1,0:T(8,128)S(1)} %shard_map.127.p0), channel_id=1, source_target_pairs={{0,3},{1,0},{2,1},{3,2},{4,7},{5,4},{6,5},{7,6},{8,11},{9,8},{10,9... | collective-permute-start | bytes 98312 | tf_op jit(solution)/shard_map/ppermute | solution.py:314
  102.6 5.7 %collective-permute-start.6 = (f32[136,128]{1,0:T(8,128)S(1)}, f32[136,128]{1,0:T(8,128)S(1)}, u32[]{:S(2)}, u32[]{:S(2)}) collective-permute-start(f32[136,128]{1,0:T(8,128)S(1)} %get-tuple-element.13), channel_id=1, source_target_pairs={{0,8},{4,12},{8,16},{12,20},{16,24},{20,28},{24,32},{28,36},{32,40... | collective-permute-start | bytes 208904 | tf_op jit(solution)/shard_map/ppermute | solution.py:298
  106.4 2.2 %collective-permute-start.7 = (f32[136,128]{1,0:T(8,128)S(1)}, f32[136,128]{1,0:T(8,128)S(1)}, u32[]{:S(2)}, u32[]{:S(2)}) collective-permute-start(f32[136,128]{1,0:T(8,128)S(1)} %get-tuple-element.13), channel_id=1, source_target_pairs={{0,4},{4,8},{8,12},{12,16},{16,20},{20,24},{24,28},{28,32},{32,36}... | collective-permute-start | bytes 208904 | tf_op jit(solution)/shard_map/ppermute | solution.py:298
  108.6 54.9 %copy-start.7 = (bf16[256,1024]{1,0:T(8,128)(2,1)S(1)}, bf16[256,1024]{1,0:T(8,128)(2,1)}, u32[]{:S(2)}) copy-start(bf16[256,1024]{1,0:T(8,128)(2,1)} %gate.1) | copy-start | bytes 1572868
  108.6 15.0 %collective-permute-start.8 = (f32[136,128]{1,0:T(8,128)S(1)}, f32[136,128]{1,0:T(8,128)S(1)}, u32[]{:S(2)}, u32[]{:S(2)}) collective-permute-start(f32[136,128]{1,0:T(8,128)S(1)} %shard_map.129.refs_3_), channel_id=1, source_target_pairs={{0,24},{4,28},{8,32},{12,36},{16,40},{20,44},{24,48},{28,52},{32,5... | collective-permute-start | bytes 208904 | tf_op jit(solution)/shard_map/ppermute | solution.py:298
  118.6 7.1 %collective-permute-start.9 = (f32[136,128]{1,0:T(8,128)S(1)}, f32[136,128]{1,0:T(8,128)S(1)}, u32[]{:S(2)}, u32[]{:S(2)}) collective-permute-start(f32[136,128]{1,0:T(8,128)S(1)} %shard_map.129.refs_3_), channel_id=1, source_target_pairs={{0,16},{4,20},{8,24},{12,28},{16,32},{20,36},{24,40},{28,44},{32,4... | collective-permute-start | bytes 208904 | tf_op jit(solution)/shard_map/ppermute | solution.py:298
  121.1 5.8 %collective-permute-start.10 = (f32[136,128]{1,0:T(8,128)S(1)}, f32[136,128]{1,0:T(8,128)S(1)}, u32[]{:S(2)}, u32[]{:S(2)}) collective-permute-start(f32[136,128]{1,0:T(8,128)S(1)} %shard_map.129.refs_3_), channel_id=1, source_target_pairs={{0,8},{4,12},{8,16},{12,20},{16,24},{20,28},{24,32},{28,36},{32,40... | collective-permute-start | bytes 208904 | tf_op jit(solution)/shard_map/ppermute | solution.py:298
  126.9 36.6 %copy-start.9 = (f32[1024]{0:T(1024)S(1)}, f32[1024]{0:T(1024)}, u32[]{:S(2)}) copy-start(f32[1024]{0:T(1024)} %param.21) | copy-start | bytes 12292
  126.9 22.1 %collective-permute-start.11 = (f32[136,128]{1,0:T(8,128)S(1)}, f32[136,128]{1,0:T(8,128)S(1)}, u32[]{:S(2)}, u32[]{:S(2)}) collective-permute-start(f32[136,128]{1,0:T(8,128)S(1)} %shard_map.130.refs_3_), channel_id=1, source_target_pairs={{0,96},{4,100},{8,104},{12,108},{16,112},{20,116},{24,120},{28,124... | collective-permute-start | bytes 208904 | tf_op jit(solution)/shard_map/ppermute | solution.py:298
  137.0 11.9 %collective-permute-start.12 = (f32[136,128]{1,0:T(8,128)S(1)}, f32[136,128]{1,0:T(8,128)S(1)}, u32[]{:S(2)}, u32[]{:S(2)}) collective-permute-start(f32[136,128]{1,0:T(8,128)S(1)} %shard_map.130.refs_3_), channel_id=1, source_target_pairs={{0,64},{4,68},{8,72},{12,76},{16,80},{20,84},{24,88},{28,92},{32,9... | collective-permute-start | bytes 208904 | tf_op jit(solution)/shard_map/ppermute | solution.py:298
  142.5 8.3 %collective-permute-start.13 = (f32[136,128]{1,0:T(8,128)S(1)}, f32[136,128]{1,0:T(8,128)S(1)}, u32[]{:S(2)}, u32[]{:S(2)}) collective-permute-start(f32[136,128]{1,0:T(8,128)S(1)} %shard_map.130.refs_3_), channel_id=1, source_target_pairs={{0,32},{4,36},{8,40},{12,44},{16,48},{20,52},{24,56},{28,60},{32,6... | collective-permute-start | bytes 208904 | tf_op jit(solution)/shard_map/ppermute | solution.py:298
  150.9 10.6 %collective-permute-start.14 = (f32[136,128]{1,0:T(8,128)S(1)}, f32[136,128]{1,0:T(8,128)S(1)}, u32[]{:S(2)}, u32[]{:S(2)}) collective-permute-start(f32[136,128]{1,0:T(8,128)S(1)} %shard_map.131.e3), channel_id=1, source_target_pairs={{0,384},{4,388},{8,392},{12,396},{16,400},{20,404},{24,408},{28,41... | collective-permute-start | bytes 208904 | tf_op jit(solution)/shard_map/ppermute | solution.py:298
  155.5 6.6 %collective-permute-start.15 = (f32[136,128]{1,0:T(8,128)S(1)}, f32[136,128]{1,0:T(8,128)S(1)}, u32[]{:S(2)}, u32[]{:S(2)}) collective-permute-start(f32[136,128]{1,0:T(8,128)S(1)} %shard_map.131.e3), channel_id=1, source_target_pairs={{0,256},{4,260},{8,264},{12,268},{16,272},{20,276},{24,280},{28,28... | collective-permute-start | bytes 208904 | tf_op jit(solution)/shard_map/ppermute | solution.py:298
  160.2 3.2 %collective-permute-start.16 = (f32[136,128]{1,0:T(8,128)S(1)}, f32[136,128]{1,0:T(8,128)S(1)}, u32[]{:S(2)}, u32[]{:S(2)}) collective-permute-start(f32[136,128]{1,0:T(8,128)S(1)} %shard_map.131.e3), channel_id=1, source_target_pairs={{0,128},{4,132},{8,136},{12,140},{16,144},{20,148},{24,152},{28,15... | collective-permute-start | bytes 208904 | tf_op jit(solution)/shard_map/ppermute | solution.py:298
  (7 other events, 30.9 us)

commit v2 on v1

v2 whole, which is shorter than its diff:
```python
import jax
import jax.numpy as jnp
from jax import lax
from jax.experimental import pallas as pl
from jax.experimental.pallas import tpu as pltpu
from jax.sharding import PartitionSpec as P


HD = 128
WINDOW = 2048
NS = 16
LANES = 128
TILES = 8
LOG2E = 1.4426950408889634
F32 = jnp.float32
BF16 = jnp.bfloat16
VMEM = pl.BlockSpec(memory_space=pltpu.VMEM)
SMEM = pl.BlockSpec(memory_space=pltpu.SMEM)


def cost(flops, moved, exps=0):
    return pl.CostEstimate(flops=flops, bytes_accessed=moved, transcendentals=exps)


def local(body, outs, scratch=(), scalars=0, arrays=1, estimate=None, limit=48 << 20):
    return pl.pallas_call(
        body,
        out_shape=outs,
        in_specs=[SMEM] * scalars + [VMEM] * arrays,
        out_specs=jax.tree.map(lambda _: VMEM, outs),
        scratch_shapes=list(scratch),
        cost_estimate=estimate,
        compiler_params=pltpu.CompilerParams(vmem_limit_bytes=limit),
    )


def parity_of(place):
    return place[0] & 1


def plane_of(place):
    return place[0] >> 4


def pack_body(*refs):
    *ins, out, sems = refs
    rows = ins[0].shape[0]
    copies = []
    for head in range(out.shape[0]):
        for k, part in enumerate(ins):
            source = part.at[:, pl.ds(head * HD, HD)]
            target = out.at[head, pl.ds(k * rows, rows), :]
            copies.append(pltpu.make_async_copy(source, target, sems.at[head, k]))
    for copy in copies:
        copy.start()
    for copy in copies:
        copy.wait()


def pack(*parts):
    rows, width = parts[0].shape
    heads = width // HD
    return pl.pallas_call(
        pack_body,
        out_shape=jax.ShapeDtypeStruct((heads, len(parts) * rows, HD), BF16),
        in_specs=[pl.BlockSpec(memory_space=pl.ANY)] * len(parts),
        out_specs=VMEM,
        scratch_shapes=[pltpu.SemaphoreType.DMA((heads, len(parts)))],
        name="pack",
        cost_estimate=cost(0, 4 * len(parts) * rows * width),
    )(*parts)


def unpack_body(blocks, out):
    for head in range(blocks.shape[0]):
        out[:, head * HD : (head + 1) * HD] = blocks[head]


def unpack(blocks):
    heads, rows, _ = blocks.shape
    out = jax.ShapeDtypeStruct((rows, heads * HD), BF16)
    return local(unpack_body, out, estimate=cost(0, 4 * rows * heads * HD))(blocks)


def weigh(q, edge_pair, full, out, i):
    rows = q.shape[0]
    scale = HD**-0.5 * LOG2E
    columns = lax.broadcasted_iota(jnp.int32, (rows, rows), 1)
    below = columns <= lax.broadcasted_iota(jnp.int32, (rows, rows), 0)

    def dots(keys):
        return lax.dot_general(q, keys, (((1,), (1,)), ((), ())), preferred_element_type=F32)

    def gather(weights, values, ones):
        side = jnp.concatenate([values, ones], axis=1)
        return jnp.dot(weights, side, preferred_element_type=F32)

    (k_near, v_near, one_near), (k_far, v_far, one_far) = edge_pair
    scores = [jnp.where(below, dots(k_near), dots(k_far))] + [dots(k) for k, _, _ in full]
    top = None
    for part in scores:
        for c in range(0, rows, LANES):
            piece = part[:, c : c + LANES]
            top = piece if top is None else jnp.maximum(top, piece)
    top = jnp.max(top, axis=1, keepdims=True) * scale
    weights = [jnp.exp2(part * scale - top) for part in scores]
    total = gather(jnp.where(below, weights[0], 0.0).astype(BF16), v_near, one_near)
    total += gather(jnp.where(below, 0.0, weights[0]).astype(BF16), v_far, one_far)
    for part, (_, values, ones) in zip(weights[1:], full):
        total += gather(part.astype(BF16), values, ones)
    out[i] = (total[:, 0:HD] / total[:, HD : 2 * HD]).astype(BF16)


def late_body(place, queries, own, other, out):
    half = out.shape[0]
    rows = queries.shape[1]
    parity = parity_of(place)
    ones = jnp.ones((rows, HD), BF16)

    def block(source, b):
        return source[b, 0:rows, :], source[b, rows : 2 * rows, :], ones

    for i in range(half):
        full = [block(own, i + 1 + j) for j in range(half - 1)]
        full += [block(other, i + parity + j) for j in range(half)]
        weigh(queries[half + i], (block(own, half + i), block(own, i)), full, out, i)


def early_body(place, queries, own, other, old, past, later, out, ko, kp):
    half = later.shape[0]
    rows = queries.shape[1]
    even = parity_of(place) == 0
    live = plane_of(place) > 0
    out[half:] = later[...]
    key0 = jnp.where(even, own[0, 0:1, :].astype(F32), other[0, 0:1, :].astype(F32))
    key0 = jnp.broadcast_to(key0, (rows, HD)).astype(BF16)
    ones = jnp.ones((rows, HD), BF16)
    shown = jnp.where(live, jnp.ones((rows, HD), F32), jnp.zeros((rows, HD), F32)).astype(BF16)
    for keys, source in ((ko, old), (kp, past)):

        @pl.when(live)
        def _():
            for b in range(half):
                keys[b] = source[b, 0:rows, :]

        @pl.when(jnp.logical_not(live))
        def _():
            for b in range(half):
                keys[b] = key0

    def new(source, b):
        return source[b, 0:rows, :], source[b, rows : 2 * rows, :], ones

    def before(keys, source, b):
        return keys[b], source[b, rows : 2 * rows, :], shown

    def mine(b):
        return before(ko, old, b) if b < half else new(own, b - half)

    def either(first, second):
        return tuple(
            jnp.where(even, a.astype(F32), b.astype(F32)).astype(BF16) for a, b in zip(first, second)
        )

    def theirs(b):
        if b + 1 < half:
            at = b + parity_of(place)
            return kp[at], past[at, rows : 2 * rows, :], shown
        if b >= half:
            at = b - half + parity_of(place)
            return other[at, 0:rows, :], other[at, rows : 2 * rows, :], ones
        return either(before(kp, past, b), new(other, 0))

    for i in range(half):
        full = [mine(i + 1 + j) for j in range(half - 1)] + [theirs(i + j) for j in range(half)]
        weigh(queries[i], (mine(half + i), mine(i)), full, out, i)


def attend_late(place, queries, own, other):
    blocks, rows, _ = queries.shape
    half = blocks // 2
    out = jax.ShapeDtypeStruct((half, rows, HD), BF16)
    estimate = cost(4 * half * rows * WINDOW * 2 * HD, 4 << 20, half * rows * WINDOW)
    return local(late_body, out, (), 1, 3, estimate)(place, queries, own, other)


def attend_early(place, queries, own, other, old, past, later):
    blocks, rows, _ = queries.shape
    half = blocks // 2
    scratch = [pltpu.VMEM((half, rows, HD), BF16)] * 2
    out = jax.ShapeDtypeStruct(queries.shape, BF16)
    estimate = cost(4 * half * rows * WINDOW * 2 * HD, 4 << 20, half * rows * WINDOW)
    return local(early_body, out, scratch, 1, 6, estimate)(
        place, queries, own, other, old, past, later
    )


def rows_of(step):
    return pl.ds(pl.multiple_of(step * TILES, TILES), TILES)


def project_body(xin, w_bc, out):
    out[...] = jnp.dot(xin[...], w_bc[...], preferred_element_type=F32).T


def project(xin, w_bc):
    out = jax.ShapeDtypeStruct((w_bc.shape[1], xin.shape[0]), F32)
    return local(project_body, out, arrays=2, estimate=cost(0, 2 * xin.size))(xin, w_bc)


def load_steps(low, proj, bias, xin, steps, drive):
    rows = low.shape[0]
    for c in range(TILES):
        col = slice(c * LANES, (c + 1) * LANES)
        raw = jnp.dot(low[...], proj[:, col], preferred_element_type=F32) + bias[:, col]
        size = jnp.maximum(raw, 0.0) + jnp.log1p(jnp.exp(-jnp.abs(raw)))
        steps[pl.ds(c, rows, stride=TILES), :] = size
        drive[pl.ds(c, rows, stride=TILES), :] = size * xin[:, col].astype(F32)


def spread(parts, count, wide):
    total = parts[0][0:count, :]
    for part in parts[1:]:
        total = total + part[0:count, :]
    total = total.T
    rows = total.shape[0]
    for n in range(count):
        column = jnp.broadcast_to(total[:, n : n + 1], (rows, LANES))
        wide[pl.ds(n, rows, stride=count), :] = column


def load_rates(a_rate, held):
    for c in range(TILES):
        held[pl.ds(c, NS, stride=TILES), :] = a_rate[:, c * LANES : (c + 1) * LANES] * -LOG2E
    return [held[n * TILES : (n + 1) * TILES, :] for n in range(NS)]


def ends_body(low, proj, bias, xin, p0, p1, p2, p3, a_rate, out, held, wide, steps, drive):
    rows = p0.shape[1]
    load_steps(low, proj, bias, xin, steps, drive)
    spread((p0, p1, p2, p3), NS, wide)
    rates = load_rates(a_rate, held)

    def step(t, carry):
        state, through = carry
        size, push = steps[rows_of(t), :], drive[rows_of(t), :]
        state = tuple(
            jnp.exp2(size * rates[n]) * state[n] + push * wide[pl.ds(t * NS + n, 1), :]
            for n in range(NS)
        )
        return state, through + size

    zero = jnp.zeros((TILES, LANES), F32)
    state, through = lax.fori_loop(0, rows, step, ((zero,) * NS, zero), unroll=4)
    for n in range(NS):
        out[n * TILES : (n + 1) * TILES, :] = state[n]
    out[NS * TILES :, :] = through


def block_ends(sources, partials, a_rate):
    rows, width = sources[3].shape
    out = jax.ShapeDtypeStruct(((NS + 1) * TILES, LANES), F32)
    rates = jax.ShapeDtypeStruct((NS * TILES, LANES), F32)
    scratch = [pltpu.VMEM((rows * NS, LANES), F32)] + [pltpu.VMEM((rows * TILES, LANES), F32)] * 2
    estimate = cost(6 * rows * width * NS, 4 * rows * width, rows * width * NS)
    return local(ends_body, (out, rates), scratch, 0, 9, estimate)(*sources, *partials, a_rate)


def fold(rates, parts):
    state = [parts[0][n * TILES : (n + 1) * TILES, :] for n in range(NS)]
    through = parts[0][NS * TILES :, :]
    for part in parts[1:]:
        size = part[NS * TILES :, :]
        for n in range(NS):
            row = slice(n * TILES, (n + 1) * TILES)
            state[n] = jnp.exp2(size * rates[row, :]) * state[n] + part[row, :]
        through = through + size
    return state, through


def join_body(rates, *refs):
    *parts, out = refs
    state, through = fold(rates, parts)
    for n in range(NS):
        out[n * TILES : (n + 1) * TILES, :] = state[n]
    out[NS * TILES :, :] = through


def join(rates, parts):
    out = jax.ShapeDtypeStruct(parts[0].shape, F32)
    estimate = cost(1 << 16, 1 << 18)
    return local(join_body, out, arrays=1 + len(parts), estimate=estimate)(rates, *parts)


def final_body(
    low, proj, bias, xin, p0, p1, p2, p3, held, e0, e1, gate, skip, out, wide, mix, steps, drive
):
    rows = p0.shape[1]
    load_steps(low, proj, bias, xin, steps, drive)
    spread((p0, p1, p2, p3), 2 * NS, wide)
    rates = [held[n * TILES : (n + 1) * TILES, :] for n in range(NS)]
    state, _ = fold(held, (e0, e1))

    def step(t, state):
        size, push = steps[rows_of(t), :], drive[rows_of(t), :]
        after = []
        result = None
        for n in range(NS):
            at = t * 2 * NS + n
            now = jnp.exp2(size * rates[n]) * state[n] + push * wide[pl.ds(at, 1), :]
            after.append(now)
            term = now * wide[pl.ds(at + NS, 1), :]
            result = term if result is None else result + term
        mix[rows_of(t), :] = result
        return tuple(after)

    lax.fori_loop(0, rows, step, tuple(state), unroll=4)
    for c in range(TILES):
        col = slice(c * LANES, (c + 1) * LANES)
        mixed = mix[pl.ds(c, rows, stride=TILES), :] + skip[:, col] * xin[:, col].astype(F32)
        opened = gate[:, col].astype(F32)
        out[:, col] = (mixed * (opened / (1.0 + jnp.exp(-opened)))).astype(BF16)


def finish(sources, partials, rates, entering, gate, skip):
    rows, width = gate.shape
    out = jax.ShapeDtypeStruct(gate.shape, BF16)
    tall = pltpu.VMEM((rows * TILES, LANES), F32)
    scratch = [pltpu.VMEM((rows * 2 * NS, LANES), F32), tall, tall, tall]
    estimate = cost(9 * rows * width * NS, 8 * rows * width, rows * width * NS)
    return local(final_body, out, scratch, 0, 13, estimate)(
        *sources, *partials, rates, *entering, gate, skip.reshape(1, -1)
    )


def exchange(x, groups):
    return lax.all_to_all(x, "ctx", 0, 0, axis_index_groups=groups, tiled=True)


def after(part, distance):
    count = lax.axis_size("ctx")
    return lax.ppermute(part, "ctx", [(i, i + distance) for i in range(count - distance)])


def shards(query, key, value, xin, gate_z, w_bc, dt_low, dt_proj, dt_bias, a_rate, skip):
    ctx, tp = lax.axis_size("ctx"), lax.axis_size("tp")
    side, planes = 8, ctx // 16
    line = 2 * side
    index = lax.axis_index("ctx")
    place = index.astype(jnp.int32).reshape(1)
    along_y = [[z * line + 2 * y + c for y in range(side)] for z in range(planes) for c in (0, 1)]
    partner = [(i, i ^ 1) for i in range(ctx)]
    next_row = [(i, i + line) for i in range(ctx - line)]

    own_kv = exchange(pack(key, value), along_y)
    partial = project(xin, w_bc)
    partials = [partial] + [
        lax.ppermute(partial, "tp", [(i, (i + d) % tp) for i in range(tp)])
        for d in range(1, tp)
    ]
    sources = (dt_low, dt_proj, dt_bias.reshape(1, -1), xin)
    ends, rates = block_ends(sources, partials, a_rate)
    queries = pack(query)
    own_kv, queries = lax.optimization_barrier((own_kv, queries))
    queries = exchange(queries, along_y)
    old_kv = lax.ppermute(own_kv[side // 2 :], "ctx", next_row)
    other_kv = lax.ppermute(own_kv, "ctx", partner)
    past_kv = lax.ppermute(old_kv, "ctx", partner)
    ends = join(rates, [after(ends, 2), after(ends, 1)])
    ends = join(rates, [after(ends, 6), after(ends, 4), after(ends, 2), ends])
    ends = join(rates, [after(ends, 8), ends])
    ends = join(rates, [after(ends, 48), after(ends, 32), after(ends, 16), ends])
    entering = [after(ends, 64), ends]
    later = attend_late(place, queries, own_kv, other_kv)
    attended = attend_early(place, queries, own_kv, other_kv, old_kv, past_kv, later)
    attended = exchange(attended, along_y)
    attended = unpack(attended)
    mixed = finish(sources, partials, rates, entering, gate_z, skip)
    return (attended, mixed)


def solution(mesh):
    in_specs = (
        P("ctx", "tp"),
        P("ctx", "tp"),
        P("ctx", "tp"),
        P("ctx", "tp"),
        P("ctx", "tp"),
        P("tp", None),
        P("ctx", None),
        P(None, "tp"),
        P("tp"),
        P(None, "tp"),
        P("tp"),
    )
    out_specs = (P("ctx", "tp"), P("ctx", "tp"))
    return jax.shard_map(shards, mesh=mesh, in_specs=in_specs, out_specs=out_specs, check_vma=False)
```

time: 175 us -> 177 us (1.011)
  starting transfers between devices: 83.8 us -> 90.4 us
  local copies, waits for them, and re-layouts: 3.12 us -> 0.25 us
  waiting for transfers between devices: 56.3 us -> 54.4 us
    all_to_all x3, waiting for transfers between devices: 38.1 us -> 27.1 us  [exchange(): return lax.all_to_all(x, 'ctx', 0, 0, axis_index_groups=groups, tiled=True)]
    ppermute x1, waiting for transfers between devices: 6.19 us -> 11.8 us  [shards(): old_kv = lax.ppermute(own_kv[side // 2:], 'ctx', next_row)]
    ppermute x11 -> x10, starting transfers between devices: 52.7 us -> 56.3 us  [after(): lax.ppermute(part, 'ctx', [(i, i + distance) for i in range(count - dista...]
    all_to_all x3, starting transfers between devices: 14.4 us -> 17.3 us  [exchange(): return lax.all_to_all(x, 'ctx', 0, 0, axis_index_groups=groups, tiled=True)]
    ppermute x11 -> x10, waiting for transfers between devices: 7.95 us -> 10.4 us  [after(): lax.ppermute(part, 'ctx', [(i, i + distance) for i in range(count - dista...]
    unnamed x23 -> x17, local copies, waits for them, and re-layouts: 2.29 us -> 0.21 us
  transfers between devices with their start and end apart: 20 -> 19, of which waited for: 11 -> 12; matrix products, arithmetic and copies ran while one was open for 0% -> 0% of each run, Pallas kernels for 9% -> 12%
where the time goes in v2:
time: 177 us; the launch traced here: 176 us
  starting transfers between devices  90.4 us (51%)
  waiting for transfers between devices  54.4 us (31%)
  Pallas kernels  30 us (17%)
    ppermute x10, starting transfers between devices, after(): lax.ppermute(part, 'ctx', [(i, i + distance) for i in range(count - dista...  56.3 us
    all_to_all x3, waiting for transfers between devices, exchange(): return lax.all_to_all(x, 'ctx', 0, 0, axis_index_groups=groups, tiled=True)  27.1 us
    all_to_all x3, starting transfers between devices, exchange(): return lax.all_to_all(x, 'ctx', 0, 0, axis_index_groups=groups, tiled=True)  17.3 us
    ppermute x1, waiting for transfers between devices, shards(): old_kv = lax.ppermute(own_kv[side // 2:], 'ctx', next_row)  11.8 us
    ppermute x10, waiting for transfers between devices, after(): lax.ppermute(part, 'ctx', [(i, i + distance) for i in range(count - dista...  10.4 us
    pallas_call x1, Pallas kernels, finish(): local(final_body, out, scratch, 0, 13, estimate)  10.1 us
    ppermute x3, starting transfers between devices, shards(): lax.ppermute(partial, 'tp', [(i, (i + d) % tp) for i in range(tp)])  8.62 us
    pallas_call x1, Pallas kernels, attend_early(): local(early_body, out, scratch, 1, 6, estimate)  5.52 us
  transfers between devices with their start and end apart: 19, of which 12 were waited for; matrix products, arithmetic and copies ran while one was open for 0% of the time, Pallas kernels for 12%

profile of v2, /device:TPU:6, one launch (start us, length us, event | category | flops | bytes accessed | tf_op | source)
XLA Modules:
  0.0 176.0 jit_solution(14049473496171639226)
XLA Ops:
  0.6 2.4 %pack.2 = bf16[8,512,128]{2,1,0:T(8,128)(2,1)} custom-call(bf16[256,1024]{1,0:T(8,128)(2,1)} %refs_0_.2, bf16[256,1024]{1,0:T(8,128)(2,1)} %refs_1_.1), custom_call_target="tpu_custom_call" | custom-call | bytes 2097152 | tf_op jit(solution)/shard_map/pack/pallas_call | solution.py:63
  3.0 7.1 %all-to-all-start = ((bf16[8,512,128]{2,1,0:T(8,128)(2,1)}), bf16[8,512,128]{2,1,0:T(8,128)(2,1)S(1)}, u32[]{:S(2)}, u32[]{:S(2)}) async-start(bf16[8,512,128]{2,1,0:T(8,128)(2,1)} %pack.2), calls=%async_computation | async-start | bytes 2097152 | tf_op jit(solution)/shard_map/all_to_all | solution.py:337
  12.1 26.8 %all-to-all-done.own = bf16[8,512,128]{2,1,0:T(8,128)(2,1)S(1)} async-done(((bf16[8,512,128]{2,1,0:T(8,128)(2,1)}), bf16[8,512,128]{2,1,0:T(8,128)(2,1)S(1)}, u32[]{:S(2)}, u32[]{:S(2)}) %all-to-all-start) | async-done | bytes 1048608 | tf_op jit(solution)/shard_map/all_to_all | solution.py:337
  40.8 3.5 %all-to-all-start.1 = ((bf16[8,256,128]{2,1,0:T(8,128)(2,1)}), bf16[8,256,128]{2,1,0:T(8,128)(2,1)S(1)}, u32[]{:S(2)}, u32[]{:S(2)}) async-start(bf16[8,256,128]{2,1,0:T(8,128)(2,1)} %pack.3), calls=%async_computation.1 | async-start | bytes 1048576 | tf_op jit(solution)/shard_map/all_to_all | solution.py:337
  44.4 4.3 %collective-permute-start.1 = (bf16[4,512,128]{2,1,0:T(8,128)(2,1)S(1)}, bf16[4,512,128]{2,1,0:T(8,128)(2,1)S(1)}, u32[]{:S(2)}, u32[]{:S(2)}) collective-permute-start(bf16[4,512,128]{2,1,0:T(8,128)(2,1)S(1)} %slice.3), channel_id=1, source_target_pairs={{0,64},{4,68},{8,72},{12,76},{16,80},{20,84},{24,88},{28,92},{32,9... | collective-permute-start | bytes 1572872 | tf_op jit(solution)/shard_map/ppermute | solution.py:366
  48.7 11.8 %collective-permute-done.1.old = bf16[4,512,128]{2,1,0:T(8,128)(2,1)S(1)} collective-permute-done((bf16[4,512,128]{2,1,0:T(8,128)(2,1)S(1)}, bf16[4,512,128]{2,1,0:T(8,128)(2,1)S(1)}, u32[]{:S(2)}, u32[]{:S(2)}) %collective-permute-start.1) | collective-permute-done | bytes 524320 | tf_op jit(solution)/shard_map/ppermute | solution.py:366
  62.7 3.6 %shard_map.122.later = bf16[4,256,128]{2,1,0:T(8,128)(2,1)S(1)} custom-call(s32[1]{0:T(128)} %bitcast.place, bf16[8,256,128]{2,1,0:T(8,128)(2,1)S(1)} %all-to-all-done.1.queries, bf16[8,512,128]{2,1,0:T(8,128)(2,1)S(1)} %all-to-all-done.own, bf16[8,512,128]{2,1,0:T(8,128)(2,1)S(1)} %collective-permute-done.other), custom_call_target="tpu_custom_call" | custom-call | flops 2147483648 | bytes 4194304 | tf_op jit(solution)/shard_map/pallas_call | solution.py:184
  66.3 5.5 %shard_map.123 = bf16[8,256,128]{2,1,0:T(8,128)(2,1)} custom-call(s32[1]{0:T(128)} %bitcast.place, bf16[8,256,128]{2,1,0:T(8,128)(2,1)S(1)} %all-to-all-done.1.queries, bf16[8,512,128]{2,1,0:T(8,128)(2,1)S(1)} %all-to-all-done.own, bf16[8,512,128]{2,1,0:T(8,128)(2,1)S(1)} %collective-permute-done.other, bf16[4,512,128]{2,1,0:T(8,128)(2,1)S(1)} %collective-permute-done.1.old, ...), custom_call_target="tpu_custom_call" | custom-call | flops 2147483648 | bytes 4194304 | tf_op jit(solution)/shard_map/pallas_call | solution.py:193
  71.8 6.7 %all-to-all-start.2 = ((bf16[8,256,128]{2,1,0:T(8,128)(2,1)}), bf16[8,256,128]{2,1,0:T(8,128)(2,1)S(1)}, u32[]{:S(2)}, u32[]{:S(2)}) async-start(bf16[8,256,128]{2,1,0:T(8,128)(2,1)} %shard_map.123), calls=%async_computation.2 | async-start | bytes 1048576 | tf_op jit(solution)/shard_map/all_to_all | solution.py:337
  79.1 2.4 %collective-permute-start.3 = (f32[32,256]{1,0:T(8,128)S(1)}, f32[32,256]{1,0:T(8,128)S(1)}, u32[]{:S(2)}, u32[]{:S(2)}) collective-permute-start(f32[32,256]{1,0:T(8,128)S(1)} %shard_map.125.p0), channel_id=1, source_target_pairs={{0,1},{1,2},{2,3},{3,0},{4,5},{5,6},{6,7},{7,4},{8,9},{9,10},{10,1... | collective-permute-start | bytes 98312 | tf_op jit(solution)/shard_map/ppermute | solution.py:358
  81.4 4.3 %collective-permute-start.4 = (f32[32,256]{1,0:T(8,128)S(1)}, f32[32,256]{1,0:T(8,128)S(1)}, u32[]{:S(2)}, u32[]{:S(2)}) collective-permute-start(f32[32,256]{1,0:T(8,128)S(1)} %shard_map.125.p0), channel_id=1, source_target_pairs={{0,2},{1,3},{2,0},{3,1},{4,6},{5,7},{6,4},{7,5},{8,10},{9,11},{10,... | collective-permute-start | bytes 98312 | tf_op jit(solution)/shard_map/ppermute | solution.py:358
  88.8 4.0 %collective-permute-done.5.p3 = f32[32,256]{1,0:T(8,128)S(1)} collective-permute-done((f32[32,256]{1,0:T(8,128)S(1)}, f32[32,256]{1,0:T(8,128)S(1)}, u32[]{:S(2)}, u32[]{:S(2)}) %collective-permute-start.5) | collective-permute-done | bytes 32800 | tf_op jit(solution)/shard_map/ppermute | solution.py:358
  92.8 5.1 %shard_map.126 = (f32[136,128]{1,0:T(8,128)S(1)}, f32[128,128]{1,0:T(8,128)S(1)}) custom-call(bf16[256,256]{1,0:T(8,128)(2,1)S(1)} %copy-done.3, bf16[256,1024]{1,0:T(8,128)(2,1)S(1)} %copy-done.1, f32[1,1024]{1,0:T(1,128)S(1)} %bitcast.3, bf16[256,1024]{1,0:T(8,128)(2,1)S(1)} %copy-done, f32[32,256]{1,0:T(8,128)S(1)} %shard_map.125.p0, ...), custom_call_target="tpu_custom_call" | custom-call | flops 25165824 | bytes 1048576 | tf_op jit(solution)/shard_map/pallas_call | solution.py:266
  97.9 3.9 %collective-permute-start.6 = (f32[136,128]{1,0:T(8,128)S(1)}, f32[136,128]{1,0:T(8,128)S(1)}, u32[]{:S(2)}, u32[]{:S(2)}) collective-permute-start(f32[136,128]{1,0:T(8,128)S(1)} %get-tuple-element.9), channel_id=1, source_target_pairs={{0,8},{4,12},{8,16},{12,20},{16,24},{20,28},{24,32},{28,36},{32,40... | collective-permute-start | bytes 208904 | tf_op jit(solution)/shard_map/ppermute | solution.py:342
  104.0 10.0 %collective-permute-start.8 = (f32[136,128]{1,0:T(8,128)S(1)}, f32[136,128]{1,0:T(8,128)S(1)}, u32[]{:S(2)}, u32[]{:S(2)}) collective-permute-start(f32[136,128]{1,0:T(8,128)S(1)} %shard_map.127.refs_3_), channel_id=1, source_target_pairs={{0,24},{4,28},{8,32},{12,36},{16,40},{20,44},{24,48},{28,52},{32,5... | collective-permute-start | bytes 208904 | tf_op jit(solution)/shard_map/ppermute | solution.py:342
  114.0 2.5 %collective-permute-start.9 = (f32[136,128]{1,0:T(8,128)S(1)}, f32[136,128]{1,0:T(8,128)S(1)}, u32[]{:S(2)}, u32[]{:S(2)}) collective-permute-start(f32[136,128]{1,0:T(8,128)S(1)} %shard_map.127.refs_3_), channel_id=1, source_target_pairs={{0,16},{4,20},{8,24},{12,28},{16,32},{20,36},{24,40},{28,44},{32,4... | collective-permute-start | bytes 208904 | tf_op jit(solution)/shard_map/ppermute | solution.py:342
  116.5 2.5 %collective-permute-start.10 = (f32[136,128]{1,0:T(8,128)S(1)}, f32[136,128]{1,0:T(8,128)S(1)}, u32[]{:S(2)}, u32[]{:S(2)}) collective-permute-start(f32[136,128]{1,0:T(8,128)S(1)} %shard_map.127.refs_3_), channel_id=1, source_target_pairs={{0,8},{4,12},{8,16},{12,20},{16,24},{20,28},{24,32},{28,36},{32,40... | collective-permute-start | bytes 208904 | tf_op jit(solution)/shard_map/ppermute | solution.py:342
  122.3 8.5 %collective-permute-start.11 = (f32[136,128]{1,0:T(8,128)S(1)}, f32[136,128]{1,0:T(8,128)S(1)}, u32[]{:S(2)}, u32[]{:S(2)}) collective-permute-start(f32[136,128]{1,0:T(8,128)S(1)} %shard_map.128.refs_1_), channel_id=1, source_target_pairs={{0,32},{4,36},{8,40},{12,44},{16,48},{20,52},{24,56},{28,60},{32,6... | collective-permute-start | bytes 208904 | tf_op jit(solution)/shard_map/ppermute | solution.py:342
  130.8 2.6 %collective-permute-done.11.refs_0_ = f32[136,128]{1,0:T(8,128)S(1)} collective-permute-done((f32[136,128]{1,0:T(8,128)S(1)}, f32[136,128]{1,0:T(8,128)S(1)}, u32[]{:S(2)}, u32[]{:S(2)}) %collective-permute-start.11) | collective-permute-done | bytes 69664 | tf_op jit(solution)/shard_map/ppermute | solution.py:342
  133.4 13.1 %collective-permute-start.12 = (f32[136,128]{1,0:T(8,128)S(1)}, f32[136,128]{1,0:T(8,128)S(1)}, u32[]{:S(2)}, u32[]{:S(2)}) collective-permute-start(f32[136,128]{1,0:T(8,128)S(1)} %shard_map.129.refs_3_), channel_id=1, source_target_pairs={{0,192},{4,196},{8,200},{12,204},{16,208},{20,212},{24,216},{28,22... | collective-permute-start | bytes 208904 | tf_op jit(solution)/shard_map/ppermute | solution.py:342
  146.5 5.2 %collective-permute-start.13 = (f32[136,128]{1,0:T(8,128)S(1)}, f32[136,128]{1,0:T(8,128)S(1)}, u32[]{:S(2)}, u32[]{:S(2)}) collective-permute-start(f32[136,128]{1,0:T(8,128)S(1)} %shard_map.129.refs_3_), channel_id=1, source_target_pairs={{0,128},{4,132},{8,136},{12,140},{16,144},{20,148},{24,152},{28,15... | collective-permute-start | bytes 208904 | tf_op jit(solution)/shard_map/ppermute | solution.py:342
  151.7 3.4 %collective-permute-start.14 = (f32[136,128]{1,0:T(8,128)S(1)}, f32[136,128]{1,0:T(8,128)S(1)}, u32[]{:S(2)}, u32[]{:S(2)}) collective-permute-start(f32[136,128]{1,0:T(8,128)S(1)} %shard_map.129.refs_3_), channel_id=1, source_target_pairs={{0,64},{4,68},{8,72},{12,76},{16,80},{20,84},{24,88},{28,92},{32,9... | collective-permute-start | bytes 208904 | tf_op jit(solution)/shard_map/ppermute | solution.py:342
  157.1 6.0 %collective-permute-start.15 = (f32[136,128]{1,0:T(8,128)S(1)}, f32[136,128]{1,0:T(8,128)S(1)}, u32[]{:S(2)}, u32[]{:S(2)}) collective-permute-start(f32[136,128]{1,0:T(8,128)S(1)} %shard_map.130.e1), channel_id=1, source_target_pairs={{0,256},{4,260},{8,264},{12,268},{16,272},{20,276},{24,280},{28,28... | collective-permute-start | bytes 208904 | tf_op jit(solution)/shard_map/ppermute | solution.py:342
  164.9 10.1 %shard_map.131 = bf16[256,1024]{1,0:T(8,128)(2,1)} custom-call(bf16[256,256]{1,0:T(8,128)(2,1)S(1)} %copy-done.3, bf16[256,1024]{1,0:T(8,128)(2,1)S(1)} %copy-done.1, f32[1,1024]{1,0:T(1,128)S(1)} %bitcast.4, bf16[256,1024]{1,0:T(8,128)(2,1)S(1)} %copy-done, f32[32,256]{1,0:T(8,128)S(1)} %shard_map.125.p0, f32[32,256]{1,0:T(8,128)S(1)} %collective-permute-done.3.p1, ...), custom_call_target="tpu_custom_call" | custom-call | flops 37748736 | bytes 2097152 | tf_op jit(solution)/shard_map/pallas_call | solution.py:331
  (44 shorter events, 19.8 us)
Async XLA Ops:
  3.0 35.8 %all-to-all-start = ((bf16[8,512,128]{2,1,0:T(8,128)(2,1)}), bf16[8,512,128]{2,1,0:T(8,128)(2,1)S(1)}, u32[]{:S(2)}, u32[]{:S(2)}) async-start(bf16[8,512,128]{2,1,0:T(8,128)(2,1)} %pack.2), calls=%async_computation | async-start | bytes 2097152 | tf_op jit(solution)/shard_map/all_to_all | solution.py:337
  38.9 23.8 %collective-permute-start = (bf16[8,512,128]{2,1,0:T(8,128)(2,1)S(1)}, bf16[8,512,128]{2,1,0:T(8,128)(2,1)S(1)}, u32[]{:S(2)}, u32[]{:S(2)}) collective-permute-start(bf16[8,512,128]{2,1,0:T(8,128)(2,1)S(1)} %all-to-all-done.own), channel_id=1, source_target_pairs={{0,4},{4,0},{8,12},{12,8},{16,20},{20,16},{24,28},{28,24},{32,36},... | collective-permute-start | bytes 3145736 | tf_op jit(solution)/shard_map/ppermute | solution.py:367
  40.8 21.9 %all-to-all-start.1 = ((bf16[8,256,128]{2,1,0:T(8,128)(2,1)}), bf16[8,256,128]{2,1,0:T(8,128)(2,1)S(1)}, u32[]{:S(2)}, u32[]{:S(2)}) async-start(bf16[8,256,128]{2,1,0:T(8,128)(2,1)} %pack.3), calls=%async_computation.1 | async-start | bytes 1048576 | tf_op jit(solution)/shard_map/all_to_all | solution.py:337
  44.4 16.1 %collective-permute-start.1 = (bf16[4,512,128]{2,1,0:T(8,128)(2,1)S(1)}, bf16[4,512,128]{2,1,0:T(8,128)(2,1)S(1)}, u32[]{:S(2)}, u32[]{:S(2)}) collective-permute-start(bf16[4,512,128]{2,1,0:T(8,128)(2,1)S(1)} %slice.3), channel_id=1, source_target_pairs={{0,64},{4,68},{8,72},{12,76},{16,80},{20,84},{24,88},{28,92},{32,9... | collective-permute-start | bytes 1572872 | tf_op jit(solution)/shard_map/ppermute | solution.py:366
  60.5 5.8 %collective-permute-start.2 = (bf16[4,512,128]{2,1,0:T(8,128)(2,1)S(1)}, bf16[4,512,128]{2,1,0:T(8,128)(2,1)}, u32[]{:S(2)}, u32[]{:S(2)}) collective-permute-start(bf16[4,512,128]{2,1,0:T(8,128)(2,1)S(1)} %collective-permute-done.1.old), channel_id=1, source_target_pairs={{0,4},{4,0},{8,12},{12,8},{16,20},{20,16},{24,28},{28,24},{32,36},... | collective-permute-start | bytes 1572872 | tf_op jit(solution)/shard_map/ppermute | solution.py:368
  71.8 103.2 %all-to-all-start.2 = ((bf16[8,256,128]{2,1,0:T(8,128)(2,1)}), bf16[8,256,128]{2,1,0:T(8,128)(2,1)S(1)}, u32[]{:S(2)}, u32[]{:S(2)}) async-start(bf16[8,256,128]{2,1,0:T(8,128)(2,1)} %shard_map.123), calls=%async_computation.2 | async-start | bytes 1048576 | tf_op jit(solution)/shard_map/all_to_all | solution.py:337
  78.5 14.3 %copy-start.1 = (bf16[256,1024]{1,0:T(8,128)(2,1)S(1)}, bf16[256,1024]{1,0:T(8,128)(2,1)}, u32[]{:S(2)}) copy-start(bf16[256,1024]{1,0:T(8,128)(2,1)} %proj.3) | copy-start | bytes 1572868
  78.7 14.1 %copy-start.3 = (bf16[256,256]{1,0:T(8,128)(2,1)S(1)}, bf16[256,256]{1,0:T(8,128)(2,1)}, u32[]{:S(2)}) copy-start(bf16[256,256]{1,0:T(8,128)(2,1)} %low.3) | copy-start | bytes 393220
  78.7 14.1 %copy-start.4 = (f32[16,1024]{1,0:T(8,128)S(1)}, f32[16,1024]{1,0:T(8,128)}, u32[]{:S(2)}) copy-start(f32[16,1024]{1,0:T(8,128)} %a_rate.1) | copy-start | bytes 196612
  79.1 8.6 %collective-permute-start.3 = (f32[32,256]{1,0:T(8,128)S(1)}, f32[32,256]{1,0:T(8,128)S(1)}, u32[]{:S(2)}, u32[]{:S(2)}) collective-permute-start(f32[32,256]{1,0:T(8,128)S(1)} %shard_map.125.p0), channel_id=1, source_target_pairs={{0,1},{1,2},{2,3},{3,0},{4,5},{5,6},{6,7},{7,4},{8,9},{9,10},{10,1... | collective-permute-start | bytes 98312 | tf_op jit(solution)/shard_map/ppermute | solution.py:358
  81.4 7.3 %collective-permute-start.4 = (f32[32,256]{1,0:T(8,128)S(1)}, f32[32,256]{1,0:T(8,128)S(1)}, u32[]{:S(2)}, u32[]{:S(2)}) collective-permute-start(f32[32,256]{1,0:T(8,128)S(1)} %shard_map.125.p0), channel_id=1, source_target_pairs={{0,2},{1,3},{2,0},{3,1},{4,6},{5,7},{6,4},{7,5},{8,10},{9,11},{10,... | collective-permute-start | bytes 98312 | tf_op jit(solution)/shard_map/ppermute | solution.py:358
  85.8 7.0 %collective-permute-start.5 = (f32[32,256]{1,0:T(8,128)S(1)}, f32[32,256]{1,0:T(8,128)S(1)}, u32[]{:S(2)}, u32[]{:S(2)}) collective-permute-start(f32[32,256]{1,0:T(8,128)S(1)} %shard_map.125.p0), channel_id=1, source_target_pairs={{0,3},{1,0},{2,1},{3,2},{4,7},{5,4},{6,5},{7,6},{8,11},{9,8},{10,9... | collective-permute-start | bytes 98312 | tf_op jit(solution)/shard_map/ppermute | solution.py:358
  97.9 5.8 %collective-permute-start.6 = (f32[136,128]{1,0:T(8,128)S(1)}, f32[136,128]{1,0:T(8,128)S(1)}, u32[]{:S(2)}, u32[]{:S(2)}) collective-permute-start(f32[136,128]{1,0:T(8,128)S(1)} %get-tuple-element.9), channel_id=1, source_target_pairs={{0,8},{4,12},{8,16},{12,20},{16,24},{20,28},{24,32},{28,36},{32,40... | collective-permute-start | bytes 208904 | tf_op jit(solution)/shard_map/ppermute | solution.py:342
  101.8 2.2 %collective-permute-start.7 = (f32[136,128]{1,0:T(8,128)S(1)}, f32[136,128]{1,0:T(8,128)S(1)}, u32[]{:S(2)}, u32[]{:S(2)}) collective-permute-start(f32[136,128]{1,0:T(8,128)S(1)} %get-tuple-element.9), channel_id=1, source_target_pairs={{0,4},{4,8},{8,12},{12,16},{16,20},{20,24},{24,28},{28,32},{32,36}... | collective-permute-start | bytes 208904 | tf_op jit(solution)/shard_map/ppermute | solution.py:342
  104.0 60.8 %copy-start.2 = (bf16[256,1024]{1,0:T(8,128)(2,1)S(1)}, bf16[256,1024]{1,0:T(8,128)(2,1)}, u32[]{:S(2)}) copy-start(bf16[256,1024]{1,0:T(8,128)(2,1)} %gate.1) | copy-start | bytes 1572868
  104.0 15.0 %collective-permute-start.8 = (f32[136,128]{1,0:T(8,128)S(1)}, f32[136,128]{1,0:T(8,128)S(1)}, u32[]{:S(2)}, u32[]{:S(2)}) collective-permute-start(f32[136,128]{1,0:T(8,128)S(1)} %shard_map.127.refs_3_), channel_id=1, source_target_pairs={{0,24},{4,28},{8,32},{12,36},{16,40},{20,44},{24,48},{28,52},{32,5... | collective-permute-start | bytes 208904 | tf_op jit(solution)/shard_map/ppermute | solution.py:342
  114.0 7.3 %collective-permute-start.9 = (f32[136,128]{1,0:T(8,128)S(1)}, f32[136,128]{1,0:T(8,128)S(1)}, u32[]{:S(2)}, u32[]{:S(2)}) collective-permute-start(f32[136,128]{1,0:T(8,128)S(1)} %shard_map.127.refs_3_), channel_id=1, source_target_pairs={{0,16},{4,20},{8,24},{12,28},{16,32},{20,36},{24,40},{28,44},{32,4... | collective-permute-start | bytes 208904 | tf_op jit(solution)/shard_map/ppermute | solution.py:342
  116.5 5.8 %collective-permute-start.10 = (f32[136,128]{1,0:T(8,128)S(1)}, f32[136,128]{1,0:T(8,128)S(1)}, u32[]{:S(2)}, u32[]{:S(2)}) collective-permute-start(f32[136,128]{1,0:T(8,128)S(1)} %shard_map.127.refs_3_), channel_id=1, source_target_pairs={{0,8},{4,12},{8,16},{12,20},{16,24},{20,28},{24,32},{28,36},{32,40... | collective-permute-start | bytes 208904 | tf_op jit(solution)/shard_map/ppermute | solution.py:342
  122.3 11.1 %collective-permute-start.11 = (f32[136,128]{1,0:T(8,128)S(1)}, f32[136,128]{1,0:T(8,128)S(1)}, u32[]{:S(2)}, u32[]{:S(2)}) collective-permute-start(f32[136,128]{1,0:T(8,128)S(1)} %shard_map.128.refs_1_), channel_id=1, source_target_pairs={{0,32},{4,36},{8,40},{12,44},{16,48},{20,52},{24,56},{28,60},{32,6... | collective-permute-start | bytes 208904 | tf_op jit(solution)/shard_map/ppermute | solution.py:342
  133.4 31.4 %copy-start.6 = (f32[1024]{0:T(1024)S(1)}, f32[1024]{0:T(1024)}, u32[]{:S(2)}) copy-start(f32[1024]{0:T(1024)} %param.21) | copy-start | bytes 12292
  133.4 21.7 %collective-permute-start.12 = (f32[136,128]{1,0:T(8,128)S(1)}, f32[136,128]{1,0:T(8,128)S(1)}, u32[]{:S(2)}, u32[]{:S(2)}) collective-permute-start(f32[136,128]{1,0:T(8,128)S(1)} %shard_map.129.refs_3_), channel_id=1, source_target_pairs={{0,192},{4,196},{8,200},{12,204},{16,208},{20,212},{24,216},{28,22... | collective-permute-start | bytes 208904 | tf_op jit(solution)/shard_map/ppermute | solution.py:342
  146.5 8.6 %collective-permute-start.13 = (f32[136,128]{1,0:T(8,128)S(1)}, f32[136,128]{1,0:T(8,128)S(1)}, u32[]{:S(2)}, u32[]{:S(2)}) collective-permute-start(f32[136,128]{1,0:T(8,128)S(1)} %shard_map.129.refs_3_), channel_id=1, source_target_pairs={{0,128},{4,132},{8,136},{12,140},{16,144},{20,148},{24,152},{28,15... | collective-permute-start | bytes 208904 | tf_op jit(solution)/shard_map/ppermute | solution.py:342
  151.7 5.3 %collective-permute-start.14 = (f32[136,128]{1,0:T(8,128)S(1)}, f32[136,128]{1,0:T(8,128)S(1)}, u32[]{:S(2)}, u32[]{:S(2)}) collective-permute-start(f32[136,128]{1,0:T(8,128)S(1)} %shard_map.129.refs_3_), channel_id=1, source_target_pairs={{0,64},{4,68},{8,72},{12,76},{16,80},{20,84},{24,88},{28,92},{32,9... | collective-permute-start | bytes 208904 | tf_op jit(solution)/shard_map/ppermute | solution.py:342
  157.1 7.8 %collective-permute-start.15 = (f32[136,128]{1,0:T(8,128)S(1)}, f32[136,128]{1,0:T(8,128)S(1)}, u32[]{:S(2)}, u32[]{:S(2)}) collective-permute-start(f32[136,128]{1,0:T(8,128)S(1)} %shard_map.130.e1), channel_id=1, source_target_pairs={{0,256},{4,260},{8,264},{12,268},{16,272},{20,276},{24,280},{28,28... | collective-permute-start | bytes 208904 | tf_op jit(solution)/shard_map/ppermute | solution.py:342
  (3 other events, 27.6 us)

commit v3 on v2

--- a/solution.py
+++ b/solution.py
@@ -219,9 +219,9 @@
 
 
 def spread(parts, count, wide):
-    total = parts[0][0:count, :]
-    for part in parts[1:]:
-        total = total + part[0:count, :]
+    total = parts[0, 0:count, :]
+    for k in range(1, parts.shape[0]):
+        total = total + parts[k, 0:count, :]
     total = total.T
     rows = total.shape[0]
     for n in range(count):
@@ -235,10 +235,10 @@
     return [held[n * TILES : (n + 1) * TILES, :] for n in range(NS)]
 
 
-def ends_body(low, proj, bias, xin, p0, p1, p2, p3, a_rate, out, held, wide, steps, drive):
-    rows = p0.shape[1]
+def ends_body(low, proj, bias, xin, partials, a_rate, out, held, wide, steps, drive):
+    rows = xin.shape[0]
     load_steps(low, proj, bias, xin, steps, drive)
-    spread((p0, p1, p2, p3), NS, wide)
+    spread(partials, NS, wide)
     rates = load_rates(a_rate, held)
 
     def step(t, carry):
@@ -263,43 +263,53 @@
     rates = jax.ShapeDtypeStruct((NS * TILES, LANES), F32)
     scratch = [pltpu.VMEM((rows * NS, LANES), F32)] + [pltpu.VMEM((rows * TILES, LANES), F32)] * 2
     estimate = cost(6 * rows * width * NS, 4 * rows * width, rows * width * NS)
-    return local(ends_body, (out, rates), scratch, 0, 9, estimate)(*sources, *partials, a_rate)
-
-
-def fold(rates, parts):
-    state = [parts[0][n * TILES : (n + 1) * TILES, :] for n in range(NS)]
-    through = parts[0][NS * TILES :, :]
-    for part in parts[1:]:
-        size = part[NS * TILES :, :]
-        for n in range(NS):
-            row = slice(n * TILES, (n + 1) * TILES)
-            state[n] = jnp.exp2(size * rates[row, :]) * state[n] + part[row, :]
-        through = through + size
-    return state, through
-
-
-def join_body(rates, *refs):
-    *parts, out = refs
-    state, through = fold(rates, parts)
+    return local(ends_body, (out, rates), scratch, 0, 6, estimate)(*sources, partials, a_rate)
+
+
+def fold(rates, state, through, part):
+    size = part[NS * TILES :, :]
+    out = []
     for n in range(NS):
-        out[n * TILES : (n + 1) * TILES, :] = state[n]
-    out[NS * TILES :, :] = through
-
-
-def join(rates, parts):
-    out = jax.ShapeDtypeStruct(parts[0].shape, F32)
-    estimate = cost(1 << 16, 1 << 18)
-    return local(join_body, out, arrays=1 + len(parts), estimate=estimate)(rates, *parts)
+        row = slice(n * TILES, (n + 1) * TILES)
+        out.append(jnp.exp2(size * rates[row, :]) * state[n] + part[row, :])
+    return out, through + size
+
+
+def row_body(place, rates, blocks, before, whole):
+    mine = place[0] & (blocks.shape[0] - 1)
+    state = [jnp.zeros((TILES, LANES), F32)] * NS
+    through = jnp.zeros((TILES, LANES), F32)
+    held = state + [through]
+    for k in range(blocks.shape[0]):
+        here = mine == k
+        held = [jnp.where(here, now, old) for now, old in zip(state + [through], held)]
+        state, through = fold(rates, state, through, blocks[k])
+    for n in range(NS + 1):
+        row = slice(n * TILES, (n + 1) * TILES)
+        before[row, :] = held[n]
+        whole[row, :] = (state + [through])[n]
+
+
+def join_row(place, rates, blocks):
+    out = jax.ShapeDtypeStruct(blocks.shape[1:], F32)
+    estimate = cost(1 << 20, 2 << 20)
+    return local(row_body, (out, out), (), 1, 2, estimate)(place, rates, blocks)
 
 
 def final_body(
-    low, proj, bias, xin, p0, p1, p2, p3, held, e0, e1, gate, skip, out, wide, mix, steps, drive
+    place, low, proj, bias, xin, partials, held, planes, before, gate, skip, out, wide, mix, steps, drive
 ):
-    rows = p0.shape[1]
+    rows = xin.shape[0]
     load_steps(low, proj, bias, xin, steps, drive)
-    spread((p0, p1, p2, p3), 2 * NS, wide)
+    spread(partials, 2 * NS, wide)
     rates = [held[n * TILES : (n + 1) * TILES, :] for n in range(NS)]
-    state, _ = fold(held, (e0, e1))
+    state = [jnp.zeros((TILES, LANES), F32)] * NS
+    through = jnp.zeros((TILES, LANES), F32)
+    for z in range(planes.shape[0]):
+        earlier = z < plane_of(place)
+        later, _ = fold(held, state, through, planes[z])
+        state = [jnp.where(earlier, new, old) for new, old in zip(later, state)]
+    state, _ = fold(held, state, through, before)
 
     def step(t, state):
         size, push = steps[rows_of(t), :], drive[rows_of(t), :]
@@ -322,14 +332,14 @@
         out[:, col] = (mixed * (opened / (1.0 + jnp.exp(-opened)))).astype(BF16)
 
 
-def finish(sources, partials, rates, entering, gate, skip):
+def finish(place, sources, partials, rates, planes, before, gate, skip):
     rows, width = gate.shape
     out = jax.ShapeDtypeStruct(gate.shape, BF16)
     tall = pltpu.VMEM((rows * TILES, LANES), F32)
     scratch = [pltpu.VMEM((rows * 2 * NS, LANES), F32), tall, tall, tall]
     estimate = cost(9 * rows * width * NS, 8 * rows * width, rows * width * NS)
-    return local(final_body, out, scratch, 0, 13, estimate)(
-        *sources, *partials, rates, *entering, gate, skip.reshape(1, -1)
+    return local(final_body, out, scratch, 1, 10, estimate)(
+        place, *sources, partials, rates, planes, before, gate, skip.reshape(1, -1)
     )
 
 
@@ -337,27 +347,21 @@
     return lax.all_to_all(x, "ctx", 0, 0, axis_index_groups=groups, tiled=True)
 
 
-def after(part, distance):
-    count = lax.axis_size("ctx")
-    return lax.ppermute(part, "ctx", [(i, i + distance) for i in range(count - distance)])
-
-
 def shards(query, key, value, xin, gate_z, w_bc, dt_low, dt_proj, dt_bias, a_rate, skip):
-    ctx, tp = lax.axis_size("ctx"), lax.axis_size("tp")
+    ctx = lax.axis_size("ctx")
     side, planes = 8, ctx // 16
     line = 2 * side
     index = lax.axis_index("ctx")
     place = index.astype(jnp.int32).reshape(1)
     along_y = [[z * line + 2 * y + c for y in range(side)] for z in range(planes) for c in (0, 1)]
+    along_z = [[z * line + k for z in range(planes)] for k in range(line)]
+    along_row = [[z * line + k for k in range(line)] for z in range(planes)]
     partner = [(i, i ^ 1) for i in range(ctx)]
     next_row = [(i, i + line) for i in range(ctx - line)]
 
     own_kv = exchange(pack(key, value), along_y)
     partial = project(xin, w_bc)
-    partials = [partial] + [
-        lax.ppermute(partial, "tp", [(i, (i + d) % tp) for i in range(tp)])
-        for d in range(1, tp)
-    ]
+    partials = lax.all_gather(partial, "tp")
     sources = (dt_low, dt_proj, dt_bias.reshape(1, -1), xin)
     ends, rates = block_ends(sources, partials, a_rate)
     queries = pack(query)
@@ -366,16 +370,14 @@
     old_kv = lax.ppermute(own_kv[side // 2 :], "ctx", next_row)
     other_kv = lax.ppermute(own_kv, "ctx", partner)
     past_kv = lax.ppermute(old_kv, "ctx", partner)
-    ends = join(rates, [after(ends, 2), after(ends, 1)])
-    ends = join(rates, [after(ends, 6), after(ends, 4), after(ends, 2), ends])
-    ends = join(rates, [after(ends, 8), ends])
-    ends = join(rates, [after(ends, 48), after(ends, 32), after(ends, 16), ends])
-    entering = [after(ends, 64), ends]
+    blocks = lax.all_gather(ends, "ctx", axis_index_groups=along_row)
+    before, whole = join_row(place, rates, blocks)
+    wholes = lax.all_gather(whole, "ctx", axis_index_groups=along_z)
     later = attend_late(place, queries, own_kv, other_kv)
     attended = attend_early(place, queries, own_kv, other_kv, old_kv, past_kv, later)
     attended = exchange(attended, along_y)
     attended = unpack(attended)
-    mixed = finish(sources, partials, rates, entering, gate_z, skip)
+    mixed = finish(place, sources, partials, rates, wholes, before, gate_z, skip)
     return (attended, mixed)
 
 

time: 177 us -> 155 us (0.88)
  the two profiles are of different devices: /device:TPU:6 before, /device:TPU:2 now
where the time goes in v3:
time: 155 us
  blocking collectives  40.3 us (26%)
  waiting for transfers between devices  39.9 us (26%)
  Pallas kernels  31.4 us (20%)
  starting transfers between devices  26.3 us (17%)
  between operations  14.2 us (9%)
  local copies, waits for them, and re-layouts  2.53 us (2%)
    all_gather x1, blocking collectives, shards(): wholes = lax.all_gather(whole, 'ctx', axis_index_groups=along_z)  28.3 us
    all_to_all x3, waiting for transfers between devices, exchange(): return lax.all_to_all(x, 'ctx', 0, 0, axis_index_groups=groups, tiled=True)  26.5 us
    all_to_all x3, starting transfers between devices, exchange(): return lax.all_to_all(x, 'ctx', 0, 0, axis_index_groups=groups, tiled=True)  17.4 us
    all_gather x1, blocking collectives, shards(): partials = lax.all_gather(partial, 'tp')  12.1 us
    pallas_call x1, Pallas kernels, finish(): local(final_body, out, scratch, 1, 10, estimate)  10.2 us
    ppermute x1, waiting for transfers between devices, shards(): old_kv = lax.ppermute(own_kv[side // 2:], 'ctx', next_row)  8.14 us
    pallas_call x1, Pallas kernels, attend_early(): local(early_body, out, scratch, 1, 6, estimate)  5.79 us
    pallas_call x1, Pallas kernels, block_ends(): local(ends_body, (out, rates), scratch, 0, 6, estimate)  5.78 us
  transfers between devices with their start and end apart: 7, of which 4 were waited for; matrix products, arithmetic and copies ran while one was open for 0% of the time, Pallas kernels for 18%

profile of v3, /device:TPU:2, one launch (start us, length us, event | category | flops | bytes accessed | tf_op | source)
XLA Modules:
  0.0 154.7 jit_solution(10007026458610662928)
XLA Ops:
  7.2 2.4 %pack.2 = bf16[8,512,128]{2,1,0:T(8,128)(2,1)} custom-call(bf16[256,1024]{1,0:T(8,128)(2,1)} %refs_0_.2, bf16[256,1024]{1,0:T(8,128)(2,1)} %refs_1_.1), custom_call_target="tpu_custom_call" | custom-call | bytes 2097152 | tf_op jit(solution)/shard_map/pack/pallas_call | solution.py:63
  9.6 7.2 %all-to-all-start = ((bf16[8,512,128]{2,1,0:T(8,128)(2,1)}), bf16[8,512,128]{2,1,0:T(8,128)(2,1)S(1)}, u32[]{:S(2)}, u32[]{:S(2)}) async-start(bf16[8,512,128]{2,1,0:T(8,128)(2,1)} %pack.2), calls=%async_computation | async-start | bytes 2097152 | tf_op jit(solution)/shard_map/all_to_all | solution.py:347
  16.9 2.0 %pack.3 = bf16[8,256,128]{2,1,0:T(8,128)(2,1)} custom-call(bf16[256,1024]{1,0:T(8,128)(2,1)} %refs_0_.3), custom_call_target="tpu_custom_call" | custom-call | bytes 1048576 | tf_op jit(solution)/shard_map/pack/pallas_call | solution.py:63
  18.9 0.2 copy.13.w_bc
  19.1 0.3 shard_map.125
  19.4 26.1 %all-to-all-done.own = bf16[8,512,128]{2,1,0:T(8,128)(2,1)S(1)} async-done(((bf16[8,512,128]{2,1,0:T(8,128)(2,1)}), bf16[8,512,128]{2,1,0:T(8,128)(2,1)S(1)}, u32[]{:S(2)}, u32[]{:S(2)}) %all-to-all-start) | async-done | bytes 1048608 | tf_op jit(solution)/shard_map/all_to_all | solution.py:347
  45.6 1.9 %collective-permute-start = (bf16[8,512,128]{2,1,0:T(8,128)(2,1)S(1)}, bf16[8,512,128]{2,1,0:T(8,128)(2,1)S(1)}, u32[]{:S(2)}, u32[]{:S(2)}) collective-permute-start(bf16[8,512,128]{2,1,0:T(8,128)(2,1)S(1)} %all-to-all-done.own), channel_id=1, source_target_pairs={{0,4},{4,0},{8,12},{12,8},{16,20},{20,16},{24,28},{28,24},{32,36},... | collective-permute-start | bytes 3145736 | tf_op jit(solution)/shard_map/ppermute | solution.py:371
  47.5 12.1 %all-gather = f32[128,256]{1,0:T(8,128)S(1)} all-gather(f32[32,256]{1,0:T(8,128)S(1)} %shard_map.125), channel_id=2, replica_groups=mesh['ctx'=128,'tp'=4] {'tp'}, dimensions={0}, use_global_device_ids=true | all-gather | bytes 163840 | tf_op jit(solution)/shard_map/all_gather | solution.py:364
  59.5 1.0 copy-done.2
  60.6 5.8 %shard_map.126 = (f32[136,128]{1,0:T(8,128)}, f32[128,128]{1,0:T(8,128)S(1)}) custom-call(bf16[256,256]{1,0:T(8,128)(2,1)S(1)} %copy-done.5, bf16[256,1024]{1,0:T(8,128)(2,1)S(1)} %copy-done.2, f32[1,1024]{1,0:T(1,128)S(1)} %bitcast.10, bf16[256,1024]{1,0:T(8,128)(2,1)S(1)} %copy-done.1, f32[4,32,256]{2,1,0:T(8,128)S(1)} %bitcast.8, f32[16,1024]{1,0:T(8,128)S(1)} %copy-done.7), custom_call_target="tpu_custom_call" | custom-call | flops 25165824 | bytes 1048576 | tf_op jit(solution)/shard_map/pallas_call | solution.py:266
  66.4 3.5 %all-to-all-start.1 = ((bf16[8,256,128]{2,1,0:T(8,128)(2,1)}), bf16[8,256,128]{2,1,0:T(8,128)(2,1)S(1)}, u32[]{:S(2)}, u32[]{:S(2)}) async-start(bf16[8,256,128]{2,1,0:T(8,128)(2,1)} %pack.3), calls=%async_computation.1 | async-start | bytes 1048576 | tf_op jit(solution)/shard_map/all_to_all | solution.py:347
  69.9 5.1 %collective-permute-start.1 = (bf16[4,512,128]{2,1,0:T(8,128)(2,1)S(1)}, bf16[4,512,128]{2,1,0:T(8,128)(2,1)}, u32[]{:S(2)}, u32[]{:S(2)}) collective-permute-start(bf16[4,512,128]{2,1,0:T(8,128)(2,1)S(1)} %slice.3), channel_id=1, source_target_pairs={{0,64},{4,68},{8,72},{12,76},{16,80},{20,84},{24,88},{28,92},{32,9... | collective-permute-start | bytes 1572872 | tf_op jit(solution)/shard_map/ppermute | solution.py:370
  75.0 8.1 %collective-permute-done.1.old = bf16[4,512,128]{2,1,0:T(8,128)(2,1)} collective-permute-done((bf16[4,512,128]{2,1,0:T(8,128)(2,1)S(1)}, bf16[4,512,128]{2,1,0:T(8,128)(2,1)}, u32[]{:S(2)}, u32[]{:S(2)}) %collective-permute-start.1) | collective-permute-done | bytes 524320 | tf_op jit(solution)/shard_map/ppermute | solution.py:370
  83.2 1.9 %collective-permute-start.2 = (bf16[4,512,128]{2,1,0:T(8,128)(2,1)}, bf16[4,512,128]{2,1,0:T(8,128)(2,1)}, u32[]{:S(2)}, u32[]{:S(2)}) collective-permute-start(bf16[4,512,128]{2,1,0:T(8,128)(2,1)} %collective-permute-done.1.old), channel_id=1, source_target_pairs={{0,4},{4,0},{8,12},{12,8},{16,20},{20,16},{24,28},{28,24},{32,36},... | collective-permute-start | bytes 1572872 | tf_op jit(solution)/shard_map/ppermute | solution.py:372
  85.1 0.4 all-to-all-done.1.queries
  85.5 3.7 %shard_map.122.later = bf16[4,256,128]{2,1,0:T(8,128)(2,1)S(1)} custom-call(s32[1]{0:T(128)} %bitcast.place, bf16[8,256,128]{2,1,0:T(8,128)(2,1)S(1)} %all-to-all-done.1.queries, bf16[8,512,128]{2,1,0:T(8,128)(2,1)S(1)} %all-to-all-done.own, bf16[8,512,128]{2,1,0:T(8,128)(2,1)S(1)} %collective-permute-done.other), custom_call_target="tpu_custom_call" | custom-call | flops 2147483648 | bytes 4194304 | tf_op jit(solution)/shard_map/pallas_call | solution.py:184
  89.2 5.8 %shard_map.123 = bf16[8,256,128]{2,1,0:T(8,128)(2,1)} custom-call(s32[1]{0:T(128)} %bitcast.place, bf16[8,256,128]{2,1,0:T(8,128)(2,1)S(1)} %all-to-all-done.1.queries, bf16[8,512,128]{2,1,0:T(8,128)(2,1)S(1)} %all-to-all-done.own, bf16[8,512,128]{2,1,0:T(8,128)(2,1)S(1)} %collective-permute-done.other, bf16[4,512,128]{2,1,0:T(8,128)(2,1)} %collective-permute-done.1.old, ...), custom_call_target="tpu_custom_call" | custom-call | flops 2147483648 | bytes 4194304 | tf_op jit(solution)/shard_map/pallas_call | solution.py:193
  95.0 6.6 %all-to-all-start.2 = ((bf16[8,256,128]{2,1,0:T(8,128)(2,1)}), bf16[8,256,128]{2,1,0:T(8,128)(2,1)S(1)}, u32[]{:S(2)}, u32[]{:S(2)}) async-start(bf16[8,256,128]{2,1,0:T(8,128)(2,1)} %shard_map.123), calls=%async_computation.2 | async-start | bytes 1048576 | tf_op jit(solution)/shard_map/all_to_all | solution.py:347
  101.6 5.3 %all-gather.5.cloned.1.call-done = f32[2176,128]{1,0:T(8,128)} async-done(((f32[136,128]{1,0:T(8,128)}), f32[2176,128]{1,0:T(8,128)}) %all-gather.5.cloned.1.call-update) | async-done | bytes 1114128 | tf_op jit(solution)/shard_map/all_gather | solution.py:373
  106.9 1.2 copy-done
  108.2 0.2 shard_map.127
  108.4 28.3 %all-gather.2 = f32[1088,128]{1,0:T(8,128)S(1)} all-gather(f32[136,128]{1,0:T(8,128)S(1)} %get-tuple-element.12), channel_id=4, replica_groups={{0,64,128,192,256,320,384,448},{4,68,132,196,260,324,388,452},{8,72,136..., dimensions={0}, use_global_device_ids=true | all-gather | bytes 626688 | tf_op jit(solution)/shard_map/all_gather | solution.py:375
  136.7 10.2 %shard_map.128 = bf16[256,1024]{1,0:T(8,128)(2,1)} custom-call(s32[1]{0:T(128)} %bitcast.place, bf16[256,256]{1,0:T(8,128)(2,1)S(1)} %copy-done.6, bf16[256,1024]{1,0:T(8,128)(2,1)S(1)} %copy-done.3, f32[1,1024]{1,0:T(1,128)S(1)} %bitcast.11, bf16[256,1024]{1,0:T(8,128)(2,1)S(1)} %copy-done.1, f32[4,32,256]{2,1,0:T(8,128)S(1)} %bitcast.9, ...), custom_call_target="tpu_custom_call" | custom-call | flops 37748736 | bytes 2097152 | tf_op jit(solution)/shard_map/pallas_call | solution.py:341
  146.9 0.9 shard_map.124
  (26 shorter events, 0.2 us)
Async XLA Ops:
  9.6 9.3 %copy-start.10 = (bf16[1024,32]{0,1:T(8,128)(2,1)S(1)}, bf16[1024,32]{0,1:T(8,128)(2,1)}, u32[]{:S(2)}) copy-start(bf16[1024,32]{0,1:T(8,128)(2,1)} %param.16) | copy-start | bytes 196612
  9.6 36.0 %all-to-all-start = ((bf16[8,512,128]{2,1,0:T(8,128)(2,1)}), bf16[8,512,128]{2,1,0:T(8,128)(2,1)S(1)}, u32[]{:S(2)}, u32[]{:S(2)}) async-start(bf16[8,512,128]{2,1,0:T(8,128)(2,1)} %pack.2), calls=%async_computation | async-start | bytes 2097152 | tf_op jit(solution)/shard_map/all_to_all | solution.py:347
  16.8 2.3 %copy-start.1 = (bf16[256,1024]{1,0:T(8,128)(2,1)S(1)}, bf16[256,1024]{1,0:T(8,128)(2,1)}, u32[]{:S(2)}) copy-start(bf16[256,1024]{1,0:T(8,128)(2,1)} %xin.5) | copy-start | bytes 1572868
  16.8 42.7 %copy-start.5 = (bf16[256,256]{1,0:T(8,128)(2,1)S(1)}, bf16[256,256]{1,0:T(8,128)(2,1)}, u32[]{:S(2)}) copy-start(bf16[256,256]{1,0:T(8,128)(2,1)} %low.3) | copy-start | bytes 393220
  16.8 42.7 %copy-start.7 = (f32[16,1024]{1,0:T(8,128)S(1)}, f32[16,1024]{1,0:T(8,128)}, u32[]{:S(2)}) copy-start(f32[16,1024]{1,0:T(8,128)} %a_rate.1) | copy-start | bytes 196612
  16.9 42.7 %copy-start.8 = (f32[1024]{0:T(1024)S(1)}, f32[1024]{0:T(1024)}, u32[]{:S(2)}) copy-start(f32[1024]{0:T(1024)} %param.19) | copy-start | bytes 12292
  16.9 90.1 %all-gather.5.cloned.1.call-start = ((), (), s32[]{:S(2)}) async-start(), calls=%async_computation.3 | async-start | bytes 1183744 | tf_op jit(solution)/shard_map/all_gather | solution.py:373
  45.6 39.9 %collective-permute-start = (bf16[8,512,128]{2,1,0:T(8,128)(2,1)S(1)}, bf16[8,512,128]{2,1,0:T(8,128)(2,1)S(1)}, u32[]{:S(2)}, u32[]{:S(2)}) collective-permute-start(bf16[8,512,128]{2,1,0:T(8,128)(2,1)S(1)} %all-to-all-done.own), channel_id=1, source_target_pairs={{0,4},{4,0},{8,12},{12,8},{16,20},{20,16},{24,28},{28,24},{32,36},... | collective-permute-start | bytes 3145736 | tf_op jit(solution)/shard_map/ppermute | solution.py:371
  59.5 1.0 copy-start.2
  66.4 19.1 %all-to-all-start.1 = ((bf16[8,256,128]{2,1,0:T(8,128)(2,1)}), bf16[8,256,128]{2,1,0:T(8,128)(2,1)S(1)}, u32[]{:S(2)}, u32[]{:S(2)}) async-start(bf16[8,256,128]{2,1,0:T(8,128)(2,1)} %pack.3), calls=%async_computation.1 | async-start | bytes 1048576 | tf_op jit(solution)/shard_map/all_to_all | solution.py:347
  69.9 13.2 %collective-permute-start.1 = (bf16[4,512,128]{2,1,0:T(8,128)(2,1)S(1)}, bf16[4,512,128]{2,1,0:T(8,128)(2,1)}, u32[]{:S(2)}, u32[]{:S(2)}) collective-permute-start(bf16[4,512,128]{2,1,0:T(8,128)(2,1)S(1)} %slice.3), channel_id=1, source_target_pairs={{0,64},{4,68},{8,72},{12,76},{16,80},{20,84},{24,88},{28,92},{32,9... | collective-permute-start | bytes 1572872 | tf_op jit(solution)/shard_map/ppermute | solution.py:370
  83.2 6.0 %collective-permute-start.2 = (bf16[4,512,128]{2,1,0:T(8,128)(2,1)}, bf16[4,512,128]{2,1,0:T(8,128)(2,1)}, u32[]{:S(2)}, u32[]{:S(2)}) collective-permute-start(bf16[4,512,128]{2,1,0:T(8,128)(2,1)} %collective-permute-done.1.old), channel_id=1, source_target_pairs={{0,4},{4,0},{8,12},{12,8},{16,20},{20,16},{24,28},{28,24},{32,36},... | collective-permute-start | bytes 1572872 | tf_op jit(solution)/shard_map/ppermute | solution.py:372
  89.2 47.5 %copy-start.9 = (f32[1024]{0:T(1024)S(1)}, f32[1024]{0:T(1024)}, u32[]{:S(2)}) copy-start(f32[1024]{0:T(1024)} %param.21) | copy-start | bytes 12292
  95.0 41.7 %copy-start.3 = (bf16[256,1024]{1,0:T(8,128)(2,1)S(1)}, bf16[256,1024]{1,0:T(8,128)(2,1)}, u32[]{:S(2)}) copy-start(bf16[256,1024]{1,0:T(8,128)(2,1)} %proj.3) | copy-start | bytes 1572868
  95.0 41.7 %copy-start.4 = (bf16[256,1024]{1,0:T(8,128)(2,1)S(1)}, bf16[256,1024]{1,0:T(8,128)(2,1)}, u32[]{:S(2)}) copy-start(bf16[256,1024]{1,0:T(8,128)(2,1)} %gate.1) | copy-start | bytes 1572868
  95.0 51.9 %all-to-all-start.2 = ((bf16[8,256,128]{2,1,0:T(8,128)(2,1)}), bf16[8,256,128]{2,1,0:T(8,128)(2,1)S(1)}, u32[]{:S(2)}, u32[]{:S(2)}) async-start(bf16[8,256,128]{2,1,0:T(8,128)(2,1)} %shard_map.123), calls=%async_computation.2 | async-start | bytes 1048576 | tf_op jit(solution)/shard_map/all_to_all | solution.py:347
  106.9 1.2 copy-start
  108.2 28.5 %copy-start.6 = (bf16[256,256]{1,0:T(8,128)(2,1)S(1)}, bf16[256,256]{1,0:T(8,128)(2,1)}, u32[]{:S(2)}) copy-start(bf16[256,256]{1,0:T(8,128)(2,1)} %low.3) | copy-start | bytes 393220
Sparse Core Ops, SparseCore 0:
  66.5 40.3 all-gather.4

commit v4 on v2

--- a/solution.py
+++ b/solution.py
@@ -1,3 +1,5 @@
+import functools
+
 import jax
 import jax.numpy as jnp
 from jax import lax
@@ -111,9 +113,9 @@
     out[i] = (total[:, 0:HD] / total[:, HD : 2 * HD]).astype(BF16)
 
 
-def late_body(place, queries, own, other, out):
+def late_body(place, own, other, out):
     half = out.shape[0]
-    rows = queries.shape[1]
+    rows = out.shape[1]
     parity = parity_of(place)
     ones = jnp.ones((rows, HD), BF16)
 
@@ -123,12 +125,11 @@
     for i in range(half):
         full = [block(own, i + 1 + j) for j in range(half - 1)]
         full += [block(other, i + parity + j) for j in range(half)]
-        weigh(queries[half + i], (block(own, half + i), block(own, i)), full, out, i)
-
-
-def early_body(place, queries, own, other, old, past, later, out, ko, kp):
-    half = later.shape[0]
-    rows = queries.shape[1]
+        weigh(own[half + i, 2 * rows :, :], (block(own, half + i), block(own, i)), full, out, i)
+
+
+def early_body(place, own, other, old, past, later, out, ko, kp):
+    half, rows, _ = later.shape
     even = parity_of(place) == 0
     live = plane_of(place) > 0
     out[half:] = later[...]
@@ -173,26 +174,22 @@
 
     for i in range(half):
         full = [mine(i + 1 + j) for j in range(half - 1)] + [theirs(i + j) for j in range(half)]
-        weigh(queries[i], (mine(half + i), mine(i)), full, out, i)
-
-
-def attend_late(place, queries, own, other):
-    blocks, rows, _ = queries.shape
-    half = blocks // 2
+        weigh(own[i, 2 * rows :, :], (mine(half + i), mine(i)), full, out, i)
+
+
+def attend_late(place, own, other):
+    half, rows = own.shape[0] // 2, own.shape[1] // 3
     out = jax.ShapeDtypeStruct((half, rows, HD), BF16)
     estimate = cost(4 * half * rows * WINDOW * 2 * HD, 4 << 20, half * rows * WINDOW)
-    return local(late_body, out, (), 1, 3, estimate)(place, queries, own, other)
-
-
-def attend_early(place, queries, own, other, old, past, later):
-    blocks, rows, _ = queries.shape
-    half = blocks // 2
+    return local(late_body, out, (), 1, 2, estimate)(place, own, other)
+
+
+def attend_early(place, own, other, old, past, later):
+    half, rows, _ = later.shape
     scratch = [pltpu.VMEM((half, rows, HD), BF16)] * 2
-    out = jax.ShapeDtypeStruct(queries.shape, BF16)
+    out = jax.ShapeDtypeStruct((2 * half, rows, HD), BF16)
     estimate = cost(4 * half * rows * WINDOW * 2 * HD, 4 << 20, half * rows * WINDOW)
-    return local(early_body, out, scratch, 1, 6, estimate)(
-        place, queries, own, other, old, past, later
-    )
+    return local(early_body, out, scratch, 1, 5, estimate)(place, own, other, old, past, later)
 
 
 def rows_of(step):
@@ -266,40 +263,76 @@
     return local(ends_body, (out, rates), scratch, 0, 9, estimate)(*sources, *partials, a_rate)
 
 
-def fold(rates, parts):
-    state = [parts[0][n * TILES : (n + 1) * TILES, :] for n in range(NS)]
-    through = parts[0][NS * TILES :, :]
-    for part in parts[1:]:
-        size = part[NS * TILES :, :]
-        for n in range(NS):
-            row = slice(n * TILES, (n + 1) * TILES)
-            state[n] = jnp.exp2(size * rates[row, :]) * state[n] + part[row, :]
-        through = through + size
-    return state, through
-
-
-def join_body(rates, *refs):
-    *parts, out = refs
-    state, through = fold(rates, parts)
+def fold(rates, state, through, part):
+    size = part[NS * TILES :, :]
+    out = []
+    for n in range(NS):
+        row = slice(n * TILES, (n + 1) * TILES)
+        out.append(jnp.exp2(size * rates[row, :]) * state[n] + part[row, :])
+    return out, through + size
+
+
+def nothing():
+    zero = jnp.zeros((TILES, LANES), F32)
+    return [zero] * NS, zero
+
+
+def keep(out, state, through):
     for n in range(NS):
         out[n * TILES : (n + 1) * TILES, :] = state[n]
     out[NS * TILES :, :] = through
 
 
-def join(rates, parts):
-    out = jax.ShapeDtypeStruct(parts[0].shape, F32)
-    estimate = cost(1 << 16, 1 << 18)
-    return local(join_body, out, arrays=1 + len(parts), estimate=estimate)(rates, *parts)
+def join_body(shift, bits, *refs):
+    place, rates, *rest = refs
+    maps, rest = rest[: 1 << bits], rest[1 << bits :]
+    before = rest[0] if len(rest) == 3 else None
+    whole_out, before_out = rest[-2:]
+    spot = (place[0] >> shift) & ((1 << bits) - 1)
+    state, through = nothing()
+    held_state, held_through = nothing()
+    for k in range(1 << bits):
+        here = spot == k
+        held_state = [jnp.where(here, now, old) for now, old in zip(state, held_state)]
+        held_through = jnp.where(here, through, held_through)
+        part = maps[0][...]
+        for distance in range(1, 1 << bits):
+            part = jnp.where((spot ^ k) == distance, maps[distance][...], part)
+        state, through = fold(rates, state, through, part)
+    if len(whole_out.shape) == 3:
+        for z in range(whole_out.shape[0]):
+            keep(whole_out.at[z], state, through)
+    else:
+        keep(whole_out, state, through)
+    if before is not None:
+        held_state, held_through = fold(rates, held_state, held_through, before)
+    keep(before_out, held_state, held_through)
+
+
+def join(place, rates, maps, before, shift, copies):
+    bits = len(maps).bit_length() - 1
+    one = jax.ShapeDtypeStruct(maps[0].shape, F32)
+    whole = jax.ShapeDtypeStruct((copies, *maps[0].shape), F32) if copies else one
+    given = [rates, *maps] + ([] if before is None else [before])
+    body = functools.partial(join_body, shift, bits)
+    estimate = cost(1 << 18, 1 << 19)
+    return local(body, (whole, one), (), 1, len(given), estimate)(place, *given)
 
 
 def final_body(
-    low, proj, bias, xin, p0, p1, p2, p3, held, e0, e1, gate, skip, out, wide, mix, steps, drive
+    place, low, proj, bias, xin, p0, p1, p2, p3, held, planes, before, gate, skip,
+    out, wide, mix, steps, drive,
 ):
     rows = p0.shape[1]
     load_steps(low, proj, bias, xin, steps, drive)
     spread((p0, p1, p2, p3), 2 * NS, wide)
     rates = [held[n * TILES : (n + 1) * TILES, :] for n in range(NS)]
-    state, _ = fold(held, (e0, e1))
+    state, through = nothing()
+    for z in range(planes.shape[0]):
+        earlier = z < plane_of(place)
+        later, _ = fold(held, state, through, planes[z])
+        state = [jnp.where(earlier, new, old) for new, old in zip(later, state)]
+    state, _ = fold(held, state, through, before)
 
     def step(t, state):
         size, push = steps[rows_of(t), :], drive[rows_of(t), :]
@@ -322,14 +355,14 @@
         out[:, col] = (mixed * (opened / (1.0 + jnp.exp(-opened)))).astype(BF16)
 
 
-def finish(sources, partials, rates, entering, gate, skip):
+def finish(place, sources, partials, rates, planes, before, gate, skip):
     rows, width = gate.shape
     out = jax.ShapeDtypeStruct(gate.shape, BF16)
     tall = pltpu.VMEM((rows * TILES, LANES), F32)
     scratch = [pltpu.VMEM((rows * 2 * NS, LANES), F32), tall, tall, tall]
     estimate = cost(9 * rows * width * NS, 8 * rows * width, rows * width * NS)
-    return local(final_body, out, scratch, 0, 13, estimate)(
-        *sources, *partials, rates, *entering, gate, skip.reshape(1, -1)
+    return local(final_body, out, scratch, 1, 13, estimate)(
+        place, *sources, *partials, rates, planes, before, gate, skip.reshape(1, -1)
     )
 
 
@@ -337,9 +370,9 @@
     return lax.all_to_all(x, "ctx", 0, 0, axis_index_groups=groups, tiled=True)
 
 
-def after(part, distance):
+def across(part, distance):
     count = lax.axis_size("ctx")
-    return lax.ppermute(part, "ctx", [(i, i + distance) for i in range(count - distance)])
+    return lax.ppermute(part, "ctx", [(i, i ^ distance) for i in range(count)])
 
 
 def shards(query, key, value, xin, gate_z, w_bc, dt_low, dt_proj, dt_bias, a_rate, skip):
@@ -352,7 +385,8 @@
     partner = [(i, i ^ 1) for i in range(ctx)]
     next_row = [(i, i + line) for i in range(ctx - line)]
 
-    own_kv = exchange(pack(key, value), along_y)
+    along_z = [[z * line + k for z in range(planes)] for k in range(line)]
+    own = exchange(pack(key, value, query), along_y)
     partial = project(xin, w_bc)
     partials = [partial] + [
         lax.ppermute(partial, "tp", [(i, (i + d) % tp) for i in range(tp)])
@@ -360,22 +394,19 @@
     ]
     sources = (dt_low, dt_proj, dt_bias.reshape(1, -1), xin)
     ends, rates = block_ends(sources, partials, a_rate)
-    queries = pack(query)
-    own_kv, queries = lax.optimization_barrier((own_kv, queries))
-    queries = exchange(queries, along_y)
-    old_kv = lax.ppermute(own_kv[side // 2 :], "ctx", next_row)
-    other_kv = lax.ppermute(own_kv, "ctx", partner)
+    whole, before = join(place, rates, [ends, across(ends, 1)], None, 0, 0)
+    maps = [whole] + [across(whole, 2 * d) for d in (1, 2, 3)]
+    whole, before = join(place, rates, maps, before, 1, 0)
+    whole, before = join(place, rates, [whole, across(whole, 8)], before, 3, planes)
+    old_kv = lax.ppermute(own[side // 2 :, : 2 * key.shape[0]], "ctx", next_row)
+    wholes = exchange(whole, along_z)
+    other = lax.ppermute(own, "ctx", partner)
     past_kv = lax.ppermute(old_kv, "ctx", partner)
-    ends = join(rates, [after(ends, 2), after(ends, 1)])
-    ends = join(rates, [after(ends, 6), after(ends, 4), after(ends, 2), ends])
-    ends = join(rates, [after(ends, 8), ends])
-    ends = join(rates, [after(ends, 48), after(ends, 32), after(ends, 16), ends])
-    entering = [after(ends, 64), ends]
-    later = attend_late(place, queries, own_kv, other_kv)
-    attended = attend_early(place, queries, own_kv, other_kv, old_kv, past_kv, later)
+    later = attend_late(place, own, other)
+    attended = attend_early(place, own, other, old_kv, past_kv, later)
     attended = exchange(attended, along_y)
     attended = unpack(attended)
-    mixed = finish(sources, partials, rates, entering, gate_z, skip)
+    mixed = finish(place, sources, partials, rates, wholes, before, gate_z, skip)
     return (attended, mixed)
 
 

time: 177 us -> 153 us (0.86)
  the two profiles are of different devices: /device:TPU:6 before, /device:TPU:1 now
where the time goes in v4:
time: 153 us; the launch traced here: 151 us
  starting transfers between devices  57.5 us (38%)
  blocking collectives  44.7 us (29%)
  Pallas kernels  31.6 us (21%)
  waiting for transfers between devices  13.6 us (9%)
  local copies, waits for them, and re-layouts  2.83 us (2%)
    all_to_all x1, blocking collectives, exchange(): return lax.all_to_all(x, 'ctx', 0, 0, axis_index_groups=groups, tiled=True)  44.7 us
    ppermute x5, starting transfers between devices, across(): return lax.ppermute(part, 'ctx', [(i, i ^ distance) for i in range(count)])  17 us
    all_to_all x2, starting transfers between devices, exchange(): return lax.all_to_all(x, 'ctx', 0, 0, axis_index_groups=groups, tiled=True)  13.2 us
    ppermute x3, starting transfers between devices, shards(): lax.ppermute(partial, 'tp', [(i, (i + d) % tp) for i in range(tp)])  10.5 us
    pallas_call x1, Pallas kernels, finish(): local(final_body, out, scratch, 1, 13, estimate)  10.2 us
    ppermute x5, waiting for transfers between devices, across(): return lax.ppermute(part, 'ctx', [(i, i ^ distance) for i in range(count)])  8.06 us
    pallas_call x1, Pallas kernels, attend_early(): local(early_body, out, scratch, 1, 5, estimate)  6.1 us
    ppermute x1, starting transfers between devices, shards(): other = lax.ppermute(own, 'ctx', partner)  6.05 us
  transfers between devices with their start and end apart: 13, of which 5 were waited for; matrix products, arithmetic and copies ran while one was open for 1% of the time, Pallas kernels for 18%

profile of v4, /device:TPU:1, one launch (start us, length us, event | category | flops | bytes accessed | tf_op | source)
XLA Modules:
  0.0 151.1 jit_solution(947504791366724656)
XLA Ops:
  0.6 2.8 %pack.1 = bf16[8,768,128]{2,1,0:T(8,128)(2,1)} custom-call(bf16[256,1024]{1,0:T(8,128)(2,1)} %refs_0_.1, bf16[256,1024]{1,0:T(8,128)(2,1)} %refs_1_.1, bf16[256,1024]{1,0:T(8,128)(2,1)} %refs_2_.1), custom_call_target="tpu_custom_call" | custom-call | bytes 3145728 | tf_op jit(solution)/shard_map/pack/pallas_call | solution.py:65
  3.5 44.7 %all_to_all.15.own = bf16[8,768,128]{2,1,0:T(8,128)(2,1)S(1)} all-to-all(bf16[8,768,128]{2,1,0:T(8,128)(2,1)} %pack.1), channel_id=1, replica_groups={{0,8,16,24,32,40,48,56},{4,12,20,28,36,44,52,60},{64,72,80,88,96,104,11..., dimensions={0} | all-to-all | bytes 3145728 | tf_op jit(solution)/shard_map/all_to_all | solution.py:370
  48.2 6.1 %collective-permute-start = (bf16[8,768,128]{2,1,0:T(8,128)(2,1)S(1)}, bf16[8,768,128]{2,1,0:T(8,128)(2,1)}, u32[]{:S(2)}, u32[]{:S(2)}) collective-permute-start(bf16[8,768,128]{2,1,0:T(8,128)(2,1)S(1)} %all_to_all.15.own), channel_id=1, source_target_pairs={{0,4},{4,0},{8,12},{12,8},{16,20},{20,16},{24,28},{28,24},{32,36},... | collective-permute-start | bytes 4718600 | tf_op jit(solution)/shard_map/ppermute | solution.py:403
  55.1 4.8 %collective-permute-start.1 = (bf16[4,512,128]{2,1,0:T(8,128)(2,1)}, bf16[4,512,128]{2,1,0:T(8,128)(2,1)}, u32[]{:S(2)}, u32[]{:S(2)}) collective-permute-start(bf16[4,512,128]{2,1,0:T(8,128)(2,1)} %slice.4), channel_id=1, source_target_pairs={{0,64},{4,68},{8,72},{12,76},{16,80},{20,84},{24,88},{28,92},{32,9... | collective-permute-start | bytes 1572872 | tf_op jit(solution)/shard_map/ppermute | solution.py:401
  60.4 3.1 %collective-permute-start.3 = (f32[32,256]{1,0:T(8,128)S(1)}, f32[32,256]{1,0:T(8,128)S(1)}, u32[]{:S(2)}, u32[]{:S(2)}) collective-permute-start(f32[32,256]{1,0:T(8,128)S(1)} %shard_map.125.p0), channel_id=1, source_target_pairs={{0,1},{1,2},{2,3},{3,0},{4,5},{5,6},{6,7},{7,4},{8,9},{9,10},{10,1... | collective-permute-start | bytes 98312 | tf_op jit(solution)/shard_map/ppermute | solution.py:392
  63.5 4.4 %collective-permute-start.4 = (f32[32,256]{1,0:T(8,128)S(1)}, f32[32,256]{1,0:T(8,128)S(1)}, u32[]{:S(2)}, u32[]{:S(2)}) collective-permute-start(f32[32,256]{1,0:T(8,128)S(1)} %shard_map.125.p0), channel_id=1, source_target_pairs={{0,2},{1,3},{2,0},{3,1},{4,6},{5,7},{6,4},{7,5},{8,10},{9,11},{10,... | collective-permute-start | bytes 98312 | tf_op jit(solution)/shard_map/ppermute | solution.py:392
  67.9 3.1 %collective-permute-start.5 = (f32[32,256]{1,0:T(8,128)S(1)}, f32[32,256]{1,0:T(8,128)S(1)}, u32[]{:S(2)}, u32[]{:S(2)}) collective-permute-start(f32[32,256]{1,0:T(8,128)S(1)} %shard_map.125.p0), channel_id=1, source_target_pairs={{0,3},{1,0},{2,1},{3,2},{4,7},{5,4},{6,5},{7,6},{8,11},{9,8},{10,9... | collective-permute-start | bytes 98312 | tf_op jit(solution)/shard_map/ppermute | solution.py:392
  71.0 1.6 %collective-permute-done.5.p3 = f32[32,256]{1,0:T(8,128)S(1)} collective-permute-done((f32[32,256]{1,0:T(8,128)S(1)}, f32[32,256]{1,0:T(8,128)S(1)}, u32[]{:S(2)}, u32[]{:S(2)}) %collective-permute-start.5) | collective-permute-done | bytes 32800 | tf_op jit(solution)/shard_map/ppermute | solution.py:392
  72.6 5.1 %shard_map.126 = (f32[136,128]{1,0:T(8,128)S(1)}, f32[128,128]{1,0:T(8,128)S(1)}) custom-call(bf16[256,256]{1,0:T(8,128)(2,1)S(1)} %copy-done.3, bf16[256,1024]{1,0:T(8,128)(2,1)S(1)} %copy-done.1, f32[1,1024]{1,0:T(1,128)S(1)} %bitcast.3, bf16[256,1024]{1,0:T(8,128)(2,1)S(1)} %copy-done, f32[32,256]{1,0:T(8,128)S(1)} %shard_map.125.p0, ...), custom_call_target="tpu_custom_call" | custom-call | flops 25165824 | bytes 1048576 | tf_op jit(solution)/shard_map/pallas_call | solution.py:263
  77.7 3.9 %collective-permute-start.6 = (f32[136,128]{1,0:T(8,128)S(1)}, f32[136,128]{1,0:T(8,128)S(1)}, u32[]{:S(2)}, u32[]{:S(2)}) collective-permute-start(f32[136,128]{1,0:T(8,128)S(1)} %get-tuple-element.11.refs_2_), channel_id=1, source_target_pairs={{0,4},{4,0},{8,12},{12,8},{16,20},{20,16},{24,28},{28,24},{32,36},... | collective-permute-start | bytes 208904 | tf_op jit(solution)/shard_map/ppermute | solution.py:375
  82.5 2.2 %collective-permute-start.7 = (f32[136,128]{1,0:T(8,128)S(1)}, f32[136,128]{1,0:T(8,128)S(1)}, u32[]{:S(2)}, u32[]{:S(2)}) collective-permute-start(f32[136,128]{1,0:T(8,128)S(1)} %get-tuple-element.12.refs_2_), channel_id=1, source_target_pairs={{0,8},{4,12},{8,0},{12,4},{16,24},{20,28},{24,16},{28,20},{32,40},... | collective-permute-start | bytes 208904 | tf_op jit(solution)/shard_map/ppermute | solution.py:375
  84.7 1.9 %collective-permute-start.8 = (f32[136,128]{1,0:T(8,128)S(1)}, f32[136,128]{1,0:T(8,128)S(1)}, u32[]{:S(2)}, u32[]{:S(2)}) collective-permute-start(f32[136,128]{1,0:T(8,128)S(1)} %get-tuple-element.12.refs_2_), channel_id=1, source_target_pairs={{0,16},{4,20},{8,24},{12,28},{16,0},{20,4},{24,8},{28,12},{32,48},... | collective-permute-start | bytes 208904 | tf_op jit(solution)/shard_map/ppermute | solution.py:375
  86.7 5.2 %collective-permute-start.9 = (f32[136,128]{1,0:T(8,128)S(1)}, f32[136,128]{1,0:T(8,128)S(1)}, u32[]{:S(2)}, u32[]{:S(2)}) collective-permute-start(f32[136,128]{1,0:T(8,128)S(1)} %get-tuple-element.12.refs_2_), channel_id=1, source_target_pairs={{0,24},{4,28},{8,16},{12,20},{16,8},{20,12},{24,0},{28,4},{32,56},... | collective-permute-start | bytes 208904 | tf_op jit(solution)/shard_map/ppermute | solution.py:375
  91.9 1.7 %collective-permute-done.9.refs_5_ = f32[136,128]{1,0:T(8,128)S(1)} collective-permute-done((f32[136,128]{1,0:T(8,128)S(1)}, f32[136,128]{1,0:T(8,128)S(1)}, u32[]{:S(2)}, u32[]{:S(2)}) %collective-permute-start.9) | collective-permute-done | bytes 69664 | tf_op jit(solution)/shard_map/ppermute | solution.py:375
  93.6 3.8 %collective-permute-start.10 = (f32[136,128]{1,0:T(8,128)S(1)}, f32[136,128]{1,0:T(8,128)S(1)}, u32[]{:S(2)}, u32[]{:S(2)}) collective-permute-start(f32[136,128]{1,0:T(8,128)S(1)} %get-tuple-element.14.refs_2_), channel_id=1, source_target_pairs={{0,32},{4,36},{8,40},{12,44},{16,48},{20,52},{24,56},{28,60},{32,0... | collective-permute-start | bytes 208904 | tf_op jit(solution)/shard_map/ppermute | solution.py:375
  97.4 5.5 %collective-permute-done.10.refs_3_ = f32[136,128]{1,0:T(8,128)S(1)} collective-permute-done((f32[136,128]{1,0:T(8,128)S(1)}, f32[136,128]{1,0:T(8,128)S(1)}, u32[]{:S(2)}, u32[]{:S(2)}) %collective-permute-start.10) | collective-permute-done | bytes 69664 | tf_op jit(solution)/shard_map/ppermute | solution.py:375
  103.8 8.3 %all-to-all-start.2 = ((f32[8,136,128]{2,1,0:T(8,128)}), f32[8,136,128]{2,1,0:T(8,128)S(1)}, u32[]{:S(2)}, u32[]{:S(2)}) async-start(f32[8,136,128]{2,1,0:T(8,128)} %get-tuple-element.16), calls=%async_computation.2 | async-start | bytes 1114112 | tf_op jit(solution)/shard_map/all_to_all | solution.py:370
  112.1 5.9 %collective-permute-start.2 = (bf16[4,512,128]{2,1,0:T(8,128)(2,1)}, bf16[4,512,128]{2,1,0:T(8,128)(2,1)S(1)}, u32[]{:S(2)}, u32[]{:S(2)}) collective-permute-start(bf16[4,512,128]{2,1,0:T(8,128)(2,1)} %collective-permute-done.1.old), channel_id=1, source_target_pairs={{0,4},{4,0},{8,12},{12,8},{16,20},{20,16},{24,28},{28,24},{32,36},... | collective-permute-start | bytes 1572872 | tf_op jit(solution)/shard_map/ppermute | solution.py:404
  118.1 5.1 %shard_map.122.later = bf16[4,256,128]{2,1,0:T(8,128)(2,1)S(1)} custom-call(s32[1]{0:T(128)} %bitcast.place.refs_0_, bf16[8,768,128]{2,1,0:T(8,128)(2,1)S(1)} %all_to_all.15.own, bf16[8,768,128]{2,1,0:T(8,128)(2,1)} %collective-permute-done.other), custom_call_target="tpu_custom_call" | custom-call | flops 2147483648 | bytes 4194304 | tf_op jit(solution)/shard_map/pallas_call | solution.py:184
  123.2 6.1 %shard_map.123 = bf16[8,256,128]{2,1,0:T(8,128)(2,1)} custom-call(s32[1]{0:T(128)} %bitcast.place.refs_0_, bf16[8,768,128]{2,1,0:T(8,128)(2,1)S(1)} %all_to_all.15.own, bf16[8,768,128]{2,1,0:T(8,128)(2,1)} %collective-permute-done.other, bf16[4,512,128]{2,1,0:T(8,128)(2,1)} %collective-permute-done.1.old, ...), custom_call_target="tpu_custom_call" | custom-call | flops 2147483648 | bytes 4194304 | tf_op jit(solution)/shard_map/pallas_call | solution.py:192
  129.3 4.9 %all-to-all-start.1 = ((bf16[8,256,128]{2,1,0:T(8,128)(2,1)}), bf16[8,256,128]{2,1,0:T(8,128)(2,1)S(1)}, u32[]{:S(2)}, u32[]{:S(2)}) async-start(bf16[8,256,128]{2,1,0:T(8,128)(2,1)} %shard_map.123), calls=%async_computation.1 | async-start | bytes 1048576 | tf_op jit(solution)/shard_map/all_to_all | solution.py:370
  134.2 1.0 copy-done.2
  136.0 10.2 %shard_map.130 = bf16[256,1024]{1,0:T(8,128)(2,1)} custom-call(s32[1]{0:T(128)} %bitcast.place.refs_0_, bf16[256,256]{1,0:T(8,128)(2,1)S(1)} %copy-done.3, bf16[256,1024]{1,0:T(8,128)(2,1)S(1)} %copy-done.1, f32[1,1024]{1,0:T(1,128)S(1)} %bitcast.4, bf16[256,1024]{1,0:T(8,128)(2,1)S(1)} %copy-done, f32[32,256]{1,0:T(8,128)S(1)} %shard_map.125.p0, ...), custom_call_target="tpu_custom_call" | custom-call | flops 37748736 | bytes 2097152 | tf_op jit(solution)/shard_map/pallas_call | solution.py:364
  146.2 4.0 %all-to-all-done.1.blocks = bf16[8,256,128]{2,1,0:T(8,128)(2,1)S(1)} async-done(((bf16[8,256,128]{2,1,0:T(8,128)(2,1)}), bf16[8,256,128]{2,1,0:T(8,128)(2,1)S(1)}, u32[]{:S(2)}, u32[]{:S(2)}) %all-to-all-start.1) | async-done | bytes 524320 | tf_op jit(solution)/shard_map/all_to_all | solution.py:370
  (35 shorter events, 5.0 us)
Async XLA Ops:
  3.5 56.4 %copy-start.9 = (bf16[1024,32]{0,1:T(8,128)(2,1)S(1)}, bf16[1024,32]{0,1:T(8,128)(2,1)}, u32[]{:S(2)}) copy-start(bf16[1024,32]{0,1:T(8,128)(2,1)} %param.16) | copy-start | bytes 196612
  3.5 56.6 %copy-start = (bf16[256,1024]{1,0:T(8,128)(2,1)S(1)}, bf16[256,1024]{1,0:T(8,128)(2,1)}, u32[]{:S(2)}) copy-start(bf16[256,1024]{1,0:T(8,128)(2,1)} %xin.5) | copy-start | bytes 1572868
  48.2 24.4 %copy-start.1 = (bf16[256,1024]{1,0:T(8,128)(2,1)S(1)}, bf16[256,1024]{1,0:T(8,128)(2,1)}, u32[]{:S(2)}) copy-start(bf16[256,1024]{1,0:T(8,128)(2,1)} %proj.3) | copy-start | bytes 1572868
  48.2 24.4 %copy-start.3 = (bf16[256,256]{1,0:T(8,128)(2,1)S(1)}, bf16[256,256]{1,0:T(8,128)(2,1)}, u32[]{:S(2)}) copy-start(bf16[256,256]{1,0:T(8,128)(2,1)} %low.3) | copy-start | bytes 393220
  48.2 24.4 %copy-start.4 = (f32[16,1024]{1,0:T(8,128)S(1)}, f32[16,1024]{1,0:T(8,128)}, u32[]{:S(2)}) copy-start(f32[16,1024]{1,0:T(8,128)} %a_rate.1) | copy-start | bytes 196612
  48.2 24.4 %copy-start.7 = (f32[1024]{0:T(1024)S(1)}, f32[1024]{0:T(1024)}, u32[]{:S(2)}) copy-start(f32[1024]{0:T(1024)} %param.19) | copy-start | bytes 12292
  48.2 69.9 %collective-permute-start = (bf16[8,768,128]{2,1,0:T(8,128)(2,1)S(1)}, bf16[8,768,128]{2,1,0:T(8,128)(2,1)}, u32[]{:S(2)}, u32[]{:S(2)}) collective-permute-start(bf16[8,768,128]{2,1,0:T(8,128)(2,1)S(1)} %all_to_all.15.own), channel_id=1, source_target_pairs={{0,4},{4,0},{8,12},{12,8},{16,20},{20,16},{24,28},{28,24},{32,36},... | collective-permute-start | bytes 4718600 | tf_op jit(solution)/shard_map/ppermute | solution.py:403
  55.1 57.1 %collective-permute-start.1 = (bf16[4,512,128]{2,1,0:T(8,128)(2,1)}, bf16[4,512,128]{2,1,0:T(8,128)(2,1)}, u32[]{:S(2)}, u32[]{:S(2)}) collective-permute-start(bf16[4,512,128]{2,1,0:T(8,128)(2,1)} %slice.4), channel_id=1, source_target_pairs={{0,64},{4,68},{8,72},{12,76},{16,80},{20,84},{24,88},{28,92},{32,9... | collective-permute-start | bytes 1572872 | tf_op jit(solution)/shard_map/ppermute | solution.py:401
  60.4 10.6 %collective-permute-start.3 = (f32[32,256]{1,0:T(8,128)S(1)}, f32[32,256]{1,0:T(8,128)S(1)}, u32[]{:S(2)}, u32[]{:S(2)}) collective-permute-start(f32[32,256]{1,0:T(8,128)S(1)} %shard_map.125.p0), channel_id=1, source_target_pairs={{0,1},{1,2},{2,3},{3,0},{4,5},{5,6},{6,7},{7,4},{8,9},{9,10},{10,1... | collective-permute-start | bytes 98312 | tf_op jit(solution)/shard_map/ppermute | solution.py:392
  63.5 7.5 %collective-permute-start.4 = (f32[32,256]{1,0:T(8,128)S(1)}, f32[32,256]{1,0:T(8,128)S(1)}, u32[]{:S(2)}, u32[]{:S(2)}) collective-permute-start(f32[32,256]{1,0:T(8,128)S(1)} %shard_map.125.p0), channel_id=1, source_target_pairs={{0,2},{1,3},{2,0},{3,1},{4,6},{5,7},{6,4},{7,5},{8,10},{9,11},{10,... | collective-permute-start | bytes 98312 | tf_op jit(solution)/shard_map/ppermute | solution.py:392
  67.9 4.7 %collective-permute-start.5 = (f32[32,256]{1,0:T(8,128)S(1)}, f32[32,256]{1,0:T(8,128)S(1)}, u32[]{:S(2)}, u32[]{:S(2)}) collective-permute-start(f32[32,256]{1,0:T(8,128)S(1)} %shard_map.125.p0), channel_id=1, source_target_pairs={{0,3},{1,0},{2,1},{3,2},{4,7},{5,4},{6,5},{7,6},{8,11},{9,8},{10,9... | collective-permute-start | bytes 98312 | tf_op jit(solution)/shard_map/ppermute | solution.py:392
  72.5 5.1 %copy-start.5 = (f32[32,256]{1,0:T(8,128)}, f32[32,256]{1,0:T(8,128)S(1)}, u32[]{:S(2)}) copy-start(f32[32,256]{1,0:T(8,128)S(1)} %collective-permute-done.5.p3) | copy-start | bytes 98308
  77.7 4.8 %collective-permute-start.6 = (f32[136,128]{1,0:T(8,128)S(1)}, f32[136,128]{1,0:T(8,128)S(1)}, u32[]{:S(2)}, u32[]{:S(2)}) collective-permute-start(f32[136,128]{1,0:T(8,128)S(1)} %get-tuple-element.11.refs_2_), channel_id=1, source_target_pairs={{0,4},{4,0},{8,12},{12,8},{16,20},{20,16},{24,28},{28,24},{32,36},... | collective-permute-start | bytes 208904 | tf_op jit(solution)/shard_map/ppermute | solution.py:375
  82.5 9.3 %collective-permute-start.7 = (f32[136,128]{1,0:T(8,128)S(1)}, f32[136,128]{1,0:T(8,128)S(1)}, u32[]{:S(2)}, u32[]{:S(2)}) collective-permute-start(f32[136,128]{1,0:T(8,128)S(1)} %get-tuple-element.12.refs_2_), channel_id=1, source_target_pairs={{0,8},{4,12},{8,0},{12,4},{16,24},{20,28},{24,16},{28,20},{32,40},... | collective-permute-start | bytes 208904 | tf_op jit(solution)/shard_map/ppermute | solution.py:375
  84.7 7.1 %collective-permute-start.8 = (f32[136,128]{1,0:T(8,128)S(1)}, f32[136,128]{1,0:T(8,128)S(1)}, u32[]{:S(2)}, u32[]{:S(2)}) collective-permute-start(f32[136,128]{1,0:T(8,128)S(1)} %get-tuple-element.12.refs_2_), channel_id=1, source_target_pairs={{0,16},{4,20},{8,24},{12,28},{16,0},{20,4},{24,8},{28,12},{32,48},... | collective-permute-start | bytes 208904 | tf_op jit(solution)/shard_map/ppermute | solution.py:375
  86.7 6.9 %collective-permute-start.9 = (f32[136,128]{1,0:T(8,128)S(1)}, f32[136,128]{1,0:T(8,128)S(1)}, u32[]{:S(2)}, u32[]{:S(2)}) collective-permute-start(f32[136,128]{1,0:T(8,128)S(1)} %get-tuple-element.12.refs_2_), channel_id=1, source_target_pairs={{0,24},{4,28},{8,16},{12,20},{16,8},{20,12},{24,0},{28,4},{32,56},... | collective-permute-start | bytes 208904 | tf_op jit(solution)/shard_map/ppermute | solution.py:375
  93.6 9.3 %collective-permute-start.10 = (f32[136,128]{1,0:T(8,128)S(1)}, f32[136,128]{1,0:T(8,128)S(1)}, u32[]{:S(2)}, u32[]{:S(2)}) collective-permute-start(f32[136,128]{1,0:T(8,128)S(1)} %get-tuple-element.14.refs_2_), channel_id=1, source_target_pairs={{0,32},{4,36},{8,40},{12,44},{16,48},{20,52},{24,56},{28,60},{32,0... | collective-permute-start | bytes 208904 | tf_op jit(solution)/shard_map/ppermute | solution.py:375
  103.8 25.5 %all-to-all-start.2 = ((f32[8,136,128]{2,1,0:T(8,128)}), f32[8,136,128]{2,1,0:T(8,128)S(1)}, u32[]{:S(2)}, u32[]{:S(2)}) async-start(f32[8,136,128]{2,1,0:T(8,128)} %get-tuple-element.16), calls=%async_computation.2 | async-start | bytes 1114112 | tf_op jit(solution)/shard_map/all_to_all | solution.py:370
  112.1 11.0 %collective-permute-start.2 = (bf16[4,512,128]{2,1,0:T(8,128)(2,1)}, bf16[4,512,128]{2,1,0:T(8,128)(2,1)S(1)}, u32[]{:S(2)}, u32[]{:S(2)}) collective-permute-start(bf16[4,512,128]{2,1,0:T(8,128)(2,1)} %collective-permute-done.1.old), channel_id=1, source_target_pairs={{0,4},{4,0},{8,12},{12,8},{16,20},{20,16},{24,28},{28,24},{32,36},... | collective-permute-start | bytes 1572872 | tf_op jit(solution)/shard_map/ppermute | solution.py:404
  123.2 11.0 %copy-start.8 = (f32[1024]{0:T(1024)S(1)}, f32[1024]{0:T(1024)}, u32[]{:S(2)}) copy-start(f32[1024]{0:T(1024)} %param.21) | copy-start | bytes 12292
  129.3 20.9 %all-to-all-start.1 = ((bf16[8,256,128]{2,1,0:T(8,128)(2,1)}), bf16[8,256,128]{2,1,0:T(8,128)(2,1)S(1)}, u32[]{:S(2)}, u32[]{:S(2)}) async-start(bf16[8,256,128]{2,1,0:T(8,128)(2,1)} %shard_map.123), calls=%async_computation.1 | async-start | bytes 1048576 | tf_op jit(solution)/shard_map/all_to_all | solution.py:370
  134.2 1.0 copy-start.2
  135.2 0.8 copy-start.6

commit v5 on v4

--- a/solution.py
+++ b/solution.py
@@ -11,6 +11,7 @@
 HD = 128
 WINDOW = 2048
 NS = 16
+HALF = NS // 2
 LANES = 128
 TILES = 8
 LOG2E = 1.4426950408889634
@@ -24,7 +25,7 @@
     return pl.CostEstimate(flops=flops, bytes_accessed=moved, transcendentals=exps)
 
 
-def local(body, outs, scratch=(), scalars=0, arrays=1, estimate=None, limit=48 << 20):
+def local(body, outs, scratch=(), scalars=0, arrays=1, estimate=None, limit=20 << 20):
     return pl.pallas_call(
         body,
         out_shape=outs,
@@ -113,7 +114,7 @@
     out[i] = (total[:, 0:HD] / total[:, HD : 2 * HD]).astype(BF16)
 
 
-def late_body(place, own, other, out):
+def late_body(place, queries, own, other, out):
     half = out.shape[0]
     rows = out.shape[1]
     parity = parity_of(place)
@@ -125,10 +126,10 @@
     for i in range(half):
         full = [block(own, i + 1 + j) for j in range(half - 1)]
         full += [block(other, i + parity + j) for j in range(half)]
-        weigh(own[half + i, 2 * rows :, :], (block(own, half + i), block(own, i)), full, out, i)
-
-
-def early_body(place, own, other, old, past, later, out, ko, kp):
+        weigh(queries[half + i], (block(own, half + i), block(own, i)), full, out, i)
+
+
+def early_body(place, queries, own, other, old, past, later, out, ko, kp):
     half, rows, _ = later.shape
     even = parity_of(place) == 0
     live = plane_of(place) > 0
@@ -174,22 +175,24 @@
 
     for i in range(half):
         full = [mine(i + 1 + j) for j in range(half - 1)] + [theirs(i + j) for j in range(half)]
-        weigh(own[i, 2 * rows :, :], (mine(half + i), mine(i)), full, out, i)
-
-
-def attend_late(place, own, other):
-    half, rows = own.shape[0] // 2, own.shape[1] // 3
+        weigh(queries[i], (mine(half + i), mine(i)), full, out, i)
+
+
+def attend_late(place, queries, own, other):
+    half, rows = queries.shape[0] // 2, queries.shape[1]
     out = jax.ShapeDtypeStruct((half, rows, HD), BF16)
     estimate = cost(4 * half * rows * WINDOW * 2 * HD, 4 << 20, half * rows * WINDOW)
-    return local(late_body, out, (), 1, 2, estimate)(place, own, other)
-
-
-def attend_early(place, own, other, old, past, later):
+    return local(late_body, out, (), 1, 3, estimate)(place, queries, own, other)
+
+
+def attend_early(place, queries, own, other, old, past, later):
     half, rows, _ = later.shape
     scratch = [pltpu.VMEM((half, rows, HD), BF16)] * 2
     out = jax.ShapeDtypeStruct((2 * half, rows, HD), BF16)
     estimate = cost(4 * half * rows * WINDOW * 2 * HD, 4 << 20, half * rows * WINDOW)
-    return local(early_body, out, scratch, 1, 5, estimate)(place, own, other, old, past, later)
+    return local(early_body, out, scratch, 1, 6, estimate)(
+        place, queries, own, other, old, past, later
+    )
 
 
 def rows_of(step):
@@ -300,8 +303,13 @@
             part = jnp.where((spot ^ k) == distance, maps[distance][...], part)
         state, through = fold(rates, state, through, part)
     if len(whole_out.shape) == 3:
+        even = parity_of(place) == 0
+        for n in range(HALF):
+            mine = jnp.where(even, state[n], state[n + HALF])
+            for z in range(whole_out.shape[0]):
+                whole_out[z, n * TILES : (n + 1) * TILES, :] = mine
         for z in range(whole_out.shape[0]):
-            keep(whole_out.at[z], state, through)
+            whole_out[z, HALF * TILES :, :] = through
     else:
         keep(whole_out, state, through)
     if before is not None:
@@ -312,26 +320,42 @@
 def join(place, rates, maps, before, shift, copies):
     bits = len(maps).bit_length() - 1
     one = jax.ShapeDtypeStruct(maps[0].shape, F32)
-    whole = jax.ShapeDtypeStruct((copies, *maps[0].shape), F32) if copies else one
+    halved = ((HALF + 1) * TILES, LANES)
+    whole = jax.ShapeDtypeStruct((copies, *halved), F32) if copies else one
     given = [rates, *maps] + ([] if before is None else [before])
     body = functools.partial(join_body, shift, bits)
     estimate = cost(1 << 18, 1 << 19)
     return local(body, (whole, one), (), 1, len(given), estimate)(place, *given)
 
 
+def planes_body(place, rates, planes, out):
+    half = rates[pl.ds(pl.multiple_of(parity_of(place) * HALF * TILES, TILES), HALF * TILES), :]
+    state = jnp.zeros((HALF * TILES, LANES), F32)
+    for z in range(planes.shape[0]):
+        size = jnp.concatenate([planes[z, HALF * TILES :, :]] * HALF, axis=0)
+        later = jnp.exp2(size * half) * state + planes[z, : HALF * TILES, :]
+        state = jnp.where(z < plane_of(place), later, state)
+    out[...] = state
+
+
+def join_planes(place, rates, planes):
+    out = jax.ShapeDtypeStruct((HALF * TILES, LANES), F32)
+    return local(planes_body, out, (), 1, 2, cost(1 << 18, 1 << 19))(place, rates, planes)
+
+
 def final_body(
-    place, low, proj, bias, xin, p0, p1, p2, p3, held, planes, before, gate, skip,
+    place, low, proj, bias, xin, p0, p1, p2, p3, held, mine, theirs, before, gate, skip,
     out, wide, mix, steps, drive,
 ):
     rows = p0.shape[1]
     load_steps(low, proj, bias, xin, steps, drive)
     spread((p0, p1, p2, p3), 2 * NS, wide)
     rates = [held[n * TILES : (n + 1) * TILES, :] for n in range(NS)]
-    state, through = nothing()
-    for z in range(planes.shape[0]):
-        earlier = z < plane_of(place)
-        later, _ = fold(held, state, through, planes[z])
-        state = [jnp.where(earlier, new, old) for new, old in zip(later, state)]
+    even = parity_of(place) == 0
+    rows_half = [slice(n * TILES, (n + 1) * TILES) for n in range(HALF)]
+    state = [jnp.where(even, mine[row, :], theirs[row, :]) for row in rows_half]
+    state += [jnp.where(even, theirs[row, :], mine[row, :]) for row in rows_half]
+    _, through = nothing()
     state, _ = fold(held, state, through, before)
 
     def step(t, state):
@@ -355,14 +379,14 @@
         out[:, col] = (mixed * (opened / (1.0 + jnp.exp(-opened)))).astype(BF16)
 
 
-def finish(place, sources, partials, rates, planes, before, gate, skip):
+def finish(place, sources, partials, rates, halves, before, gate, skip):
     rows, width = gate.shape
     out = jax.ShapeDtypeStruct(gate.shape, BF16)
     tall = pltpu.VMEM((rows * TILES, LANES), F32)
     scratch = [pltpu.VMEM((rows * 2 * NS, LANES), F32), tall, tall, tall]
     estimate = cost(9 * rows * width * NS, 8 * rows * width, rows * width * NS)
-    return local(final_body, out, scratch, 1, 13, estimate)(
-        place, *sources, *partials, rates, planes, before, gate, skip.reshape(1, -1)
+    return local(final_body, out, scratch, 1, 14, estimate)(
+        place, *sources, *partials, rates, *halves, before, gate, skip.reshape(1, -1)
     )
 
 
@@ -386,7 +410,10 @@
     next_row = [(i, i + line) for i in range(ctx - line)]
 
     along_z = [[z * line + k for z in range(planes)] for k in range(line)]
-    own = exchange(pack(key, value, query), along_y)
+    own = exchange(pack(key, value), along_y)
+    queries = pack(query)
+    own, queries = lax.optimization_barrier((own, queries))
+    queries = exchange(queries, along_y)
     partial = project(xin, w_bc)
     partials = [partial] + [
         lax.ppermute(partial, "tp", [(i, (i + d) % tp) for i in range(tp)])
@@ -398,15 +425,17 @@
     maps = [whole] + [across(whole, 2 * d) for d in (1, 2, 3)]
     whole, before = join(place, rates, maps, before, 1, 0)
     whole, before = join(place, rates, [whole, across(whole, 8)], before, 3, planes)
-    old_kv = lax.ppermute(own[side // 2 :, : 2 * key.shape[0]], "ctx", next_row)
+    old_kv = lax.ppermute(own[side // 2 :], "ctx", next_row)
     wholes = exchange(whole, along_z)
     other = lax.ppermute(own, "ctx", partner)
+    mine = join_planes(place, rates, wholes)
+    theirs = across(mine, 1)
     past_kv = lax.ppermute(old_kv, "ctx", partner)
-    later = attend_late(place, own, other)
-    attended = attend_early(place, own, other, old_kv, past_kv, later)
+    later = attend_late(place, queries, own, other)
+    attended = attend_early(place, queries, own, other, old_kv, past_kv, later)
     attended = exchange(attended, along_y)
     attended = unpack(attended)
-    mixed = finish(place, sources, partials, rates, wholes, before, gate_z, skip)
+    mixed = finish(place, sources, partials, rates, (mine, theirs), before, gate_z, skip)
     return (attended, mixed)
 
 

time: 153 us -> 144 us (0.941)
  blocking collectives: 44.7 us -> 0 us
  waiting for transfers between devices: 13.6 us -> 37.7 us
  starting transfers between devices: 57.5 us -> 71.1 us
    all_to_all x1 -> x0, blocking collectives: 44.7 us -> none  [exchange(): return lax.all_to_all(x, 'ctx', 0, 0, axis_index_groups=groups, tiled=True)]
    all_to_all x2 -> x4, waiting for transfers between devices: 4 us -> 25.7 us  [exchange(): return lax.all_to_all(x, 'ctx', 0, 0, axis_index_groups=groups, tiled=True)]
    all_to_all x2 -> x4, starting transfers between devices: 13.2 us -> 26.8 us  [exchange(): return lax.all_to_all(x, 'ctx', 0, 0, axis_index_groups=groups, tiled=True)]
    ppermute x5 -> x6, starting transfers between devices: 17 us -> 22.8 us  [across(): return lax.ppermute(part, 'ctx', [(i, i ^ distance) for i in range(count)])]
    ppermute x1, starting transfers between devices: 5.92 us -> 1.92 us  [shards(): past_kv = lax.ppermute(old_kv, 'ctx', partner)]
    ppermute x5 -> x6, waiting for transfers between devices: 8.06 us -> 10.5 us  [across(): return lax.ppermute(part, 'ctx', [(i, i ^ distance) for i in range(count)])]
    ppermute x1, starting transfers between devices: 6.05 us -> 4.3 us  [shards(): other = lax.ppermute(own, 'ctx', partner)]
    pallas_call x3 -> x4, Pallas kernels: 21.4 us -> 19.7 us  [the longest x1 10.2 us: finish(): local(final_body, out, scratch, 1, 14, estimate)]
  transfers between devices with their start and end apart: 13 -> 16, of which waited for: 5 -> 7; matrix products, arithmetic and copies ran while one was open for 1% -> 1% of each run, Pallas kernels for 18% -> 20%
where the time goes in v5:
time: 144 us; the launch traced here: 143 us
  starting transfers between devices  71.1 us (49%)
  waiting for transfers between devices  37.7 us (26%)
  Pallas kernels  31.3 us (22%)
  local copies, waits for them, and re-layouts  1.7 us (1%)
    all_to_all x4, starting transfers between devices, exchange(): return lax.all_to_all(x, 'ctx', 0, 0, axis_index_groups=groups, tiled=True)  26.8 us
    all_to_all x4, waiting for transfers between devices, exchange(): return lax.all_to_all(x, 'ctx', 0, 0, axis_index_groups=groups, tiled=True)  25.7 us
    ppermute x6, starting transfers between devices, across(): return lax.ppermute(part, 'ctx', [(i, i ^ distance) for i in range(count)])  22.8 us
    ppermute x3, starting transfers between devices, shards(): lax.ppermute(partial, 'tp', [(i, (i + d) % tp) for i in range(tp)])  10.5 us
    ppermute x6, waiting for transfers between devices, across(): return lax.ppermute(part, 'ctx', [(i, i ^ distance) for i in range(count)])  10.5 us
    pallas_call x1, Pallas kernels, finish(): local(final_body, out, scratch, 1, 14, estimate)  10.2 us
    pallas_call x1, Pallas kernels, attend_early(): local(early_body, out, scratch, 1, 6, estimate)  5.77 us
    pallas_call x1, Pallas kernels, block_ends(): local(ends_body, (out, rates), scratch, 0, 9, estimate)  5.11 us
  transfers between devices with their start and end apart: 16, of which 7 were waited for; matrix products, arithmetic and copies ran while one was open for 1% of the time, Pallas kernels for 20%

profile of v5, /device:TPU:1, one launch (start us, length us, event | category | flops | bytes accessed | tf_op | source)
XLA Modules:
  0.0 142.9 jit_solution(6991602134619695466)
XLA Ops:
  0.6 2.4 %pack.2 = bf16[8,512,128]{2,1,0:T(8,128)(2,1)} custom-call(bf16[256,1024]{1,0:T(8,128)(2,1)} %refs_0_.2, bf16[256,1024]{1,0:T(8,128)(2,1)} %refs_1_.1), custom_call_target="tpu_custom_call" | custom-call | bytes 2097152 | tf_op jit(solution)/shard_map/pack/pallas_call | solution.py:66
  3.0 7.7 %all-to-all-start = ((bf16[8,512,128]{2,1,0:T(8,128)(2,1)}), bf16[8,512,128]{2,1,0:T(8,128)(2,1)S(1)}, u32[]{:S(2)}, u32[]{:S(2)}) async-start(bf16[8,512,128]{2,1,0:T(8,128)(2,1)} %pack.2), calls=%async_computation | async-start | bytes 2097152 | tf_op jit(solution)/shard_map/all_to_all | solution.py:394
  10.7 1.9 %pack.3 = bf16[8,256,128]{2,1,0:T(8,128)(2,1)} custom-call(bf16[256,1024]{1,0:T(8,128)(2,1)} %refs_0_.3), custom_call_target="tpu_custom_call" | custom-call | bytes 1048576 | tf_op jit(solution)/shard_map/pack/pallas_call | solution.py:66
  12.6 25.3 %all-to-all-done.own = bf16[8,512,128]{2,1,0:T(8,128)(2,1)S(1)} async-done(((bf16[8,512,128]{2,1,0:T(8,128)(2,1)}), bf16[8,512,128]{2,1,0:T(8,128)(2,1)S(1)}, u32[]{:S(2)}, u32[]{:S(2)}) %all-to-all-start) | async-done | bytes 1048608 | tf_op jit(solution)/shard_map/all_to_all | solution.py:394
  38.0 4.3 %collective-permute-start = (bf16[8,512,128]{2,1,0:T(8,128)(2,1)S(1)}, bf16[8,512,128]{2,1,0:T(8,128)(2,1)S(1)}, u32[]{:S(2)}, u32[]{:S(2)}) collective-permute-start(bf16[8,512,128]{2,1,0:T(8,128)(2,1)S(1)} %all-to-all-done.own), channel_id=1, source_target_pairs={{0,4},{4,0},{8,12},{12,8},{16,20},{20,16},{24,28},{28,24},{32,36},... | collective-permute-start | bytes 3145736 | tf_op jit(solution)/shard_map/ppermute | solution.py:430
  42.3 3.5 %all-to-all-start.1 = ((bf16[8,256,128]{2,1,0:T(8,128)(2,1)}), bf16[8,256,128]{2,1,0:T(8,128)(2,1)S(1)}, u32[]{:S(2)}, u32[]{:S(2)}) async-start(bf16[8,256,128]{2,1,0:T(8,128)(2,1)} %pack.3), calls=%async_computation.1 | async-start | bytes 1048576 | tf_op jit(solution)/shard_map/all_to_all | solution.py:394
  46.6 4.8 %collective-permute-start.1 = (bf16[4,512,128]{2,1,0:T(8,128)(2,1)}, bf16[4,512,128]{2,1,0:T(8,128)(2,1)}, u32[]{:S(2)}, u32[]{:S(2)}) collective-permute-start(bf16[4,512,128]{2,1,0:T(8,128)(2,1)} %slice.3), channel_id=1, source_target_pairs={{0,64},{4,68},{8,72},{12,76},{16,80},{20,84},{24,88},{28,92},{32,9... | collective-permute-start | bytes 1572872 | tf_op jit(solution)/shard_map/ppermute | solution.py:428
  52.0 3.1 %collective-permute-start.3 = (f32[32,256]{1,0:T(8,128)S(1)}, f32[32,256]{1,0:T(8,128)S(1)}, u32[]{:S(2)}, u32[]{:S(2)}) collective-permute-start(f32[32,256]{1,0:T(8,128)S(1)} %shard_map.125.p0), channel_id=1, source_target_pairs={{0,1},{1,2},{2,3},{3,0},{4,5},{5,6},{6,7},{7,4},{8,9},{9,10},{10,1... | collective-permute-start | bytes 98312 | tf_op jit(solution)/shard_map/ppermute | solution.py:419
  55.1 4.4 %collective-permute-start.4 = (f32[32,256]{1,0:T(8,128)S(1)}, f32[32,256]{1,0:T(8,128)S(1)}, u32[]{:S(2)}, u32[]{:S(2)}) collective-permute-start(f32[32,256]{1,0:T(8,128)S(1)} %shard_map.125.p0), channel_id=1, source_target_pairs={{0,2},{1,3},{2,0},{3,1},{4,6},{5,7},{6,4},{7,5},{8,10},{9,11},{10,... | collective-permute-start | bytes 98312 | tf_op jit(solution)/shard_map/ppermute | solution.py:419
  59.5 3.1 %collective-permute-start.5 = (f32[32,256]{1,0:T(8,128)S(1)}, f32[32,256]{1,0:T(8,128)S(1)}, u32[]{:S(2)}, u32[]{:S(2)}) collective-permute-start(f32[32,256]{1,0:T(8,128)S(1)} %shard_map.125.p0), channel_id=1, source_target_pairs={{0,3},{1,0},{2,1},{3,2},{4,7},{5,4},{6,5},{7,6},{8,11},{9,8},{10,9... | collective-permute-start | bytes 98312 | tf_op jit(solution)/shard_map/ppermute | solution.py:419
  64.2 5.1 %shard_map.126 = (f32[136,128]{1,0:T(8,128)S(1)}, f32[128,128]{1,0:T(8,128)S(1)}) custom-call(bf16[256,256]{1,0:T(8,128)(2,1)S(1)} %copy-done.4, bf16[256,1024]{1,0:T(8,128)(2,1)S(1)} %copy-done.1, f32[1,1024]{1,0:T(1,128)S(1)} %bitcast.3, bf16[256,1024]{1,0:T(8,128)(2,1)S(1)} %copy-done, f32[32,256]{1,0:T(8,128)S(1)} %shard_map.125.p0, ...), custom_call_target="tpu_custom_call" | custom-call | flops 25165824 | bytes 1048576 | tf_op jit(solution)/shard_map/pallas_call | solution.py:266
  69.3 3.9 %collective-permute-start.6 = (f32[136,128]{1,0:T(8,128)S(1)}, f32[136,128]{1,0:T(8,128)S(1)}, u32[]{:S(2)}, u32[]{:S(2)}) collective-permute-start(f32[136,128]{1,0:T(8,128)S(1)} %get-tuple-element.15.refs_2_), channel_id=1, source_target_pairs={{0,4},{4,0},{8,12},{12,8},{16,20},{20,16},{24,28},{28,24},{32,36},... | collective-permute-start | bytes 208904 | tf_op jit(solution)/shard_map/ppermute | solution.py:399
  75.2 3.5 %collective-permute-start.7 = (f32[136,128]{1,0:T(8,128)S(1)}, f32[136,128]{1,0:T(8,128)S(1)}, u32[]{:S(2)}, u32[]{:S(2)}) collective-permute-start(f32[136,128]{1,0:T(8,128)S(1)} %get-tuple-element.16.refs_2_), channel_id=1, source_target_pairs={{0,8},{4,12},{8,0},{12,4},{16,24},{20,28},{24,16},{28,20},{32,40},... | collective-permute-start | bytes 208904 | tf_op jit(solution)/shard_map/ppermute | solution.py:399
  78.8 4.0 %collective-permute-start.8 = (f32[136,128]{1,0:T(8,128)S(1)}, f32[136,128]{1,0:T(8,128)S(1)}, u32[]{:S(2)}, u32[]{:S(2)}) collective-permute-start(f32[136,128]{1,0:T(8,128)S(1)} %get-tuple-element.16.refs_2_), channel_id=1, source_target_pairs={{0,16},{4,20},{8,24},{12,28},{16,0},{20,4},{24,8},{28,12},{32,48},... | collective-permute-start | bytes 208904 | tf_op jit(solution)/shard_map/ppermute | solution.py:399
  84.7 2.0 %collective-permute-done.8.refs_4_ = f32[136,128]{1,0:T(8,128)S(1)} collective-permute-done((f32[136,128]{1,0:T(8,128)S(1)}, f32[136,128]{1,0:T(8,128)S(1)}, u32[]{:S(2)}, u32[]{:S(2)}) %collective-permute-start.8) | collective-permute-done | bytes 69664 | tf_op jit(solution)/shard_map/ppermute | solution.py:399
  86.7 3.1 %collective-permute-done.9.refs_5_ = f32[136,128]{1,0:T(8,128)S(1)} collective-permute-done((f32[136,128]{1,0:T(8,128)S(1)}, f32[136,128]{1,0:T(8,128)S(1)}, u32[]{:S(2)}, u32[]{:S(2)}) %collective-permute-start.9) | collective-permute-done | bytes 69664 | tf_op jit(solution)/shard_map/ppermute | solution.py:399
  89.8 4.2 %collective-permute-start.10 = (f32[136,128]{1,0:T(8,128)S(1)}, f32[136,128]{1,0:T(8,128)S(1)}, u32[]{:S(2)}, u32[]{:S(2)}) collective-permute-start(f32[136,128]{1,0:T(8,128)S(1)} %get-tuple-element.18.refs_2_), channel_id=1, source_target_pairs={{0,32},{4,36},{8,40},{12,44},{16,48},{20,52},{24,56},{28,60},{32,0... | collective-permute-start | bytes 208904 | tf_op jit(solution)/shard_map/ppermute | solution.py:399
  94.1 4.8 %collective-permute-done.10.refs_3_ = f32[136,128]{1,0:T(8,128)S(1)} collective-permute-done((f32[136,128]{1,0:T(8,128)S(1)}, f32[136,128]{1,0:T(8,128)S(1)}, u32[]{:S(2)}, u32[]{:S(2)}) %collective-permute-start.10) | collective-permute-done | bytes 69664 | tf_op jit(solution)/shard_map/ppermute | solution.py:399
  100.3 8.4 %all-to-all-start.3 = ((f32[8,72,128]{2,1,0:T(8,128)}), f32[8,72,128]{2,1,0:T(8,128)S(1)}, u32[]{:S(2)}, u32[]{:S(2)}) async-start(f32[8,72,128]{2,1,0:T(8,128)} %get-tuple-element.20), calls=%async_computation.3 | async-start | bytes 589824 | tf_op jit(solution)/shard_map/all_to_all | solution.py:394
  108.6 3.7 %shard_map.122.later = bf16[4,256,128]{2,1,0:T(8,128)(2,1)S(1)} custom-call(s32[1]{0:T(128)} %bitcast.place.refs_0_, bf16[8,256,128]{2,1,0:T(8,128)(2,1)S(1)} %all-to-all-done.1.queries, bf16[8,512,128]{2,1,0:T(8,128)(2,1)S(1)} %all-to-all-done.own, bf16[8,512,128]{2,1,0:T(8,128)(2,1)S(1)} %collective-permute-done.other), custom_call_target="tpu_custom_call" | custom-call | flops 2147483648 | bytes 4194304 | tf_op jit(solution)/shard_map/pallas_call | solution.py:185
  112.3 5.8 %shard_map.123 = bf16[8,256,128]{2,1,0:T(8,128)(2,1)} custom-call(s32[1]{0:T(128)} %bitcast.place.refs_0_, bf16[8,256,128]{2,1,0:T(8,128)(2,1)S(1)} %all-to-all-done.1.queries, bf16[8,512,128]{2,1,0:T(8,128)(2,1)S(1)} %all-to-all-done.own, bf16[8,512,128]{2,1,0:T(8,128)(2,1)S(1)} %collective-permute-done.other, ...), custom_call_target="tpu_custom_call" | custom-call | flops 2147483648 | bytes 4194304 | tf_op jit(solution)/shard_map/pallas_call | solution.py:193
  118.4 7.3 %all-to-all-start.2 = ((bf16[8,256,128]{2,1,0:T(8,128)(2,1)}), bf16[8,256,128]{2,1,0:T(8,128)(2,1)S(1)}, u32[]{:S(2)}, u32[]{:S(2)}) async-start(bf16[8,256,128]{2,1,0:T(8,128)(2,1)} %shard_map.123), calls=%async_computation.2 | async-start | bytes 1048576 | tf_op jit(solution)/shard_map/all_to_all | solution.py:394
  125.8 5.2 %collective-permute-start.11 = (f32[64,128]{1,0:T(8,128)S(1)}, f32[64,128]{1,0:T(8,128)S(1)}, u32[]{:S(2)}, u32[]{:S(2)}) collective-permute-start(f32[64,128]{1,0:T(8,128)S(1)} %shard_map.130.mine), channel_id=1, source_target_pairs={{0,4},{4,0},{8,12},{12,8},{16,20},{20,16},{24,28},{28,24},{32,36},... | collective-permute-start | bytes 98312 | tf_op jit(solution)/shard_map/ppermute | solution.py:399
  131.7 10.2 %shard_map.131 = bf16[256,1024]{1,0:T(8,128)(2,1)} custom-call(s32[1]{0:T(128)} %bitcast.place.refs_0_, bf16[256,256]{1,0:T(8,128)(2,1)S(1)} %copy-done.5, bf16[256,1024]{1,0:T(8,128)(2,1)S(1)} %copy-done.2, f32[1,1024]{1,0:T(1,128)S(1)} %bitcast.4, bf16[256,1024]{1,0:T(8,128)(2,1)S(1)} %copy-done, f32[32,256]{1,0:T(8,128)S(1)} %shard_map.125.p0, ...), custom_call_target="tpu_custom_call" | custom-call | flops 37748736 | bytes 2097152 | tf_op jit(solution)/shard_map/pallas_call | solution.py:388
  (58 shorter events, 10.3 us)
Async XLA Ops:
  3.0 34.9 %all-to-all-start = ((bf16[8,512,128]{2,1,0:T(8,128)(2,1)}), bf16[8,512,128]{2,1,0:T(8,128)(2,1)S(1)}, u32[]{:S(2)}, u32[]{:S(2)}) async-start(bf16[8,512,128]{2,1,0:T(8,128)(2,1)} %pack.2), calls=%async_computation | async-start | bytes 2097152 | tf_op jit(solution)/shard_map/all_to_all | solution.py:394
  38.0 70.6 %collective-permute-start = (bf16[8,512,128]{2,1,0:T(8,128)(2,1)S(1)}, bf16[8,512,128]{2,1,0:T(8,128)(2,1)S(1)}, u32[]{:S(2)}, u32[]{:S(2)}) collective-permute-start(bf16[8,512,128]{2,1,0:T(8,128)(2,1)S(1)} %all-to-all-done.own), channel_id=1, source_target_pairs={{0,4},{4,0},{8,12},{12,8},{16,20},{20,16},{24,28},{28,24},{32,36},... | collective-permute-start | bytes 3145736 | tf_op jit(solution)/shard_map/ppermute | solution.py:430
  42.3 58.0 %all-to-all-start.1 = ((bf16[8,256,128]{2,1,0:T(8,128)(2,1)}), bf16[8,256,128]{2,1,0:T(8,128)(2,1)S(1)}, u32[]{:S(2)}, u32[]{:S(2)}) async-start(bf16[8,256,128]{2,1,0:T(8,128)(2,1)} %pack.3), calls=%async_computation.1 | async-start | bytes 1048576 | tf_op jit(solution)/shard_map/all_to_all | solution.py:394
  46.6 26.6 %collective-permute-start.1 = (bf16[4,512,128]{2,1,0:T(8,128)(2,1)}, bf16[4,512,128]{2,1,0:T(8,128)(2,1)}, u32[]{:S(2)}, u32[]{:S(2)}) collective-permute-start(bf16[4,512,128]{2,1,0:T(8,128)(2,1)} %slice.3), channel_id=1, source_target_pairs={{0,64},{4,68},{8,72},{12,76},{16,80},{20,84},{24,88},{28,92},{32,9... | collective-permute-start | bytes 1572872 | tf_op jit(solution)/shard_map/ppermute | solution.py:428
  51.6 12.5 %copy-start.1 = (bf16[256,1024]{1,0:T(8,128)(2,1)S(1)}, bf16[256,1024]{1,0:T(8,128)(2,1)}, u32[]{:S(2)}) copy-start(bf16[256,1024]{1,0:T(8,128)(2,1)} %proj.3) | copy-start | bytes 1572868
  51.6 12.5 %copy-start.4 = (bf16[256,256]{1,0:T(8,128)(2,1)S(1)}, bf16[256,256]{1,0:T(8,128)(2,1)}, u32[]{:S(2)}) copy-start(bf16[256,256]{1,0:T(8,128)(2,1)} %low.3) | copy-start | bytes 393220
  51.6 12.5 %copy-start.8 = (f32[16,1024]{1,0:T(8,128)S(1)}, f32[16,1024]{1,0:T(8,128)}, u32[]{:S(2)}) copy-start(f32[16,1024]{1,0:T(8,128)} %a_rate.1) | copy-start | bytes 196612
  51.6 12.5 %copy-start.15 = (f32[1024]{0:T(1024)S(1)}, f32[1024]{0:T(1024)}, u32[]{:S(2)}) copy-start(f32[1024]{0:T(1024)} %param.19) | copy-start | bytes 12292
  52.0 10.6 %collective-permute-start.3 = (f32[32,256]{1,0:T(8,128)S(1)}, f32[32,256]{1,0:T(8,128)S(1)}, u32[]{:S(2)}, u32[]{:S(2)}) collective-permute-start(f32[32,256]{1,0:T(8,128)S(1)} %shard_map.125.p0), channel_id=1, source_target_pairs={{0,1},{1,2},{2,3},{3,0},{4,5},{5,6},{6,7},{7,4},{8,9},{9,10},{10,1... | collective-permute-start | bytes 98312 | tf_op jit(solution)/shard_map/ppermute | solution.py:419
  55.1 7.5 %collective-permute-start.4 = (f32[32,256]{1,0:T(8,128)S(1)}, f32[32,256]{1,0:T(8,128)S(1)}, u32[]{:S(2)}, u32[]{:S(2)}) collective-permute-start(f32[32,256]{1,0:T(8,128)S(1)} %shard_map.125.p0), channel_id=1, source_target_pairs={{0,2},{1,3},{2,0},{3,1},{4,6},{5,7},{6,4},{7,5},{8,10},{9,11},{10,... | collective-permute-start | bytes 98312 | tf_op jit(solution)/shard_map/ppermute | solution.py:419
  59.5 4.7 %collective-permute-start.5 = (f32[32,256]{1,0:T(8,128)S(1)}, f32[32,256]{1,0:T(8,128)S(1)}, u32[]{:S(2)}, u32[]{:S(2)}) collective-permute-start(f32[32,256]{1,0:T(8,128)S(1)} %shard_map.125.p0), channel_id=1, source_target_pairs={{0,3},{1,0},{2,1},{3,2},{4,7},{5,4},{6,5},{7,6},{8,11},{9,8},{10,9... | collective-permute-start | bytes 98312 | tf_op jit(solution)/shard_map/ppermute | solution.py:419
  62.6 6.7 %copy-start.9 = (f32[32,256]{1,0:T(8,128)}, f32[32,256]{1,0:T(8,128)S(1)}, u32[]{:S(2)}) copy-start(f32[32,256]{1,0:T(8,128)S(1)} %collective-permute-done.3.p1) | copy-start | bytes 98308
  62.6 6.7 %copy-start.11 = (f32[32,256]{1,0:T(8,128)}, f32[32,256]{1,0:T(8,128)S(1)}, u32[]{:S(2)}) copy-start(f32[32,256]{1,0:T(8,128)S(1)} %collective-permute-done.4.p2) | copy-start | bytes 98308
  69.3 5.9 %collective-permute-start.6 = (f32[136,128]{1,0:T(8,128)S(1)}, f32[136,128]{1,0:T(8,128)S(1)}, u32[]{:S(2)}, u32[]{:S(2)}) collective-permute-start(f32[136,128]{1,0:T(8,128)S(1)} %get-tuple-element.15.refs_2_), channel_id=1, source_target_pairs={{0,4},{4,0},{8,12},{12,8},{16,20},{20,16},{24,28},{28,24},{32,36},... | collective-permute-start | bytes 208904 | tf_op jit(solution)/shard_map/ppermute | solution.py:399
  73.2 39.1 %collective-permute-start.2 = (bf16[4,512,128]{2,1,0:T(8,128)(2,1)}, bf16[4,512,128]{2,1,0:T(8,128)(2,1)}, u32[]{:S(2)}, u32[]{:S(2)}) collective-permute-start(bf16[4,512,128]{2,1,0:T(8,128)(2,1)} %collective-permute-done.1.old), channel_id=1, source_target_pairs={{0,4},{4,0},{8,12},{12,8},{16,20},{20,16},{24,28},{28,24},{32,36},... | collective-permute-start | bytes 1572872 | tf_op jit(solution)/shard_map/ppermute | solution.py:433
  75.2 9.5 %collective-permute-start.7 = (f32[136,128]{1,0:T(8,128)S(1)}, f32[136,128]{1,0:T(8,128)S(1)}, u32[]{:S(2)}, u32[]{:S(2)}) collective-permute-start(f32[136,128]{1,0:T(8,128)S(1)} %get-tuple-element.16.refs_2_), channel_id=1, source_target_pairs={{0,8},{4,12},{8,0},{12,4},{16,24},{20,28},{24,16},{28,20},{32,40},... | collective-permute-start | bytes 208904 | tf_op jit(solution)/shard_map/ppermute | solution.py:399
  78.8 7.9 %collective-permute-start.8 = (f32[136,128]{1,0:T(8,128)S(1)}, f32[136,128]{1,0:T(8,128)S(1)}, u32[]{:S(2)}, u32[]{:S(2)}) collective-permute-start(f32[136,128]{1,0:T(8,128)S(1)} %get-tuple-element.16.refs_2_), channel_id=1, source_target_pairs={{0,16},{4,20},{8,24},{12,28},{16,0},{20,4},{24,8},{28,12},{32,48},... | collective-permute-start | bytes 208904 | tf_op jit(solution)/shard_map/ppermute | solution.py:399
  82.8 7.0 %collective-permute-start.9 = (f32[136,128]{1,0:T(8,128)S(1)}, f32[136,128]{1,0:T(8,128)S(1)}, u32[]{:S(2)}, u32[]{:S(2)}) collective-permute-start(f32[136,128]{1,0:T(8,128)S(1)} %get-tuple-element.16.refs_2_), channel_id=1, source_target_pairs={{0,24},{4,28},{8,16},{12,20},{16,8},{20,12},{24,0},{28,4},{32,56},... | collective-permute-start | bytes 208904 | tf_op jit(solution)/shard_map/ppermute | solution.py:399
  89.8 9.1 %collective-permute-start.10 = (f32[136,128]{1,0:T(8,128)S(1)}, f32[136,128]{1,0:T(8,128)S(1)}, u32[]{:S(2)}, u32[]{:S(2)}) collective-permute-start(f32[136,128]{1,0:T(8,128)S(1)} %get-tuple-element.18.refs_2_), channel_id=1, source_target_pairs={{0,32},{4,36},{8,40},{12,44},{16,48},{20,52},{24,56},{28,60},{32,0... | collective-permute-start | bytes 208904 | tf_op jit(solution)/shard_map/ppermute | solution.py:399
  100.3 18.2 %all-to-all-start.3 = ((f32[8,72,128]{2,1,0:T(8,128)}), f32[8,72,128]{2,1,0:T(8,128)S(1)}, u32[]{:S(2)}, u32[]{:S(2)}) async-start(f32[8,72,128]{2,1,0:T(8,128)} %get-tuple-element.20), calls=%async_computation.3 | async-start | bytes 589824 | tf_op jit(solution)/shard_map/all_to_all | solution.py:394
  118.1 13.6 %copy-start.2 = (bf16[256,1024]{1,0:T(8,128)(2,1)S(1)}, bf16[256,1024]{1,0:T(8,128)(2,1)}, u32[]{:S(2)}) copy-start(bf16[256,1024]{1,0:T(8,128)(2,1)} %proj.3) | copy-start | bytes 1572868
  118.1 13.6 %copy-start.3 = (bf16[256,1024]{1,0:T(8,128)(2,1)S(1)}, bf16[256,1024]{1,0:T(8,128)(2,1)}, u32[]{:S(2)}) copy-start(bf16[256,1024]{1,0:T(8,128)(2,1)} %gate.1) | copy-start | bytes 1572868
  118.4 23.5 %all-to-all-start.2 = ((bf16[8,256,128]{2,1,0:T(8,128)(2,1)}), bf16[8,256,128]{2,1,0:T(8,128)(2,1)S(1)}, u32[]{:S(2)}, u32[]{:S(2)}) async-start(bf16[8,256,128]{2,1,0:T(8,128)(2,1)} %shard_map.123), calls=%async_computation.2 | async-start | bytes 1048576 | tf_op jit(solution)/shard_map/all_to_all | solution.py:394
  125.8 5.9 %collective-permute-start.11 = (f32[64,128]{1,0:T(8,128)S(1)}, f32[64,128]{1,0:T(8,128)S(1)}, u32[]{:S(2)}, u32[]{:S(2)}) collective-permute-start(f32[64,128]{1,0:T(8,128)S(1)} %shard_map.130.mine), channel_id=1, source_target_pairs={{0,4},{4,0},{8,12},{12,8},{16,20},{20,16},{24,28},{28,24},{32,36},... | collective-permute-start | bytes 98312 | tf_op jit(solution)/shard_map/ppermute | solution.py:399
  (10 other events, 53.2 us)

commit v6 on v5

--- a/solution.py
+++ b/solution.py
@@ -114,7 +114,7 @@
     out[i] = (total[:, 0:HD] / total[:, HD : 2 * HD]).astype(BF16)
 
 
-def late_body(place, queries, own, other, out):
+def late_body(place, own, other, out):
     half = out.shape[0]
     rows = out.shape[1]
     parity = parity_of(place)
@@ -126,14 +126,18 @@
     for i in range(half):
         full = [block(own, i + 1 + j) for j in range(half - 1)]
         full += [block(other, i + parity + j) for j in range(half)]
-        weigh(queries[half + i], (block(own, half + i), block(own, i)), full, out, i)
-
-
-def early_body(place, queries, own, other, old, past, later, out, ko, kp):
+        weigh(own[half + i, 2 * rows :, :], (block(own, half + i), block(own, i)), full, out, i)
+
+
+def early_body(place, own_far, other, old, past, later, out, ko, kp, own, sems):
     half, rows, _ = later.shape
     even = parity_of(place) == 0
     live = plane_of(place) > 0
-    out[half:] = later[...]
+    fetch = pltpu.make_async_copy(own_far.at[:half], own, sems.at[0])
+    fetch.start()
+    pass_on = pltpu.make_async_copy(later, out.at[half:], sems.at[1])
+    pass_on.start()
+    fetch.wait()
     key0 = jnp.where(even, own[0, 0:1, :].astype(F32), other[0, 0:1, :].astype(F32))
     key0 = jnp.broadcast_to(key0, (rows, HD)).astype(BF16)
     ones = jnp.ones((rows, HD), BF16)
@@ -175,24 +179,35 @@
 
     for i in range(half):
         full = [mine(i + 1 + j) for j in range(half - 1)] + [theirs(i + j) for j in range(half)]
-        weigh(queries[i], (mine(half + i), mine(i)), full, out, i)
-
-
-def attend_late(place, queries, own, other):
-    half, rows = queries.shape[0] // 2, queries.shape[1]
+        weigh(own[i, 2 * rows :, :], (mine(half + i), mine(i)), full, out, i)
+    pass_on.wait()
+
+
+def attend_late(place, own, other):
+    half, rows = own.shape[0] // 2, own.shape[1] // 3
     out = jax.ShapeDtypeStruct((half, rows, HD), BF16)
     estimate = cost(4 * half * rows * WINDOW * 2 * HD, 4 << 20, half * rows * WINDOW)
-    return local(late_body, out, (), 1, 3, estimate)(place, queries, own, other)
-
-
-def attend_early(place, queries, own, other, old, past, later):
+    return local(late_body, out, (), 1, 2, estimate)(place, own, other)
+
+
+def attend_early(place, own, other, old, past, later):
     half, rows, _ = later.shape
-    scratch = [pltpu.VMEM((half, rows, HD), BF16)] * 2
-    out = jax.ShapeDtypeStruct((2 * half, rows, HD), BF16)
-    estimate = cost(4 * half * rows * WINDOW * 2 * HD, 4 << 20, half * rows * WINDOW)
-    return local(early_body, out, scratch, 1, 6, estimate)(
-        place, queries, own, other, old, past, later
-    )
+    far = pl.BlockSpec(memory_space=pl.ANY)
+    return pl.pallas_call(
+        early_body,
+        out_shape=jax.ShapeDtypeStruct((2 * half, rows, HD), BF16),
+        in_specs=[SMEM, far, VMEM, VMEM, VMEM, far],
+        out_specs=VMEM,
+        scratch_shapes=[
+            pltpu.VMEM((half, rows, HD), BF16),
+            pltpu.VMEM((half, rows, HD), BF16),
+            pltpu.VMEM((half, *own.shape[1:]), BF16),
+            pltpu.SemaphoreType.DMA((2,)),
+        ],
+        name="early",
+        cost_estimate=cost(4 * half * rows * WINDOW * 2 * HD, 4 << 20, half * rows * WINDOW),
+        compiler_params=pltpu.CompilerParams(vmem_limit_bytes=63 << 20),
+    )(place, own, other, old, past, later)
 
 
 def rows_of(step):
@@ -410,10 +425,7 @@
     next_row = [(i, i + line) for i in range(ctx - line)]
 
     along_z = [[z * line + k for z in range(planes)] for k in range(line)]
-    own = exchange(pack(key, value), along_y)
-    queries = pack(query)
-    own, queries = lax.optimization_barrier((own, queries))
-    queries = exchange(queries, along_y)
+    own = exchange(pack(key, value, query), along_y)
     partial = project(xin, w_bc)
     partials = [partial] + [
         lax.ppermute(partial, "tp", [(i, (i + d) % tp) for i in range(tp)])
@@ -425,14 +437,14 @@
     maps = [whole] + [across(whole, 2 * d) for d in (1, 2, 3)]
     whole, before = join(place, rates, maps, before, 1, 0)
     whole, before = join(place, rates, [whole, across(whole, 8)], before, 3, planes)
-    old_kv = lax.ppermute(own[side // 2 :], "ctx", next_row)
+    old_kv = lax.ppermute(own[side // 2 :, : 2 * key.shape[0]], "ctx", next_row)
     wholes = exchange(whole, along_z)
     other = lax.ppermute(own, "ctx", partner)
     mine = join_planes(place, rates, wholes)
     theirs = across(mine, 1)
     past_kv = lax.ppermute(old_kv, "ctx", partner)
-    later = attend_late(place, queries, own, other)
-    attended = attend_early(place, queries, own, other, old_kv, past_kv, later)
+    later = attend_late(place, own, other)
+    attended = attend_early(place, own, other, old_kv, past_kv, later)
     attended = exchange(attended, along_y)
     attended = unpack(attended)
     mixed = finish(place, sources, partials, rates, (mine, theirs), before, gate_z, skip)

time: 144 us -> 155 us (1.076)
  blocking collectives: 0 us -> 44.7 us
  waiting for transfers between devices: 37.7 us -> 9.58 us
  starting transfers between devices: 71.1 us -> 58.7 us
  local copies, waits for them, and re-layouts: 1.7 us -> 7.75 us
    all_to_all x0 -> x1, blocking collectives: none -> 44.7 us  [exchange(): return lax.all_to_all(x, 'ctx', 0, 0, axis_index_groups=groups, tiled=True)]
    all_to_all x4 -> x2, waiting for transfers between devices: 25.7 us -> 0.01 us  [exchange(): return lax.all_to_all(x, 'ctx', 0, 0, axis_index_groups=groups, tiled=True)]
    all_to_all x4 -> x2, starting transfers between devices: 26.8 us -> 12.7 us  [exchange(): return lax.all_to_all(x, 'ctx', 0, 0, axis_index_groups=groups, tiled=True)]
    unnamed x37 -> x35, local copies, waits for them, and re-layouts: 0.87 us -> 6.92 us
    pallas_call x2, Pallas kernels: 9.46 us -> 12.3 us  [the longest x1 7.28 us: attend_early(): pl.pallas_call(early_body, out_shape=jax.ShapeDtypeStruct((2 * half, rows...]
    ppermute x6, waiting for transfers between devices: 10.5 us -> 7.99 us  [across(): return lax.ppermute(part, 'ctx', [(i, i ^ distance) for i in range(count)])]
    ppermute x1, starting transfers between devices: 4.3 us -> 6.05 us  [shards(): other = lax.ppermute(own, 'ctx', partner)]
    pallas_call x2 -> x1, Pallas kernels: 4.33 us -> 2.82 us  [pack(): pl.pallas_call(pack_body, out_shape=jax.ShapeDtypeStruct((heads, len(part...]
  transfers between devices with their start and end apart: 16 -> 14, of which waited for: 7 -> 4; matrix products, arithmetic and copies ran while one was open for 1% -> 1% of each run, Pallas kernels for 20% -> 19%
where the time goes in v6:
time: 155 us; the launch traced here: 154 us
  starting transfers between devices  58.7 us (38%)
  blocking collectives  44.7 us (29%)
  Pallas kernels  32.5 us (21%)
  waiting for transfers between devices  9.58 us (6%)
  local copies, waits for them, and re-layouts  7.75 us (5%)
    all_to_all x1, blocking collectives, exchange(): return lax.all_to_all(x, 'ctx', 0, 0, axis_index_groups=groups, tiled=True)  44.7 us
    ppermute x6, starting transfers between devices, across(): return lax.ppermute(part, 'ctx', [(i, i ^ distance) for i in range(count)])  22.7 us
    all_to_all x2, starting transfers between devices, exchange(): return lax.all_to_all(x, 'ctx', 0, 0, axis_index_groups=groups, tiled=True)  12.7 us
    ppermute x3, starting transfers between devices, shards(): lax.ppermute(partial, 'tp', [(i, (i + d) % tp) for i in range(tp)])  10.5 us
    pallas_call x1, Pallas kernels, finish(): local(final_body, out, scratch, 1, 14, estimate)  10.1 us
    ppermute x6, waiting for transfers between devices, across(): return lax.ppermute(part, 'ctx', [(i, i ^ distance) for i in range(count)])  7.99 us
    pallas_call x1, Pallas kernels, attend_early(): pl.pallas_call(early_body, out_shape=jax.ShapeDtypeStruct((2 * half, rows...  7.28 us
    unnamed x35, local copies, waits for them, and re-layouts  6.92 us
  transfers between devices with their start and end apart: 14, of which 4 were waited for; matrix products, arithmetic and copies ran while one was open for 1% of the time, Pallas kernels for 19%

profile of v6, /device:TPU:1, one launch (start us, length us, event | category | flops | bytes accessed | tf_op | source)
XLA Modules:
  0.0 154.1 jit_solution(17752328277882232549)
XLA Ops:
  0.6 2.8 %pack.1 = bf16[8,768,128]{2,1,0:T(8,128)(2,1)} custom-call(bf16[256,1024]{1,0:T(8,128)(2,1)} %refs_0_.1, bf16[256,1024]{1,0:T(8,128)(2,1)} %refs_1_.1, bf16[256,1024]{1,0:T(8,128)(2,1)} %refs_2_.1), custom_call_target="tpu_custom_call" | custom-call | bytes 3145728 | tf_op jit(solution)/shard_map/pack/pallas_call | solution.py:66
  3.5 44.7 %all_to_all.15.own.own_far = bf16[8,768,128]{2,1,0:T(8,128)(2,1)S(1)} all-to-all(bf16[8,768,128]{2,1,0:T(8,128)(2,1)} %pack.1), channel_id=1, replica_groups={{0,8,16,24,32,40,48,56},{4,12,20,28,36,44,52,60},{64,72,80,88,96,104,11..., dimensions={0} | all-to-all | bytes 3145728 | tf_op jit(solution)/shard_map/all_to_all | solution.py:409
  48.2 6.1 %collective-permute-start = (bf16[8,768,128]{2,1,0:T(8,128)(2,1)S(1)}, bf16[8,768,128]{2,1,0:T(8,128)(2,1)}, u32[]{:S(2)}, u32[]{:S(2)}) collective-permute-start(bf16[8,768,128]{2,1,0:T(8,128)(2,1)S(1)} %all_to_all.15.own.own_far), channel_id=1, source_target_pairs={{0,4},{4,0},{8,12},{12,8},{16,20},{20,16},{24,28},{28,24},{32,36},... | collective-permute-start | bytes 4718600 | tf_op jit(solution)/shard_map/ppermute | solution.py:442
  55.1 4.8 %collective-permute-start.1 = (bf16[4,512,128]{2,1,0:T(8,128)(2,1)}, bf16[4,512,128]{2,1,0:T(8,128)(2,1)}, u32[]{:S(2)}, u32[]{:S(2)}) collective-permute-start(bf16[4,512,128]{2,1,0:T(8,128)(2,1)} %slice.4), channel_id=1, source_target_pairs={{0,64},{4,68},{8,72},{12,76},{16,80},{20,84},{24,88},{28,92},{32,9... | collective-permute-start | bytes 1572872 | tf_op jit(solution)/shard_map/ppermute | solution.py:440
  60.4 3.1 %collective-permute-start.3 = (f32[32,256]{1,0:T(8,128)S(1)}, f32[32,256]{1,0:T(8,128)S(1)}, u32[]{:S(2)}, u32[]{:S(2)}) collective-permute-start(f32[32,256]{1,0:T(8,128)S(1)} %shard_map.124.p0), channel_id=1, source_target_pairs={{0,1},{1,2},{2,3},{3,0},{4,5},{5,6},{6,7},{7,4},{8,9},{9,10},{10,1... | collective-permute-start | bytes 98312 | tf_op jit(solution)/shard_map/ppermute | solution.py:431
  63.5 4.4 %collective-permute-start.4 = (f32[32,256]{1,0:T(8,128)S(1)}, f32[32,256]{1,0:T(8,128)S(1)}, u32[]{:S(2)}, u32[]{:S(2)}) collective-permute-start(f32[32,256]{1,0:T(8,128)S(1)} %shard_map.124.p0), channel_id=1, source_target_pairs={{0,2},{1,3},{2,0},{3,1},{4,6},{5,7},{6,4},{7,5},{8,10},{9,11},{10,... | collective-permute-start | bytes 98312 | tf_op jit(solution)/shard_map/ppermute | solution.py:431
  67.9 3.1 %collective-permute-start.5 = (f32[32,256]{1,0:T(8,128)S(1)}, f32[32,256]{1,0:T(8,128)S(1)}, u32[]{:S(2)}, u32[]{:S(2)}) collective-permute-start(f32[32,256]{1,0:T(8,128)S(1)} %shard_map.124.p0), channel_id=1, source_target_pairs={{0,3},{1,0},{2,1},{3,2},{4,7},{5,4},{6,5},{7,6},{8,11},{9,8},{10,9... | collective-permute-start | bytes 98312 | tf_op jit(solution)/shard_map/ppermute | solution.py:431
  71.0 1.6 %collective-permute-done.5.p3 = f32[32,256]{1,0:T(8,128)S(1)} collective-permute-done((f32[32,256]{1,0:T(8,128)S(1)}, f32[32,256]{1,0:T(8,128)S(1)}, u32[]{:S(2)}, u32[]{:S(2)}) %collective-permute-start.5) | collective-permute-done | bytes 32800 | tf_op jit(solution)/shard_map/ppermute | solution.py:431
  72.6 5.1 %shard_map.125 = (f32[136,128]{1,0:T(8,128)S(1)}, f32[128,128]{1,0:T(8,128)S(1)}) custom-call(bf16[256,256]{1,0:T(8,128)(2,1)S(1)} %copy-done.5, bf16[256,1024]{1,0:T(8,128)(2,1)S(1)} %copy-done.2, f32[1,1024]{1,0:T(1,128)S(1)} %bitcast.3, bf16[256,1024]{1,0:T(8,128)(2,1)S(1)} %copy-done.1, f32[32,256]{1,0:T(8,128)S(1)} %shard_map.124.p0, ...), custom_call_target="tpu_custom_call" | custom-call | flops 25165824 | bytes 1048576 | tf_op jit(solution)/shard_map/pallas_call | solution.py:281
  77.6 3.9 %collective-permute-start.6 = (f32[136,128]{1,0:T(8,128)S(1)}, f32[136,128]{1,0:T(8,128)S(1)}, u32[]{:S(2)}, u32[]{:S(2)}) collective-permute-start(f32[136,128]{1,0:T(8,128)S(1)} %get-tuple-element.11.refs_2_), channel_id=1, source_target_pairs={{0,4},{4,0},{8,12},{12,8},{16,20},{20,16},{24,28},{28,24},{32,36},... | collective-permute-start | bytes 208904 | tf_op jit(solution)/shard_map/ppermute | solution.py:414
  81.6 1.9 %collective-permute-start.2 = (bf16[4,512,128]{2,1,0:T(8,128)(2,1)}, bf16[4,512,128]{2,1,0:T(8,128)(2,1)}, u32[]{:S(2)}, u32[]{:S(2)}) collective-permute-start(bf16[4,512,128]{2,1,0:T(8,128)(2,1)} %collective-permute-done.1.old), channel_id=1, source_target_pairs={{0,4},{4,0},{8,12},{12,8},{16,20},{20,16},{24,28},{28,24},{32,36},... | collective-permute-start | bytes 1572872 | tf_op jit(solution)/shard_map/ppermute | solution.py:445
  83.6 2.2 %collective-permute-start.7 = (f32[136,128]{1,0:T(8,128)S(1)}, f32[136,128]{1,0:T(8,128)S(1)}, u32[]{:S(2)}, u32[]{:S(2)}) collective-permute-start(f32[136,128]{1,0:T(8,128)S(1)} %get-tuple-element.12.refs_2_), channel_id=1, source_target_pairs={{0,8},{4,12},{8,0},{12,4},{16,24},{20,28},{24,16},{28,20},{32,40},... | collective-permute-start | bytes 208904 | tf_op jit(solution)/shard_map/ppermute | solution.py:414
  85.8 1.9 %collective-permute-start.8 = (f32[136,128]{1,0:T(8,128)S(1)}, f32[136,128]{1,0:T(8,128)S(1)}, u32[]{:S(2)}, u32[]{:S(2)}) collective-permute-start(f32[136,128]{1,0:T(8,128)S(1)} %get-tuple-element.12.refs_2_), channel_id=1, source_target_pairs={{0,16},{4,20},{8,24},{12,28},{16,0},{20,4},{24,8},{28,12},{32,48},... | collective-permute-start | bytes 208904 | tf_op jit(solution)/shard_map/ppermute | solution.py:414
  87.7 5.2 %collective-permute-start.9 = (f32[136,128]{1,0:T(8,128)S(1)}, f32[136,128]{1,0:T(8,128)S(1)}, u32[]{:S(2)}, u32[]{:S(2)}) collective-permute-start(f32[136,128]{1,0:T(8,128)S(1)} %get-tuple-element.12.refs_2_), channel_id=1, source_target_pairs={{0,24},{4,28},{8,16},{12,20},{16,8},{20,12},{24,0},{28,4},{32,56},... | collective-permute-start | bytes 208904 | tf_op jit(solution)/shard_map/ppermute | solution.py:414
  92.9 1.8 %collective-permute-done.9.refs_5_ = f32[136,128]{1,0:T(8,128)S(1)} collective-permute-done((f32[136,128]{1,0:T(8,128)S(1)}, f32[136,128]{1,0:T(8,128)S(1)}, u32[]{:S(2)}, u32[]{:S(2)}) %collective-permute-start.9) | collective-permute-done | bytes 69664 | tf_op jit(solution)/shard_map/ppermute | solution.py:414
  94.8 3.7 %collective-permute-start.10 = (f32[136,128]{1,0:T(8,128)S(1)}, f32[136,128]{1,0:T(8,128)S(1)}, u32[]{:S(2)}, u32[]{:S(2)}) collective-permute-start(f32[136,128]{1,0:T(8,128)S(1)} %get-tuple-element.14.refs_2_), channel_id=1, source_target_pairs={{0,32},{4,36},{8,40},{12,44},{16,48},{20,52},{24,56},{28,60},{32,0... | collective-permute-start | bytes 208904 | tf_op jit(solution)/shard_map/ppermute | solution.py:414
  98.5 5.5 %collective-permute-done.10.refs_3_ = f32[136,128]{1,0:T(8,128)S(1)} collective-permute-done((f32[136,128]{1,0:T(8,128)S(1)}, f32[136,128]{1,0:T(8,128)S(1)}, u32[]{:S(2)}, u32[]{:S(2)}) %collective-permute-start.10) | collective-permute-done | bytes 69664 | tf_op jit(solution)/shard_map/ppermute | solution.py:414
  104.7 8.3 %all-to-all-start.2 = ((f32[8,72,128]{2,1,0:T(8,128)}), f32[8,72,128]{2,1,0:T(8,128)S(1)}, u32[]{:S(2)}, u32[]{:S(2)}) async-start(f32[8,72,128]{2,1,0:T(8,128)} %get-tuple-element.16), calls=%async_computation.2 | async-start | bytes 589824 | tf_op jit(solution)/shard_map/all_to_all | solution.py:409
  113.1 5.0 %shard_map.122.later = bf16[4,256,128]{2,1,0:T(8,128)(2,1)S(1)} custom-call(s32[1]{0:T(128)} %bitcast.place.refs_0_, bf16[8,768,128]{2,1,0:T(8,128)(2,1)S(1)} %all_to_all.15.own.own_far, bf16[8,768,128]{2,1,0:T(8,128)(2,1)} %collective-permute-done.other), custom_call_target="tpu_custom_call" | custom-call | flops 2147483648 | bytes 4194304 | tf_op jit(solution)/shard_map/pallas_call | solution.py:190
  118.8 7.3 %early.1 = bf16[8,256,128]{2,1,0:T(8,128)(2,1)} custom-call(s32[1]{0:T(128)} %bitcast.place.refs_0_, bf16[8,768,128]{2,1,0:T(8,128)(2,1)} %copy-done, bf16[8,768,128]{2,1,0:T(8,128)(2,1)} %collective-permute-done.other, bf16[4,512,128]{2,1,0:T(8,128)(2,1)} %collective-permute-done.1.old, bf16[4,512,128]{2,1,0:T(8,128)(2,1)} %collective-permute-done.2.past, ...), custom_call_target="tpu_custom_call" | custom-call | flops 2147483648 | bytes 4194304 | tf_op jit(solution)/shard_map/early/pallas_call | solution.py:196
  126.1 4.3 %all-to-all-start.1 = ((bf16[8,256,128]{2,1,0:T(8,128)(2,1)}), bf16[8,256,128]{2,1,0:T(8,128)(2,1)S(1)}, u32[]{:S(2)}, u32[]{:S(2)}) async-start(bf16[8,256,128]{2,1,0:T(8,128)(2,1)} %early.1), calls=%async_computation.1 | async-start | bytes 1048576 | tf_op jit(solution)/shard_map/all_to_all | solution.py:409
  130.5 5.8 %collective-permute-start.11 = (f32[64,128]{1,0:T(8,128)S(1)}, f32[64,128]{1,0:T(8,128)S(1)}, u32[]{:S(2)}, u32[]{:S(2)}) collective-permute-start(f32[64,128]{1,0:T(8,128)S(1)} %shard_map.129.mine), channel_id=1, source_target_pairs={{0,4},{4,0},{8,12},{12,8},{16,20},{20,16},{24,28},{28,24},{32,36},... | collective-permute-start | bytes 98312 | tf_op jit(solution)/shard_map/ppermute | solution.py:414
  137.0 1.0 copy-done.3
  143.0 10.1 %shard_map.130 = bf16[256,1024]{1,0:T(8,128)(2,1)} custom-call(s32[1]{0:T(128)} %bitcast.place.refs_0_, bf16[256,256]{1,0:T(8,128)(2,1)S(1)} %copy-done.6, bf16[256,1024]{1,0:T(8,128)(2,1)S(1)} %copy-done.3, f32[1,1024]{1,0:T(1,128)S(1)} %bitcast.4, bf16[256,1024]{1,0:T(8,128)(2,1)S(1)} %copy-done.1, f32[32,256]{1,0:T(8,128)S(1)} %shard_map.124.p0, ...), custom_call_target="tpu_custom_call" | custom-call | flops 37748736 | bytes 2097152 | tf_op jit(solution)/shard_map/pallas_call | solution.py:403
  (52 shorter events, 9.6 us)
Async XLA Ops:
  3.5 56.4 %copy-start.16 = (bf16[1024,32]{0,1:T(8,128)(2,1)S(1)}, bf16[1024,32]{0,1:T(8,128)(2,1)}, u32[]{:S(2)}) copy-start(bf16[1024,32]{0,1:T(8,128)(2,1)} %param.16) | copy-start | bytes 196612
  3.5 56.6 %copy-start.1 = (bf16[256,1024]{1,0:T(8,128)(2,1)S(1)}, bf16[256,1024]{1,0:T(8,128)(2,1)}, u32[]{:S(2)}) copy-start(bf16[256,1024]{1,0:T(8,128)(2,1)} %xin.5) | copy-start | bytes 1572868
  48.2 64.9 %copy-start = (bf16[8,768,128]{2,1,0:T(8,128)(2,1)}, bf16[8,768,128]{2,1,0:T(8,128)(2,1)S(1)}, u32[]{:S(2)}) copy-start(bf16[8,768,128]{2,1,0:T(8,128)(2,1)S(1)} %all_to_all.15.own.own_far) | copy-start | bytes 4718596
  48.2 24.4 %copy-start.2 = (bf16[256,1024]{1,0:T(8,128)(2,1)S(1)}, bf16[256,1024]{1,0:T(8,128)(2,1)}, u32[]{:S(2)}) copy-start(bf16[256,1024]{1,0:T(8,128)(2,1)} %proj.3) | copy-start | bytes 1572868
  48.2 24.4 %copy-start.5 = (bf16[256,256]{1,0:T(8,128)(2,1)S(1)}, bf16[256,256]{1,0:T(8,128)(2,1)}, u32[]{:S(2)}) copy-start(bf16[256,256]{1,0:T(8,128)(2,1)} %low.3) | copy-start | bytes 393220
  48.2 24.4 %copy-start.9 = (f32[16,1024]{1,0:T(8,128)S(1)}, f32[16,1024]{1,0:T(8,128)}, u32[]{:S(2)}) copy-start(f32[16,1024]{1,0:T(8,128)} %a_rate.1) | copy-start | bytes 196612
  48.2 24.4 %copy-start.12 = (f32[1024]{0:T(1024)S(1)}, f32[1024]{0:T(1024)}, u32[]{:S(2)}) copy-start(f32[1024]{0:T(1024)} %param.19) | copy-start | bytes 12292
  48.2 64.9 %collective-permute-start = (bf16[8,768,128]{2,1,0:T(8,128)(2,1)S(1)}, bf16[8,768,128]{2,1,0:T(8,128)(2,1)}, u32[]{:S(2)}, u32[]{:S(2)}) collective-permute-start(bf16[8,768,128]{2,1,0:T(8,128)(2,1)S(1)} %all_to_all.15.own.own_far), channel_id=1, source_target_pairs={{0,4},{4,0},{8,12},{12,8},{16,20},{20,16},{24,28},{28,24},{32,36},... | collective-permute-start | bytes 4718600 | tf_op jit(solution)/shard_map/ppermute | solution.py:442
  55.1 26.5 %collective-permute-start.1 = (bf16[4,512,128]{2,1,0:T(8,128)(2,1)}, bf16[4,512,128]{2,1,0:T(8,128)(2,1)}, u32[]{:S(2)}, u32[]{:S(2)}) collective-permute-start(bf16[4,512,128]{2,1,0:T(8,128)(2,1)} %slice.4), channel_id=1, source_target_pairs={{0,64},{4,68},{8,72},{12,76},{16,80},{20,84},{24,88},{28,92},{32,9... | collective-permute-start | bytes 1572872 | tf_op jit(solution)/shard_map/ppermute | solution.py:440
  60.4 10.6 %collective-permute-start.3 = (f32[32,256]{1,0:T(8,128)S(1)}, f32[32,256]{1,0:T(8,128)S(1)}, u32[]{:S(2)}, u32[]{:S(2)}) collective-permute-start(f32[32,256]{1,0:T(8,128)S(1)} %shard_map.124.p0), channel_id=1, source_target_pairs={{0,1},{1,2},{2,3},{3,0},{4,5},{5,6},{6,7},{7,4},{8,9},{9,10},{10,1... | collective-permute-start | bytes 98312 | tf_op jit(solution)/shard_map/ppermute | solution.py:431
  63.5 7.4 %collective-permute-start.4 = (f32[32,256]{1,0:T(8,128)S(1)}, f32[32,256]{1,0:T(8,128)S(1)}, u32[]{:S(2)}, u32[]{:S(2)}) collective-permute-start(f32[32,256]{1,0:T(8,128)S(1)} %shard_map.124.p0), channel_id=1, source_target_pairs={{0,2},{1,3},{2,0},{3,1},{4,6},{5,7},{6,4},{7,5},{8,10},{9,11},{10,... | collective-permute-start | bytes 98312 | tf_op jit(solution)/shard_map/ppermute | solution.py:431
  67.9 4.7 %collective-permute-start.5 = (f32[32,256]{1,0:T(8,128)S(1)}, f32[32,256]{1,0:T(8,128)S(1)}, u32[]{:S(2)}, u32[]{:S(2)}) collective-permute-start(f32[32,256]{1,0:T(8,128)S(1)} %shard_map.124.p0), channel_id=1, source_target_pairs={{0,3},{1,0},{2,1},{3,2},{4,7},{5,4},{6,5},{7,6},{8,11},{9,8},{10,9... | collective-permute-start | bytes 98312 | tf_op jit(solution)/shard_map/ppermute | solution.py:431
  72.5 5.1 %copy-start.10 = (f32[32,256]{1,0:T(8,128)}, f32[32,256]{1,0:T(8,128)S(1)}, u32[]{:S(2)}) copy-start(f32[32,256]{1,0:T(8,128)S(1)} %collective-permute-done.5.p3) | copy-start | bytes 98308
  77.6 5.9 %collective-permute-start.6 = (f32[136,128]{1,0:T(8,128)S(1)}, f32[136,128]{1,0:T(8,128)S(1)}, u32[]{:S(2)}, u32[]{:S(2)}) collective-permute-start(f32[136,128]{1,0:T(8,128)S(1)} %get-tuple-element.11.refs_2_), channel_id=1, source_target_pairs={{0,4},{4,0},{8,12},{12,8},{16,20},{20,16},{24,28},{28,24},{32,36},... | collective-permute-start | bytes 208904 | tf_op jit(solution)/shard_map/ppermute | solution.py:414
  81.6 37.2 %collective-permute-start.2 = (bf16[4,512,128]{2,1,0:T(8,128)(2,1)}, bf16[4,512,128]{2,1,0:T(8,128)(2,1)}, u32[]{:S(2)}, u32[]{:S(2)}) collective-permute-start(bf16[4,512,128]{2,1,0:T(8,128)(2,1)} %collective-permute-done.1.old), channel_id=1, source_target_pairs={{0,4},{4,0},{8,12},{12,8},{16,20},{20,16},{24,28},{28,24},{32,36},... | collective-permute-start | bytes 1572872 | tf_op jit(solution)/shard_map/ppermute | solution.py:445
  83.6 9.3 %collective-permute-start.7 = (f32[136,128]{1,0:T(8,128)S(1)}, f32[136,128]{1,0:T(8,128)S(1)}, u32[]{:S(2)}, u32[]{:S(2)}) collective-permute-start(f32[136,128]{1,0:T(8,128)S(1)} %get-tuple-element.12.refs_2_), channel_id=1, source_target_pairs={{0,8},{4,12},{8,0},{12,4},{16,24},{20,28},{24,16},{28,20},{32,40},... | collective-permute-start | bytes 208904 | tf_op jit(solution)/shard_map/ppermute | solution.py:414
  85.8 7.1 %collective-permute-start.8 = (f32[136,128]{1,0:T(8,128)S(1)}, f32[136,128]{1,0:T(8,128)S(1)}, u32[]{:S(2)}, u32[]{:S(2)}) collective-permute-start(f32[136,128]{1,0:T(8,128)S(1)} %get-tuple-element.12.refs_2_), channel_id=1, source_target_pairs={{0,16},{4,20},{8,24},{12,28},{16,0},{20,4},{24,8},{28,12},{32,48},... | collective-permute-start | bytes 208904 | tf_op jit(solution)/shard_map/ppermute | solution.py:414
  87.7 7.0 %collective-permute-start.9 = (f32[136,128]{1,0:T(8,128)S(1)}, f32[136,128]{1,0:T(8,128)S(1)}, u32[]{:S(2)}, u32[]{:S(2)}) collective-permute-start(f32[136,128]{1,0:T(8,128)S(1)} %get-tuple-element.12.refs_2_), channel_id=1, source_target_pairs={{0,24},{4,28},{8,16},{12,20},{16,8},{20,12},{24,0},{28,4},{32,56},... | collective-permute-start | bytes 208904 | tf_op jit(solution)/shard_map/ppermute | solution.py:414
  94.8 9.2 %collective-permute-start.10 = (f32[136,128]{1,0:T(8,128)S(1)}, f32[136,128]{1,0:T(8,128)S(1)}, u32[]{:S(2)}, u32[]{:S(2)}) collective-permute-start(f32[136,128]{1,0:T(8,128)S(1)} %get-tuple-element.14.refs_2_), channel_id=1, source_target_pairs={{0,32},{4,36},{8,40},{12,44},{16,48},{20,52},{24,56},{28,60},{32,0... | collective-permute-start | bytes 208904 | tf_op jit(solution)/shard_map/ppermute | solution.py:414
  104.7 13.4 %copy-start.7 = (f32[136,128]{1,0:T(8,128)}, f32[136,128]{1,0:T(8,128)S(1)}, u32[]{:S(2)}) copy-start(f32[136,128]{1,0:T(8,128)S(1)} %get-tuple-element.17.before) | copy-start | bytes 208900
  104.7 21.4 %all-to-all-start.2 = ((f32[8,72,128]{2,1,0:T(8,128)}), f32[8,72,128]{2,1,0:T(8,128)S(1)}, u32[]{:S(2)}, u32[]{:S(2)}) async-start(f32[8,72,128]{2,1,0:T(8,128)} %get-tuple-element.16), calls=%async_computation.2 | async-start | bytes 589824 | tf_op jit(solution)/shard_map/all_to_all | solution.py:409
  126.1 27.0 %all-to-all-start.1 = ((bf16[8,256,128]{2,1,0:T(8,128)(2,1)}), bf16[8,256,128]{2,1,0:T(8,128)(2,1)S(1)}, u32[]{:S(2)}, u32[]{:S(2)}) async-start(bf16[8,256,128]{2,1,0:T(8,128)(2,1)} %early.1), calls=%async_computation.1 | async-start | bytes 1048576 | tf_op jit(solution)/shard_map/all_to_all | solution.py:409
  130.5 6.5 %collective-permute-start.11 = (f32[64,128]{1,0:T(8,128)S(1)}, f32[64,128]{1,0:T(8,128)S(1)}, u32[]{:S(2)}, u32[]{:S(2)}) collective-permute-start(f32[64,128]{1,0:T(8,128)S(1)} %shard_map.129.mine), channel_id=1, source_target_pairs={{0,4},{4,0},{8,12},{12,8},{16,20},{20,16},{24,28},{28,24},{32,36},... | collective-permute-start | bytes 98312 | tf_op jit(solution)/shard_map/ppermute | solution.py:414
  137.0 1.0 copy-start.3
  (7 other events, 5.7 us)

commit v7 on v6

--- a/solution.py
+++ b/solution.py
@@ -129,15 +129,20 @@
         weigh(own[half + i, 2 * rows :, :], (block(own, half + i), block(own, i)), full, out, i)
 
 
-def early_body(place, own_far, other, old, past, later, out, ko, kp, own, sems):
+def early_body(place, own_far, other_far, old, past, later, out, ko, kp, own, other, sems):
     half, rows, _ = later.shape
     even = parity_of(place) == 0
     live = plane_of(place) > 0
     fetch = pltpu.make_async_copy(own_far.at[:half], own, sems.at[0])
     fetch.start()
+    fetch_other = pltpu.make_async_copy(
+        other_far.at[:half, pl.ds(0, 2 * rows), :], other, sems.at[2]
+    )
+    fetch_other.start()
     pass_on = pltpu.make_async_copy(later, out.at[half:], sems.at[1])
     pass_on.start()
     fetch.wait()
+    fetch_other.wait()
     key0 = jnp.where(even, own[0, 0:1, :].astype(F32), other[0, 0:1, :].astype(F32))
     key0 = jnp.broadcast_to(key0, (rows, HD)).astype(BF16)
     ones = jnp.ones((rows, HD), BF16)
@@ -196,13 +201,14 @@
     return pl.pallas_call(
         early_body,
         out_shape=jax.ShapeDtypeStruct((2 * half, rows, HD), BF16),
-        in_specs=[SMEM, far, VMEM, VMEM, VMEM, far],
+        in_specs=[SMEM, far, far, VMEM, VMEM, far],
         out_specs=VMEM,
         scratch_shapes=[
             pltpu.VMEM((half, rows, HD), BF16),
             pltpu.VMEM((half, rows, HD), BF16),
             pltpu.VMEM((half, *own.shape[1:]), BF16),
-            pltpu.SemaphoreType.DMA((2,)),
+            pltpu.VMEM((half, 2 * rows, HD), BF16),
+            pltpu.SemaphoreType.DMA((3,)),
         ],
         name="early",
         cost_estimate=cost(4 * half * rows * WINDOW * 2 * HD, 4 << 20, half * rows * WINDOW),
@@ -400,7 +406,7 @@
     tall = pltpu.VMEM((rows * TILES, LANES), F32)
     scratch = [pltpu.VMEM((rows * 2 * NS, LANES), F32), tall, tall, tall]
     estimate = cost(9 * rows * width * NS, 8 * rows * width, rows * width * NS)
-    return local(final_body, out, scratch, 1, 14, estimate)(
+    return local(final_body, out, scratch, 1, 14, estimate, 63 << 20)(
         place, *sources, *partials, rates, *halves, before, gate, skip.reshape(1, -1)
     )
 

time: 155 us -> 152 us (0.981)
  local copies, waits for them, and re-layouts: 7.75 us -> 3.17 us
    unnamed x35, local copies, waits for them, and re-layouts: 6.92 us -> 2.34 us
  transfers between devices with their start and end apart: 14 -> 14, of which waited for: 4 -> 4; matrix products, arithmetic and copies ran while one was open for 1% -> 1% of each run, Pallas kernels for 19% -> 20%
where the time goes in v7:
time: 152 us; the launch traced here: 151 us
  starting transfers between devices  58.7 us (39%)
  blocking collectives  44.7 us (29%)
  Pallas kernels  33.6 us (22%)
  waiting for transfers between devices  9.56 us (6%)
  local copies, waits for them, and re-layouts  3.17 us (2%)
    all_to_all x1, blocking collectives, exchange(): return lax.all_to_all(x, 'ctx', 0, 0, axis_index_groups=groups, tiled=True)  44.7 us
    ppermute x6, starting transfers between devices, across(): return lax.ppermute(part, 'ctx', [(i, i ^ distance) for i in range(count)])  22.7 us
    all_to_all x2, starting transfers between devices, exchange(): return lax.all_to_all(x, 'ctx', 0, 0, axis_index_groups=groups, tiled=True)  12.7 us
    pallas_call x1, Pallas kernels, finish(): local(final_body, out, scratch, 1, 14, estimate, 63 << 20)  11.5 us
    ppermute x3, starting transfers between devices, shards(): lax.ppermute(partial, 'tp', [(i, (i + d) % tp) for i in range(tp)])  10.5 us
    ppermute x6, waiting for transfers between devices, across(): return lax.ppermute(part, 'ctx', [(i, i ^ distance) for i in range(count)])  7.99 us
    pallas_call x1, Pallas kernels, attend_early(): pl.pallas_call(early_body, out_shape=jax.ShapeDtypeStruct((2 * half, rows...  6.95 us
    ppermute x1, starting transfers between devices, shards(): other = lax.ppermute(own, 'ctx', partner)  6.05 us
  transfers between devices with their start and end apart: 14, of which 4 were waited for; matrix products, arithmetic and copies ran while one was open for 1% of the time, Pallas kernels for 20%

profile of v7, /device:TPU:1, one launch (start us, length us, event | category | flops | bytes accessed | tf_op | source)
XLA Modules:
  0.0 150.6 jit_solution(16805935720887161694)
XLA Ops:
  0.6 2.8 %pack.1 = bf16[8,768,128]{2,1,0:T(8,128)(2,1)} custom-call(bf16[256,1024]{1,0:T(8,128)(2,1)} %refs_0_.1, bf16[256,1024]{1,0:T(8,128)(2,1)} %refs_1_.1, bf16[256,1024]{1,0:T(8,128)(2,1)} %refs_2_.1), custom_call_target="tpu_custom_call" | custom-call | bytes 3145728 | tf_op jit(solution)/shard_map/pack/pallas_call | solution.py:66
  3.5 44.7 %all_to_all.15.own.own_far = bf16[8,768,128]{2,1,0:T(8,128)(2,1)S(1)} all-to-all(bf16[8,768,128]{2,1,0:T(8,128)(2,1)} %pack.1), channel_id=1, replica_groups={{0,8,16,24,32,40,48,56},{4,12,20,28,36,44,52,60},{64,72,80,88,96,104,11..., dimensions={0} | all-to-all | bytes 3145728 | tf_op jit(solution)/shard_map/all_to_all | solution.py:415
  48.2 6.1 %collective-permute-start = (bf16[8,768,128]{2,1,0:T(8,128)(2,1)S(1)}, bf16[8,768,128]{2,1,0:T(8,128)(2,1)}, u32[]{:S(2)}, u32[]{:S(2)}) collective-permute-start(bf16[8,768,128]{2,1,0:T(8,128)(2,1)S(1)} %all_to_all.15.own.own_far), channel_id=1, source_target_pairs={{0,4},{4,0},{8,12},{12,8},{16,20},{20,16},{24,28},{28,24},{32,36},... | collective-permute-start | bytes 4718600 | tf_op jit(solution)/shard_map/ppermute | solution.py:448
  55.1 4.8 %collective-permute-start.1 = (bf16[4,512,128]{2,1,0:T(8,128)(2,1)}, bf16[4,512,128]{2,1,0:T(8,128)(2,1)}, u32[]{:S(2)}, u32[]{:S(2)}) collective-permute-start(bf16[4,512,128]{2,1,0:T(8,128)(2,1)} %slice.4), channel_id=1, source_target_pairs={{0,64},{4,68},{8,72},{12,76},{16,80},{20,84},{24,88},{28,92},{32,9... | collective-permute-start | bytes 1572872 | tf_op jit(solution)/shard_map/ppermute | solution.py:446
  60.4 3.1 %collective-permute-start.3 = (f32[32,256]{1,0:T(8,128)S(1)}, f32[32,256]{1,0:T(8,128)S(1)}, u32[]{:S(2)}, u32[]{:S(2)}) collective-permute-start(f32[32,256]{1,0:T(8,128)S(1)} %shard_map.124.p0), channel_id=1, source_target_pairs={{0,1},{1,2},{2,3},{3,0},{4,5},{5,6},{6,7},{7,4},{8,9},{9,10},{10,1... | collective-permute-start | bytes 98312 | tf_op jit(solution)/shard_map/ppermute | solution.py:437
  63.5 4.4 %collective-permute-start.4 = (f32[32,256]{1,0:T(8,128)S(1)}, f32[32,256]{1,0:T(8,128)S(1)}, u32[]{:S(2)}, u32[]{:S(2)}) collective-permute-start(f32[32,256]{1,0:T(8,128)S(1)} %shard_map.124.p0), channel_id=1, source_target_pairs={{0,2},{1,3},{2,0},{3,1},{4,6},{5,7},{6,4},{7,5},{8,10},{9,11},{10,... | collective-permute-start | bytes 98312 | tf_op jit(solution)/shard_map/ppermute | solution.py:437
  67.9 3.1 %collective-permute-start.5 = (f32[32,256]{1,0:T(8,128)S(1)}, f32[32,256]{1,0:T(8,128)S(1)}, u32[]{:S(2)}, u32[]{:S(2)}) collective-permute-start(f32[32,256]{1,0:T(8,128)S(1)} %shard_map.124.p0), channel_id=1, source_target_pairs={{0,3},{1,0},{2,1},{3,2},{4,7},{5,4},{6,5},{7,6},{8,11},{9,8},{10,9... | collective-permute-start | bytes 98312 | tf_op jit(solution)/shard_map/ppermute | solution.py:437
  71.0 1.5 %collective-permute-done.5.p3 = f32[32,256]{1,0:T(8,128)S(1)} collective-permute-done((f32[32,256]{1,0:T(8,128)S(1)}, f32[32,256]{1,0:T(8,128)S(1)}, u32[]{:S(2)}, u32[]{:S(2)}) %collective-permute-start.5) | collective-permute-done | bytes 32800 | tf_op jit(solution)/shard_map/ppermute | solution.py:437
  72.6 5.1 %shard_map.125 = (f32[136,128]{1,0:T(8,128)S(1)}, f32[128,128]{1,0:T(8,128)S(1)}) custom-call(bf16[256,256]{1,0:T(8,128)(2,1)S(1)} %copy-done.6, bf16[256,1024]{1,0:T(8,128)(2,1)S(1)} %copy-done.5, f32[1,1024]{1,0:T(1,128)S(1)} %bitcast.4, bf16[256,1024]{1,0:T(8,128)(2,1)S(1)} %copy-done.2, f32[32,256]{1,0:T(8,128)S(1)} %shard_map.124.p0, ...), custom_call_target="tpu_custom_call" | custom-call | flops 25165824 | bytes 1048576 | tf_op jit(solution)/shard_map/pallas_call | solution.py:287
  77.7 3.9 %collective-permute-start.6 = (f32[136,128]{1,0:T(8,128)S(1)}, f32[136,128]{1,0:T(8,128)S(1)}, u32[]{:S(2)}, u32[]{:S(2)}) collective-permute-start(f32[136,128]{1,0:T(8,128)S(1)} %get-tuple-element.11.refs_2_), channel_id=1, source_target_pairs={{0,4},{4,0},{8,12},{12,8},{16,20},{20,16},{24,28},{28,24},{32,36},... | collective-permute-start | bytes 208904 | tf_op jit(solution)/shard_map/ppermute | solution.py:420
  81.6 1.9 %collective-permute-start.2 = (bf16[4,512,128]{2,1,0:T(8,128)(2,1)}, bf16[4,512,128]{2,1,0:T(8,128)(2,1)S(1)}, u32[]{:S(2)}, u32[]{:S(2)}) collective-permute-start(bf16[4,512,128]{2,1,0:T(8,128)(2,1)} %collective-permute-done.1.old), channel_id=1, source_target_pairs={{0,4},{4,0},{8,12},{12,8},{16,20},{20,16},{24,28},{28,24},{32,36},... | collective-permute-start | bytes 1572872 | tf_op jit(solution)/shard_map/ppermute | solution.py:451
  83.6 2.2 %collective-permute-start.7 = (f32[136,128]{1,0:T(8,128)S(1)}, f32[136,128]{1,0:T(8,128)S(1)}, u32[]{:S(2)}, u32[]{:S(2)}) collective-permute-start(f32[136,128]{1,0:T(8,128)S(1)} %get-tuple-element.12.refs_2_), channel_id=1, source_target_pairs={{0,8},{4,12},{8,0},{12,4},{16,24},{20,28},{24,16},{28,20},{32,40},... | collective-permute-start | bytes 208904 | tf_op jit(solution)/shard_map/ppermute | solution.py:420
  85.8 1.9 %collective-permute-start.8 = (f32[136,128]{1,0:T(8,128)S(1)}, f32[136,128]{1,0:T(8,128)S(1)}, u32[]{:S(2)}, u32[]{:S(2)}) collective-permute-start(f32[136,128]{1,0:T(8,128)S(1)} %get-tuple-element.12.refs_2_), channel_id=1, source_target_pairs={{0,16},{4,20},{8,24},{12,28},{16,0},{20,4},{24,8},{28,12},{32,48},... | collective-permute-start | bytes 208904 | tf_op jit(solution)/shard_map/ppermute | solution.py:420
  87.7 5.2 %collective-permute-start.9 = (f32[136,128]{1,0:T(8,128)S(1)}, f32[136,128]{1,0:T(8,128)S(1)}, u32[]{:S(2)}, u32[]{:S(2)}) collective-permute-start(f32[136,128]{1,0:T(8,128)S(1)} %get-tuple-element.12.refs_2_), channel_id=1, source_target_pairs={{0,24},{4,28},{8,16},{12,20},{16,8},{20,12},{24,0},{28,4},{32,56},... | collective-permute-start | bytes 208904 | tf_op jit(solution)/shard_map/ppermute | solution.py:420
  92.9 1.8 %collective-permute-done.9.refs_5_ = f32[136,128]{1,0:T(8,128)S(1)} collective-permute-done((f32[136,128]{1,0:T(8,128)S(1)}, f32[136,128]{1,0:T(8,128)S(1)}, u32[]{:S(2)}, u32[]{:S(2)}) %collective-permute-start.9) | collective-permute-done | bytes 69664 | tf_op jit(solution)/shard_map/ppermute | solution.py:420
  94.8 3.7 %collective-permute-start.10 = (f32[136,128]{1,0:T(8,128)S(1)}, f32[136,128]{1,0:T(8,128)S(1)}, u32[]{:S(2)}, u32[]{:S(2)}) collective-permute-start(f32[136,128]{1,0:T(8,128)S(1)} %get-tuple-element.14.refs_2_), channel_id=1, source_target_pairs={{0,32},{4,36},{8,40},{12,44},{16,48},{20,52},{24,56},{28,60},{32,0... | collective-permute-start | bytes 208904 | tf_op jit(solution)/shard_map/ppermute | solution.py:420
  98.5 5.5 %collective-permute-done.10.refs_3_ = f32[136,128]{1,0:T(8,128)S(1)} collective-permute-done((f32[136,128]{1,0:T(8,128)S(1)}, f32[136,128]{1,0:T(8,128)S(1)}, u32[]{:S(2)}, u32[]{:S(2)}) %collective-permute-start.10) | collective-permute-done | bytes 69664 | tf_op jit(solution)/shard_map/ppermute | solution.py:420
  104.8 8.3 %all-to-all-start.2 = ((f32[8,72,128]{2,1,0:T(8,128)}), f32[8,72,128]{2,1,0:T(8,128)S(1)}, u32[]{:S(2)}, u32[]{:S(2)}) async-start(f32[8,72,128]{2,1,0:T(8,128)} %get-tuple-element.16), calls=%async_computation.2 | async-start | bytes 589824 | tf_op jit(solution)/shard_map/all_to_all | solution.py:415
  113.1 5.0 %shard_map.122.later = bf16[4,256,128]{2,1,0:T(8,128)(2,1)S(1)} custom-call(s32[1]{0:T(128)} %bitcast.place.refs_0_, bf16[8,768,128]{2,1,0:T(8,128)(2,1)S(1)} %all_to_all.15.own.own_far, bf16[8,768,128]{2,1,0:T(8,128)(2,1)} %collective-permute-done.other.other_far), custom_call_target="tpu_custom_call" | custom-call | flops 2147483648 | bytes 4194304 | tf_op jit(solution)/shard_map/pallas_call | solution.py:195
  119.7 7.0 %early.1 = bf16[8,256,128]{2,1,0:T(8,128)(2,1)} custom-call(s32[1]{0:T(128)} %bitcast.place.refs_0_, bf16[8,768,128]{2,1,0:T(8,128)(2,1)} %copy-done, bf16[8,768,128]{2,1,0:T(8,128)(2,1)} %collective-permute-done.other.other_far, bf16[4,512,128]{2,1,0:T(8,128)(2,1)} %collective-permute-done.1.old, bf16[4,512,128]{2,1,0:T(8,128)(2,1)} %copy-done.15, ...), custom_call_target="tpu_custom_call" | custom-call | flops 2147483648 | bytes 4194304 | tf_op jit(solution)/shard_map/early/pallas_call | solution.py:201
  126.6 4.3 %all-to-all-start.1 = ((bf16[8,256,128]{2,1,0:T(8,128)(2,1)}), bf16[8,256,128]{2,1,0:T(8,128)(2,1)S(1)}, u32[]{:S(2)}, u32[]{:S(2)}) async-start(bf16[8,256,128]{2,1,0:T(8,128)(2,1)} %early.1), calls=%async_computation.1 | async-start | bytes 1048576 | tf_op jit(solution)/shard_map/all_to_all | solution.py:415
  131.1 5.8 %collective-permute-start.11 = (f32[64,128]{1,0:T(8,128)S(1)}, f32[64,128]{1,0:T(8,128)S(1)}, u32[]{:S(2)}, u32[]{:S(2)}) collective-permute-start(f32[64,128]{1,0:T(8,128)S(1)} %shard_map.129.mine), channel_id=1, source_target_pairs={{0,4},{4,0},{8,12},{12,8},{16,20},{20,16},{24,28},{28,24},{32,36},... | collective-permute-start | bytes 98312 | tf_op jit(solution)/shard_map/ppermute | solution.py:420
  138.2 11.5 %shard_map.130 = bf16[256,1024]{1,0:T(8,128)(2,1)} custom-call(s32[1]{0:T(128)} %bitcast.place.refs_0_, bf16[256,256]{1,0:T(8,128)(2,1)} %low.3, bf16[256,1024]{1,0:T(8,128)(2,1)} %proj.3, f32[1,1024]{1,0:T(1,128)} %bitcast.3, bf16[256,1024]{1,0:T(8,128)(2,1)} %xin.5, f32[32,256]{1,0:T(8,128)} %copy-done.3, f32[32,256]{1,0:T(8,128)} %copy-done.9, ...), custom_call_target="tpu_custom_call" | custom-call | flops 37748736 | bytes 2097152 | tf_op jit(solution)/shard_map/pallas_call | solution.py:409
  149.7 0.9 shard_map.123
  (52 shorter events, 5.1 us)
Async XLA Ops:
  3.5 56.4 %copy-start.14 = (bf16[1024,32]{0,1:T(8,128)(2,1)S(1)}, bf16[1024,32]{0,1:T(8,128)(2,1)}, u32[]{:S(2)}) copy-start(bf16[1024,32]{0,1:T(8,128)(2,1)} %param.16) | copy-start | bytes 196612
  3.5 56.6 %copy-start.2 = (bf16[256,1024]{1,0:T(8,128)(2,1)S(1)}, bf16[256,1024]{1,0:T(8,128)(2,1)}, u32[]{:S(2)}) copy-start(bf16[256,1024]{1,0:T(8,128)(2,1)} %xin.5) | copy-start | bytes 1572868
  48.2 65.0 %copy-start = (bf16[8,768,128]{2,1,0:T(8,128)(2,1)}, bf16[8,768,128]{2,1,0:T(8,128)(2,1)S(1)}, u32[]{:S(2)}) copy-start(bf16[8,768,128]{2,1,0:T(8,128)(2,1)S(1)} %all_to_all.15.own.own_far) | copy-start | bytes 4718596
  48.2 24.4 %copy-start.5 = (bf16[256,1024]{1,0:T(8,128)(2,1)S(1)}, bf16[256,1024]{1,0:T(8,128)(2,1)}, u32[]{:S(2)}) copy-start(bf16[256,1024]{1,0:T(8,128)(2,1)} %proj.3) | copy-start | bytes 1572868
  48.2 24.4 %copy-start.6 = (bf16[256,256]{1,0:T(8,128)(2,1)S(1)}, bf16[256,256]{1,0:T(8,128)(2,1)}, u32[]{:S(2)}) copy-start(bf16[256,256]{1,0:T(8,128)(2,1)} %low.3) | copy-start | bytes 393220
  48.2 24.4 %copy-start.8 = (f32[16,1024]{1,0:T(8,128)S(1)}, f32[16,1024]{1,0:T(8,128)}, u32[]{:S(2)}) copy-start(f32[16,1024]{1,0:T(8,128)} %a_rate.1) | copy-start | bytes 196612
  48.2 24.4 %copy-start.12 = (f32[1024]{0:T(1024)S(1)}, f32[1024]{0:T(1024)}, u32[]{:S(2)}) copy-start(f32[1024]{0:T(1024)} %param.19) | copy-start | bytes 12292
  48.2 64.9 %collective-permute-start = (bf16[8,768,128]{2,1,0:T(8,128)(2,1)S(1)}, bf16[8,768,128]{2,1,0:T(8,128)(2,1)}, u32[]{:S(2)}, u32[]{:S(2)}) collective-permute-start(bf16[8,768,128]{2,1,0:T(8,128)(2,1)S(1)} %all_to_all.15.own.own_far), channel_id=1, source_target_pairs={{0,4},{4,0},{8,12},{12,8},{16,20},{20,16},{24,28},{28,24},{32,36},... | collective-permute-start | bytes 4718600 | tf_op jit(solution)/shard_map/ppermute | solution.py:448
  55.1 26.5 %collective-permute-start.1 = (bf16[4,512,128]{2,1,0:T(8,128)(2,1)}, bf16[4,512,128]{2,1,0:T(8,128)(2,1)}, u32[]{:S(2)}, u32[]{:S(2)}) collective-permute-start(bf16[4,512,128]{2,1,0:T(8,128)(2,1)} %slice.4), channel_id=1, source_target_pairs={{0,64},{4,68},{8,72},{12,76},{16,80},{20,84},{24,88},{28,92},{32,9... | collective-permute-start | bytes 1572872 | tf_op jit(solution)/shard_map/ppermute | solution.py:446
  60.4 17.3 %copy-start.3 = (f32[32,256]{1,0:T(8,128)}, f32[32,256]{1,0:T(8,128)S(1)}, u32[]{:S(2)}) copy-start(f32[32,256]{1,0:T(8,128)S(1)} %shard_map.124.p0) | copy-start | bytes 98308
  60.4 10.6 %collective-permute-start.3 = (f32[32,256]{1,0:T(8,128)S(1)}, f32[32,256]{1,0:T(8,128)S(1)}, u32[]{:S(2)}, u32[]{:S(2)}) collective-permute-start(f32[32,256]{1,0:T(8,128)S(1)} %shard_map.124.p0), channel_id=1, source_target_pairs={{0,1},{1,2},{2,3},{3,0},{4,5},{5,6},{6,7},{7,4},{8,9},{9,10},{10,1... | collective-permute-start | bytes 98312 | tf_op jit(solution)/shard_map/ppermute | solution.py:437
  63.5 7.5 %collective-permute-start.4 = (f32[32,256]{1,0:T(8,128)S(1)}, f32[32,256]{1,0:T(8,128)S(1)}, u32[]{:S(2)}, u32[]{:S(2)}) collective-permute-start(f32[32,256]{1,0:T(8,128)S(1)} %shard_map.124.p0), channel_id=1, source_target_pairs={{0,2},{1,3},{2,0},{3,1},{4,6},{5,7},{6,4},{7,5},{8,10},{9,11},{10,... | collective-permute-start | bytes 98312 | tf_op jit(solution)/shard_map/ppermute | solution.py:437
  67.9 4.7 %collective-permute-start.5 = (f32[32,256]{1,0:T(8,128)S(1)}, f32[32,256]{1,0:T(8,128)S(1)}, u32[]{:S(2)}, u32[]{:S(2)}) collective-permute-start(f32[32,256]{1,0:T(8,128)S(1)} %shard_map.124.p0), channel_id=1, source_target_pairs={{0,3},{1,0},{2,1},{3,2},{4,7},{5,4},{6,5},{7,6},{8,11},{9,8},{10,9... | collective-permute-start | bytes 98312 | tf_op jit(solution)/shard_map/ppermute | solution.py:437
  77.7 53.3 %copy-start.1 = (f32[128,128]{1,0:T(8,128)}, f32[128,128]{1,0:T(8,128)S(1)}, u32[]{:S(2)}) copy-start(f32[128,128]{1,0:T(8,128)S(1)} %get-tuple-element.10.refs_1_.rates.held) | copy-start | bytes 196612
  77.7 5.9 %collective-permute-start.6 = (f32[136,128]{1,0:T(8,128)S(1)}, f32[136,128]{1,0:T(8,128)S(1)}, u32[]{:S(2)}, u32[]{:S(2)}) collective-permute-start(f32[136,128]{1,0:T(8,128)S(1)} %get-tuple-element.11.refs_2_), channel_id=1, source_target_pairs={{0,4},{4,0},{8,12},{12,8},{16,20},{20,16},{24,28},{28,24},{32,36},... | collective-permute-start | bytes 208904 | tf_op jit(solution)/shard_map/ppermute | solution.py:420
  81.6 37.2 %collective-permute-start.2 = (bf16[4,512,128]{2,1,0:T(8,128)(2,1)}, bf16[4,512,128]{2,1,0:T(8,128)(2,1)S(1)}, u32[]{:S(2)}, u32[]{:S(2)}) collective-permute-start(bf16[4,512,128]{2,1,0:T(8,128)(2,1)} %collective-permute-done.1.old), channel_id=1, source_target_pairs={{0,4},{4,0},{8,12},{12,8},{16,20},{20,16},{24,28},{28,24},{32,36},... | collective-permute-start | bytes 1572872 | tf_op jit(solution)/shard_map/ppermute | solution.py:451
  83.6 9.3 %collective-permute-start.7 = (f32[136,128]{1,0:T(8,128)S(1)}, f32[136,128]{1,0:T(8,128)S(1)}, u32[]{:S(2)}, u32[]{:S(2)}) collective-permute-start(f32[136,128]{1,0:T(8,128)S(1)} %get-tuple-element.12.refs_2_), channel_id=1, source_target_pairs={{0,8},{4,12},{8,0},{12,4},{16,24},{20,28},{24,16},{28,20},{32,40},... | collective-permute-start | bytes 208904 | tf_op jit(solution)/shard_map/ppermute | solution.py:420
  85.8 7.1 %collective-permute-start.8 = (f32[136,128]{1,0:T(8,128)S(1)}, f32[136,128]{1,0:T(8,128)S(1)}, u32[]{:S(2)}, u32[]{:S(2)}) collective-permute-start(f32[136,128]{1,0:T(8,128)S(1)} %get-tuple-element.12.refs_2_), channel_id=1, source_target_pairs={{0,16},{4,20},{8,24},{12,28},{16,0},{20,4},{24,8},{28,12},{32,48},... | collective-permute-start | bytes 208904 | tf_op jit(solution)/shard_map/ppermute | solution.py:420
  87.7 7.0 %collective-permute-start.9 = (f32[136,128]{1,0:T(8,128)S(1)}, f32[136,128]{1,0:T(8,128)S(1)}, u32[]{:S(2)}, u32[]{:S(2)}) collective-permute-start(f32[136,128]{1,0:T(8,128)S(1)} %get-tuple-element.12.refs_2_), channel_id=1, source_target_pairs={{0,24},{4,28},{8,16},{12,20},{16,8},{20,12},{24,0},{28,4},{32,56},... | collective-permute-start | bytes 208904 | tf_op jit(solution)/shard_map/ppermute | solution.py:420
  94.8 9.2 %collective-permute-start.10 = (f32[136,128]{1,0:T(8,128)S(1)}, f32[136,128]{1,0:T(8,128)S(1)}, u32[]{:S(2)}, u32[]{:S(2)}) collective-permute-start(f32[136,128]{1,0:T(8,128)S(1)} %get-tuple-element.14.refs_2_), channel_id=1, source_target_pairs={{0,32},{4,36},{8,40},{12,44},{16,48},{20,52},{24,56},{28,60},{32,0... | collective-permute-start | bytes 208904 | tf_op jit(solution)/shard_map/ppermute | solution.py:420
  104.8 13.4 %copy-start.7 = (f32[136,128]{1,0:T(8,128)}, f32[136,128]{1,0:T(8,128)S(1)}, u32[]{:S(2)}) copy-start(f32[136,128]{1,0:T(8,128)S(1)} %get-tuple-element.17.before) | copy-start | bytes 208900
  104.8 21.9 %all-to-all-start.2 = ((f32[8,72,128]{2,1,0:T(8,128)}), f32[8,72,128]{2,1,0:T(8,128)S(1)}, u32[]{:S(2)}, u32[]{:S(2)}) async-start(f32[8,72,128]{2,1,0:T(8,128)} %get-tuple-element.16), calls=%async_computation.2 | async-start | bytes 589824 | tf_op jit(solution)/shard_map/all_to_all | solution.py:415
  126.6 23.1 %all-to-all-start.1 = ((bf16[8,256,128]{2,1,0:T(8,128)(2,1)}), bf16[8,256,128]{2,1,0:T(8,128)(2,1)S(1)}, u32[]{:S(2)}, u32[]{:S(2)}) async-start(bf16[8,256,128]{2,1,0:T(8,128)(2,1)} %early.1), calls=%async_computation.1 | async-start | bytes 1048576 | tf_op jit(solution)/shard_map/all_to_all | solution.py:415
  131.1 6.5 %collective-permute-start.11 = (f32[64,128]{1,0:T(8,128)S(1)}, f32[64,128]{1,0:T(8,128)S(1)}, u32[]{:S(2)}, u32[]{:S(2)}) collective-permute-start(f32[64,128]{1,0:T(8,128)S(1)} %shard_map.129.mine), channel_id=1, source_target_pairs={{0,4},{4,0},{8,12},{12,8},{16,20},{20,16},{24,28},{28,24},{32,36},... | collective-permute-start | bytes 98312 | tf_op jit(solution)/shard_map/ppermute | solution.py:420
  (7 other events, 27.2 us)
